TPU v7x, 32 devices: a whole 2x2x4 slice. The times are simulated.
32 devices in a mesh: grp: 2 (over y), smp: 4 (over z), snp: 2 (over x), pair: 2 (over core).
Axes of the slice: x: 2, y: 2, z: 4, core: 2. Of those that a mesh axis runs over, the one named last changes fastest.
Arguments:
- dosage: bfloat16 [16384, 4096], P(('grp', 'smp'), ('snp', 'pair')), parts along dimension 0, may hold values from 0 to 2
- allele_mean: float32 [8192], P('grp'), parts along dimension 0, may hold values from 0.7 to 1.3
- snp_scale: float32 [8192], P('grp'), parts along dimension 0, may hold values from 1.5 to 4.5
- band_next: int32 [128], P('grp'), parts along dimension 0, may hold values from 1 to 2
- ld_prev: float32 [8192, 320], P(('grp', 'smp')), parts along dimension 0, may hold values from -0.95 to 1, as said below
- band_prev: int32 [128], P('grp'), parts along dimension 0, may hold values from 1 to 2
- zscores: float32 [8192, 512], P(('grp', 'smp'), ('snp', 'pair')), parts along dimension 0, may hold values from -22 to 22
- observed: int32 [8192, 8], P(('grp', 'smp'), ('snp', 'pair')), parts along dimension 0, may hold values 0 or 1
Outputs:
- ld_next: float32 [8192, 320], P(('grp', 'snp', 'pair')), parts along dimension 0
- imputed: float32 [8192, 512], P(('grp', 'smp'), ('snp', 'pair')), parts along dimension 0
There are 2 independent parts, one for each index of `grp`. A program takes and returns all parts, laid end to end along the dimension named above; each array names one. Nothing has to cross between parts.
Inputs may be any that keep to these rules, and one draw needn't show every extreme that they name: `ld_prev`: row i holds the band of a symmetric matrix with unit diagonal: entry (i, o) belongs to column 64 * (i // 64) - 128 + o. For every band mask, the masked matrix plus the identity is positive definite.
All inputs are finite; a program needn't handle non-finite values. No bound on the sum of `observed` on one device may be relied on, other than what follows from the above.
Results may differ from a plain program's by a relative error of at most 0.00049.
Values may be sent and summed in bfloat16 or wider, within the bound.
No kernel may reach another device: no remote copies, remote signals or barrier semaphores. Data moves between devices by JAX's collectives and lax.ppermute only.
A program may use at most 128 MiB of HBM per device.

v0:
```python
import jax
import jax.numpy as jnp
from jax import lax
from jax.sharding import PartitionSpec as P

TILE = 64
BMAX = 2
TBLK = 64
ITERS = 3


ridge_term = 1.0


def extended_2(cells, sides, width):
    for axis, dim in sides:
        count = lax.axis_size(axis)
        ends = count - 1
        head = lax.slice_in_dim(cells, 0, width, axis=dim)
        tail = lax.slice_in_dim(cells, cells.shape[dim] - width, cells.shape[dim], axis=dim)
        cells = jnp.concatenate(
            [
                lax.ppermute(tail, axis, [(i, (i + 1) % count) for i in range(ends)]),
                cells,
                lax.ppermute(head, axis, [((i + 1) % count, i) for i in range(ends)]),
            ],
            axis=dim,
        )
    return cells


def passed_along(value, axis, by):
    count = lax.axis_size(axis)
    pairs = [(i, i + by) for i in range(count) if 0 <= i + by < count]
    return lax.ppermute(value, axis, pairs)


def band_of(window, tile_size, span):
    local_rows = window.shape[0]
    tile_count = local_rows // tile_size
    blocks = window.reshape(tile_count, tile_size, tile_count + span - 1, tile_size)
    pieces = []
    for offset in range(span):
        diagonal = jnp.diagonal(blocks[:, :, offset : offset + tile_count, :], axis1=0, axis2=2)
        pieces.append(jnp.transpose(diagonal, (2, 0, 1)))
    return jnp.concatenate(pieces, axis=2).reshape(local_rows, span * tile_size)


def tile_table(widths, reach_tiles):
    tile_total = widths.shape[0]
    padded = jnp.pad(widths, reach_tiles)
    columns = []
    for offset in range(-reach_tiles, reach_tiles + 1):
        beside = padded[reach_tiles + offset : reach_tiles + offset + tile_total]
        columns.append(abs(offset) <= jnp.minimum(widths, beside))
    return jnp.stack(columns, axis=1).astype(jnp.float32)


def local_mask(widths, position, tile_count):
    tile_flags = tile_table(widths, BMAX)
    rows_here = lax.dynamic_slice_in_dim(tile_flags, position * tile_count, tile_count, 0)
    return jnp.repeat(jnp.repeat(rows_here, TILE, axis=0), TILE, axis=1)


def transpose_gram(left, right):
    return lax.dot_general(
        left, right, (((0,), (0,)), ((), ())), preferred_element_type=jnp.float32
    )


def band_product(matrix, widened, local_rows, traits_here):
    tile_count = local_rows // TILE
    stacked = widened.reshape(tile_count + 2 * BMAX, TILE, traits_here)
    windows = jnp.concatenate(
        [stacked[offset : offset + tile_count] for offset in range(2 * BMAX + 1)], axis=1
    )
    band_tiles = matrix.reshape(tile_count, TILE, (2 * BMAX + 1) * TILE)
    result = jnp.einsum("uio,uot->uit", band_tiles, windows, precision=lax.Precision.HIGHEST)
    return result.reshape(local_rows, traits_here)


def apply_band(matrix, vector):
    widened = extended_2(vector, (("smp", 0),), TILE * BMAX)
    return band_product(matrix, widened, vector.shape[0], vector.shape[1])


def operate(matrix, seen_mask, vector):
    masked = seen_mask * vector
    return (
        seen_mask * (apply_band(matrix, masked) + ridge_term * masked) + (1.0 - seen_mask) * vector
    )


def squares(residual):
    return lax.psum(jnp.sum(residual * residual, axis=0), "smp")


def local(dosage, allele_mean, snp_scale, band_next, ld_prev, band_prev, zscores, observed):
    band_reach = TILE * BMAX
    local_cols = dosage.shape[1]
    build_tiles = local_cols // TILE
    column_place = lax.axis_index(("snp", "pair"))
    first_col = column_place * local_cols
    mean_here = lax.dynamic_slice_in_dim(allele_mean, first_col, local_cols, 0)
    scale_here = lax.dynamic_slice_in_dim(snp_scale, first_col, local_cols, 0)
    normed = ((dosage.astype(jnp.float32) - mean_here) * scale_here).astype(jnp.bfloat16)
    following = passed_along(normed[:, :band_reach], ("snp", "pair"), -1)
    own_block = transpose_gram(normed, normed)
    cross_part = transpose_gram(normed[:, local_cols - band_reach :], following)
    filler = jnp.zeros((local_cols - band_reach, band_reach), jnp.float32)
    right_window = jnp.concatenate(
        [own_block, jnp.concatenate([filler, cross_part], axis=0)], axis=1
    )
    upper_band = lax.psum(band_of(right_window, TILE, BMAX + 1), "smp")
    upper_tiles = upper_band.reshape(build_tiles, TILE, BMAX + 1, TILE)
    preceding = passed_along(upper_tiles[build_tiles - BMAX :], ("snp", "pair"), 1)
    extended = jnp.concatenate([preceding, upper_tiles], axis=0)
    pieces = []
    for tile_lag in range(BMAX, 0, -1):
        source = extended[BMAX - tile_lag : BMAX - tile_lag + build_tiles, :, tile_lag, :]
        pieces.append(jnp.transpose(source, (0, 2, 1)))
    pieces.append(upper_tiles.reshape(build_tiles, TILE, (BMAX + 1) * TILE))
    gram_band = jnp.concatenate(pieces, axis=2).reshape(local_cols, (2 * BMAX + 1) * TILE)
    samples_total = dosage.shape[0] * lax.axis_size("smp")
    ld_next = local_mask(band_next, column_place, build_tiles) * gram_band / samples_total
    row_place = lax.axis_index("smp")
    local_rows = ld_prev.shape[0]
    solver_tiles = local_rows // TILE
    seen_here = jnp.repeat(observed.astype(jnp.float32), TBLK, axis=1)
    matrix = local_mask(band_prev, row_place, solver_tiles) * ld_prev
    rhs = seen_here * zscores
    solution = jnp.zeros_like(rhs)
    residual = rhs
    direction = rhs
    norm_now = squares(residual)
    for turn_index in range(ITERS):
        image = operate(matrix, seen_here, direction)
        curve = lax.psum(jnp.sum(direction * image, axis=0), "smp")
        step_size = norm_now / curve
        solution = solution + step_size * direction
        residual = residual - step_size * image
        norm_next = squares(residual)
        direction = residual + norm_next / norm_now * direction
        norm_now = norm_next
    imputed = apply_band(matrix, seen_here * solution)
    return (ld_next, imputed)


def solution(mesh):
    return jax.shard_map(
        local,
        mesh=mesh,
        in_specs=(
            P(("grp", "smp"), ("snp", "pair")),
            P("grp"),
            P("grp"),
            P("grp"),
            P(("grp", "smp"), None),
            P("grp"),
            P(("grp", "smp"), ("snp", "pair")),
            P(("grp", "smp"), ("snp", "pair")),
        ),
        out_specs=(P(("grp", "snp", "pair"), None), P(("grp", "smp"), ("snp", "pair"))),
        check_vma=False,
    )
```

profile of v0, /device:TPU:0, one launch (start us, length us, event | category | flops | bytes accessed | tf_op | source)
XLA Modules:
  0.0 322.8 jit_solution(3432829513353105369)
XLA Ops:
  8.6 3.4 %multiply_convert_fusion = bf16[2048,1024]{1,0:T(8,128)(2,1)S(1)} fusion(bf16[2048,1024]{1,0:T(8,128)(2,1)} %param.8, f32[1024]{0:T(1024)S(1)} %dynamic_slice.14, f32[1024]{0:T(1024)S(1)} %dynamic_slice.13), kind=kLoop, calls=%fused_computation.3 | loop fusion | flops 8388608 | bytes 8396800 | tf_op jit(solution)/shard_map/convert_element_type | solution.py:106
  16.1 5.7 %collective-permute-start.2 = (f32[128,128]{0,1:T(8,128)S(1)}, f32[128,128]{0,1:T(8,128)S(1)}, u32[]{:S(2)}, u32[]{:S(2)}) collective-permute-start(f32[128,128]{0,1:T(8,128)S(1)} %get-tuple-element.48), channel_id=1, source_target_pairs={{0,4},{4,8},{8,12},{1,5},{5,9},{9,13},{2,6},{6,10},{10,14},{3,7},{... | collective-permute-start | bytes 196616 | tf_op jit(solution)/shard_map/ppermute | solution.py:23
  21.8 10.0 %fusion.25 = f32[1024,1024]{0,1:T(8,128)} fusion(bf16[2048,1024]{1,0:T(8,128)(2,1)} %copy-done.3), kind=kOutput, calls=%fused_computation.111 | convolution fusion | flops 4294967296 | bytes 8388608 | tf_op jit(solution)/shard_map/dot_general | solution.py:66
  39.2 2.0 copy.59
  42.5 2.0 copy.62
  44.5 1.9 constant_dynamic-update-slice_fusion.3
  49.0 3.8 %fusion.26 = f32[16,64,128]{2,1,0:T(8,128)S(1)} fusion(f32[16,64,320]{2,1,0:T(8,128)S(1)} %bitcast.156, f32[16,320,128]{2,1,0:T(8,128)} %constant_dynamic-update-slice_fusion), kind=kOutput, calls=%fused_computation.112 | convolution fusion | flops 503316480 | bytes 4456448 | tf_op jit(solution)/shard_map/uio,uot->uit/dot_general | solution.py:78
  53.2 10.4 %all-reduce.3 = (f32[128]{0:T(128)S(1)}, f32[128]{0:T(128)S(1)}) all-reduce(f32[128]{0:T(128)S(1)} %get-tuple-element.5, f32[128]{0:T(128)S(1)} %get-tuple-element.4), channel_id=1, replica_groups=mesh['grp'=2,'smp'=4,'snp'=2,'pair'=2] {'smp'}, use_global_device_ids=true, to_apply=%region_2.3 | all-reduce | flops 256 | bytes 2048 | tf_op jit(solution)/shard_map/psum | solution.py:95
  63.9 9.0 %psum.52 = f32[128]{0:T(128)S(1)} all-reduce(f32[128]{0:T(128)S(1)} %multiply_reduce_fusion.2), channel_id=1, replica_groups=mesh['grp'=2,'smp'=4,'snp'=2,'pair'=2] {'smp'}, use_global_device_ids=true, to_apply=%region_6.7 | all-reduce | flops 128 | bytes 1024 | tf_op jit(solution)/shard_map/psum | solution.py:95
  75.3 4.7 %collective-permute-start.4 = (f32[128,128]{0,1:T(8,128)S(1)}, f32[128,128]{0,1:T(8,128)S(1)}, u32[]{:S(2)}, u32[]{:S(2)}) collective-permute-start(f32[128,128]{0,1:T(8,128)S(1)} %get-tuple-element.44), channel_id=1, source_target_pairs={{0,4},{4,8},{8,12},{1,5},{5,9},{9,13},{2,6},{6,10},{10,14},{3,7},{... | collective-permute-start | bytes 196616 | tf_op jit(solution)/shard_map/ppermute | solution.py:23
  80.3 2.0 copy.66
  82.3 3.4 %pad_maximum_fusion.5 = (f32[1024,128]{0,1:T(8,128)}, f32[1024,128]{0,1:T(8,128)}, f32[1024,128]{0,1:T(8,128)}, f32[1024,128]{0,1:T(8,128)}) fusion(f32[128,128]{0,1:T(8,128)S(1)} %collective-permute-done.5, f32[1024,128]{0,1:T(8,128)} %copy-done.2, f32[128,128]{0,1:T(8,128)S(1)} %collective-permute-done.4), kind=kLoop, calls=%fused_computation.55 | loop fusion | flops 524288 | bytes 2752512 | tf_op jit(solution)/shard_map/concatenate | solution.py:21
  85.7 2.0 copy.64
  89.6 2.0 copy.65
  91.7 2.0 copy.67
  93.7 2.1 copy.68
  95.8 1.9 constant_dynamic-update-slice_fusion.8
  102.4 4.5 %fusion.27 = f32[16,64,128]{2,1,0:T(8,128)} fusion(f32[16,64,320]{2,1,0:T(8,128)S(1)} %bitcast.157, f32[16,320,128]{2,1,0:T(8,128)} %constant_dynamic-update-slice_fusion.5), kind=kOutput, calls=%fused_computation.113 | convolution fusion | flops 503316480 | bytes 4456448 | tf_op jit(solution)/shard_map/uio,uot->uit/dot_general | solution.py:78
  106.9 2.1 copy.69
  110.2 10.3 %psum.53 = f32[128]{0:T(128)S(1)} all-reduce(f32[128]{0:T(128)S(1)} %multiply_reduce_fusion.1), channel_id=1, replica_groups=mesh['grp'=2,'smp'=4,'snp'=2,'pair'=2] {'smp'}, use_global_device_ids=true, to_apply=%region_8.9 | all-reduce | flops 128 | bytes 1024 | tf_op jit(solution)/shard_map/psum | solution.py:138
  120.6 2.2 multiply_reduce_fusion
  122.7 8.6 %psum.54 = f32[128]{0:T(128)S(1)} all-reduce(f32[128]{0:T(128)S(1)} %get-tuple-element.8), channel_id=1, replica_groups=mesh['grp'=2,'smp'=4,'snp'=2,'pair'=2] {'smp'}, use_global_device_ids=true, to_apply=%region_10.11 | all-reduce | flops 128 | bytes 1024 | tf_op jit(solution)/shard_map/psum | solution.py:95
  133.8 4.5 %collective-permute-start.6 = (f32[128,128]{0,1:T(8,128)S(1)}, f32[128,128]{0,1:T(8,128)S(1)}, u32[]{:S(2)}, u32[]{:S(2)}) collective-permute-start(f32[128,128]{0,1:T(8,128)S(1)} %get-tuple-element.40), channel_id=1, source_target_pairs={{0,4},{4,8},{8,12},{1,5},{5,9},{9,13},{2,6},{6,10},{10,14},{3,7},{... | collective-permute-start | bytes 196616 | tf_op jit(solution)/shard_map/ppermute | solution.py:23
  142.0 2.0 copy.70
  144.0 2.0 constant_dynamic-update-slice_fusion.14
  146.0 2.0 copy.71
  148.0 2.0 copy.73
  150.0 2.1 copy.74
  152.1 1.9 constant_dynamic-update-slice_fusion.13
  157.6 4.6 %fusion.28 = f32[16,64,128]{2,1,0:T(8,128)} fusion(f32[16,64,320]{2,1,0:T(8,128)S(1)} %bitcast.158, f32[16,320,128]{2,1,0:T(8,128)} %constant_dynamic-update-slice_fusion.10), kind=kOutput, calls=%fused_computation.114 | convolution fusion | flops 503316480 | bytes 4456448 | tf_op jit(solution)/shard_map/uio,uot->uit/dot_general | solution.py:78
  162.2 2.1 copy.75
  165.6 11.5 %psum.55 = f32[128]{0:T(128)S(1)} all-reduce(f32[128]{0:T(128)S(1)} %fusion.16), channel_id=1, replica_groups=mesh['grp'=2,'smp'=4,'snp'=2,'pair'=2] {'smp'}, use_global_device_ids=true, to_apply=%region_12.13 | all-reduce | flops 128 | bytes 1024 | tf_op jit(solution)/shard_map/psum | solution.py:138
  178.2 2.1 copy.78
  183.1 4.8 %collective-permute-start.8 = (f32[128,128]{0,1:T(8,128)S(1)}, f32[128,128]{0,1:T(8,128)S(1)}, u32[]{:S(2)}, u32[]{:S(2)}) collective-permute-start(f32[128,128]{0,1:T(8,128)S(1)} %get-tuple-element.36), channel_id=1, source_target_pairs={{0,4},{4,8},{8,12},{1,5},{5,9},{9,13},{2,6},{6,10},{10,14},{3,7},{... | collective-permute-start | bytes 196616 | tf_op jit(solution)/shard_map/ppermute | solution.py:23
  189.4 5.1 %select_maximum_fusion = f32[1024,1152]{0,1:T(8,128)} fusion(f32[128,128]{0,1:T(8,128)S(1)} %fusion.18, f32[1024,1024]{0,1:T(8,128)} %fusion.25), kind=kLoop, calls=%fused_computation.4 | loop fusion | flops 3538944 | bytes 8978432 | tf_op jit(solution)/shard_map/concatenate | solution.py:111
  194.5 8.2 %reshape.85 = f32[16,64,18,64]{1,0,3,2:T(8,128)} reshape(f32[1024,1152]{0,1:T(8,128)} %select_maximum_fusion) | data formatting | bytes 9437184 | tf_op jit(solution)/shard_map/reshape | solution.py:41
  202.6 17.3 %fusion.20 = (f32[16,64,16,64]{1,0,3,2:T(8,128)}, f32[16,64,16,64]{1,0,3,2:T(8,128)}, f32[16,64,16,64]{1,0,3,2:T(8,128)}) fusion(f32[16,64,18,64]{1,0,3,2:T(8,128)} %reshape.85), kind=kLoop, calls=%fused_computation.106 | loop fusion | bytes 25165824 | tf_op jit(solution)/shard_map/slice | solution.py:44
  220.0 8.7 %copy.83 = f32[16,64,16,64]{3,1,2,0:T(8,128)} copy(f32[16,64,16,64]{1,0,3,2:T(8,128)} %get-tuple-element.14) | data formatting | bytes 8388608
  228.6 8.7 %copy.82 = f32[16,64,16,64]{3,1,2,0:T(8,128)} copy(f32[16,64,16,64]{1,0,3,2:T(8,128)} %get-tuple-element.13) | data formatting | bytes 8388608
  237.3 4.0 %gather_fusion.2 = f32[16,64,64]{2,1,0:T(8,128)S(1)} fusion(f32[64,64,16,16]{1,0,3,2:T(8,128)} %bitcast.160, s32[16]{0:T(128)S(1)} %or_bitcast_fusion), kind=kCustom, calls=%fused_computation.2 | custom fusion | bytes 524416 | tf_op jit(solution)/shard_map/jit(diagonal)/gather | solution.py:44
  241.3 4.0 %gather_fusion.1 = f32[16,64,64]{2,1,0:T(8,128)S(1)} fusion(f32[64,64,16,16]{1,0,3,2:T(8,128)} %bitcast.161, s32[16]{0:T(128)S(1)} %or_bitcast_fusion), kind=kCustom, calls=%fused_computation.1 | custom fusion | bytes 524416 | tf_op jit(solution)/shard_map/jit(diagonal)/gather | solution.py:44
  245.3 8.7 %copy.81 = f32[16,64,16,64]{3,1,2,0:T(8,128)} copy(f32[16,64,16,64]{1,0,3,2:T(8,128)} %get-tuple-element.12) | data formatting | bytes 8388608
  254.0 4.0 %gather_fusion = f32[16,64,64]{2,1,0:T(8,128)S(1)} fusion(f32[64,64,16,16]{1,0,3,2:T(8,128)} %bitcast.162, s32[16]{0:T(128)S(1)} %or_bitcast_fusion), kind=kCustom, calls=%fused_computation | custom fusion | bytes 524416 | tf_op jit(solution)/shard_map/jit(diagonal)/gather | solution.py:44
  259.2 2.5 copy.53
  263.1 2.0 copy.76
  273.9 30.7 %all-reduce.6.cloned.1.call-done = f32[1024,192]{0,1:T(8,128)} async-done(((f32[1024,192]{0,1:T(8,128)}), f32[1024,192]{0,1:T(8,128)}) %all-reduce.6.cloned.1.call-update) | async-done | bytes 786448 | tf_op jit(solution)/shard_map/psum | solution.py:114
  305.7 2.0 collective-permute-start.1
  307.7 4.5 %fusion.29 = f32[16,64,128]{2,1,0:T(8,128)} fusion(f32[16,64,320]{2,1,0:T(8,128)S(1)} %bitcast.159, f32[16,320,128]{2,1,0:T(8,128)} %constant_dynamic-update-slice_fusion.15), kind=kOutput, calls=%fused_computation.115 | convolution fusion | flops 503316480 | bytes 4456448 | tf_op jit(solution)/shard_map/uio,uot->uit/dot_general | solution.py:78
  (121 shorter events, 60.3 us)
Async XLA Ops:
  7.2 297.4 %all-reduce.6.cloned.1.call-start = ((), (), s32[]{:S(2)}) async-start(), calls=%async_computation | async-start | bytes 1572864 | tf_op jit(solution)/shard_map/psum | solution.py:114
  8.6 5.8 %copy-start.12 = (s32[1024,2]{0,1:T(2,128)S(1)}, s32[1024,2]{0,1:T(2,128)}, u32[]{:S(2)}) copy-start(s32[1024,2]{0,1:T(2,128)} %param.15) | copy-start | bytes 24580
  8.6 5.8 %copy-start.11 = (f32[1024,128]{1,0:T(8,128)S(1)}, f32[1024,128]{1,0:T(8,128)}, u32[]{:S(2)}) copy-start(f32[1024,128]{1,0:T(8,128)} %param.14) | copy-start | bytes 1572868
  12.0 2.4 copy-start.3
  13.1 174.7 %collective-permute-start = (bf16[2048,128]{1,0:T(8,128)(2,1)}, bf16[2048,128]{1,0:T(8,128)(2,1)}, u32[]{:S(2)}, u32[]{:S(2)}) collective-permute-start(bf16[2048,128]{1,0:T(8,128)(2,1)} %slice.273), channel_id=1, source_target_pairs={{1,0},{2,1},{3,2},{5,4},{6,5},{7,6},{9,8},{10,9},{11,10},{13,12},{... | collective-permute-start | bytes 1572872 | tf_op jit(solution)/shard_map/ppermute | solution.py:35
  14.7 20.7 %collective-permute-start.3 = (f32[128,128]{0,1:T(8,128)S(1)}, f32[128,128]{0,1:T(8,128)S(1)}, u32[]{:S(2)}, u32[]{:S(2)}) collective-permute-start(f32[128,128]{0,1:T(8,128)S(1)} %get-tuple-element.47), channel_id=1, source_target_pairs={{4,0},{8,4},{12,8},{5,1},{9,5},{13,9},{6,2},{10,6},{14,10},{7,3},{... | collective-permute-start | bytes 196616 | tf_op jit(solution)/shard_map/ppermute | solution.py:25
  16.0 15.9 %copy-start.13 = (s32[64]{0:T(128)S(1)}, s32[64]{0:T(128)}, u32[]{:S(2)}) copy-start(s32[64]{0:T(128)} %param.13) | copy-start | bytes 772
  16.1 15.9 %copy-start.14 = (s32[64]{0:T(128)S(1)}, s32[64]{0:T(128)}, u32[]{:S(2)}) copy-start(s32[64]{0:T(128)} %param.11) | copy-start | bytes 772
  16.1 16.3 %copy-start.10 = (f32[1024,320]{0,1:T(8,128)S(1)}, f32[1024,320]{0,1:T(8,128)}, u32[]{:S(2)}) copy-start(f32[1024,320]{0,1:T(8,128)} %param.12) | copy-start | bytes 3932164
  16.1 19.3 %collective-permute-start.2 = (f32[128,128]{0,1:T(8,128)S(1)}, f32[128,128]{0,1:T(8,128)S(1)}, u32[]{:S(2)}, u32[]{:S(2)}) collective-permute-start(f32[128,128]{0,1:T(8,128)S(1)} %get-tuple-element.48), channel_id=1, source_target_pairs={{0,4},{4,8},{8,12},{1,5},{5,9},{9,13},{2,6},{6,10},{10,14},{3,7},{... | collective-permute-start | bytes 196616 | tf_op jit(solution)/shard_map/ppermute | solution.py:23
  44.5 3.6 %copy-start.7 = (f32[1024,128]{1,0:T(8,128)S(1)}, f32[1024,128]{1,0:T(8,128)}, u32[]{:S(2)}) copy-start(f32[1024,128]{1,0:T(8,128)} %copy.62) | copy-start | bytes 1572868
  73.2 0.8 copy-start.2
  74.0 8.3 %collective-permute-start.5 = (f32[128,128]{0,1:T(8,128)S(1)}, f32[128,128]{0,1:T(8,128)S(1)}, u32[]{:S(2)}, u32[]{:S(2)}) collective-permute-start(f32[128,128]{0,1:T(8,128)S(1)} %get-tuple-element.43), channel_id=1, source_target_pairs={{4,0},{8,4},{12,8},{5,1},{9,5},{13,9},{6,2},{10,6},{14,10},{7,3},{... | collective-permute-start | bytes 196616 | tf_op jit(solution)/shard_map/ppermute | solution.py:25
  75.3 7.0 %collective-permute-start.4 = (f32[128,128]{0,1:T(8,128)S(1)}, f32[128,128]{0,1:T(8,128)S(1)}, u32[]{:S(2)}, u32[]{:S(2)}) collective-permute-start(f32[128,128]{0,1:T(8,128)S(1)} %get-tuple-element.44), channel_id=1, source_target_pairs={{0,4},{4,8},{8,12},{1,5},{5,9},{9,13},{2,6},{6,10},{10,14},{3,7},{... | collective-permute-start | bytes 196616 | tf_op jit(solution)/shard_map/ppermute | solution.py:23
  95.8 5.7 %copy-start.8 = (f32[1024,128]{1,0:T(8,128)S(1)}, f32[1024,128]{1,0:T(8,128)}, u32[]{:S(2)}) copy-start(f32[1024,128]{1,0:T(8,128)} %copy.68) | copy-start | bytes 1572868
  132.5 6.9 %collective-permute-start.7 = (f32[128,128]{0,1:T(8,128)S(1)}, f32[128,128]{0,1:T(8,128)S(1)}, u32[]{:S(2)}, u32[]{:S(2)}) collective-permute-start(f32[128,128]{0,1:T(8,128)S(1)} %get-tuple-element.39), channel_id=1, source_target_pairs={{4,0},{8,4},{12,8},{5,1},{9,5},{13,9},{6,2},{10,6},{14,10},{7,3},{... | collective-permute-start | bytes 196616 | tf_op jit(solution)/shard_map/ppermute | solution.py:25
  133.8 6.4 %collective-permute-start.6 = (f32[128,128]{0,1:T(8,128)S(1)}, f32[128,128]{0,1:T(8,128)S(1)}, u32[]{:S(2)}, u32[]{:S(2)}) collective-permute-start(f32[128,128]{0,1:T(8,128)S(1)} %get-tuple-element.40), channel_id=1, source_target_pairs={{0,4},{4,8},{8,12},{1,5},{5,9},{9,13},{2,6},{6,10},{10,14},{3,7},{... | collective-permute-start | bytes 196616 | tf_op jit(solution)/shard_map/ppermute | solution.py:23
  144.0 10.1 %copy-start.6 = (f32[1024,128]{1,0:T(8,128)S(1)}, f32[1024,128]{1,0:T(8,128)}, u32[]{:S(2)}) copy-start(f32[1024,128]{1,0:T(8,128)} %copy.72) | copy-start | bytes 1572868
  152.1 4.7 %copy-start.9 = (f32[1024,128]{1,0:T(8,128)S(1)}, f32[1024,128]{1,0:T(8,128)}, u32[]{:S(2)}) copy-start(f32[1024,128]{1,0:T(8,128)} %copy.74) | copy-start | bytes 1572868
  157.6 6.7 %copy-start = (f32[1024,128]{0,1:T(8,128)S(1)}, f32[1024,128]{0,1:T(8,128)}, u32[]{:S(2)}) copy-start(f32[1024,128]{0,1:T(8,128)} %get-tuple-element.9) | copy-start | bytes 1572868
  181.8 80.0 %collective-permute-start.9 = (f32[128,128]{0,1:T(8,128)}, f32[128,128]{0,1:T(8,128)S(1)}, u32[]{:S(2)}, u32[]{:S(2)}) collective-permute-start(f32[128,128]{0,1:T(8,128)} %get-tuple-element.35), channel_id=1, source_target_pairs={{4,0},{8,4},{12,8},{5,1},{9,5},{13,9},{6,2},{10,6},{14,10},{7,3},{... | collective-permute-start | bytes 196616 | tf_op jit(solution)/shard_map/ppermute | solution.py:25
  183.1 78.7 %collective-permute-start.8 = (f32[128,128]{0,1:T(8,128)S(1)}, f32[128,128]{0,1:T(8,128)S(1)}, u32[]{:S(2)}, u32[]{:S(2)}) collective-permute-start(f32[128,128]{0,1:T(8,128)S(1)} %get-tuple-element.36), channel_id=1, source_target_pairs={{0,4},{4,8},{8,12},{1,5},{5,9},{9,13},{2,6},{6,10},{10,14},{3,7},{... | collective-permute-start | bytes 196616 | tf_op jit(solution)/shard_map/ppermute | solution.py:23
  259.2 2.5 copy-start.1
  265.2 6.2 %copy-start.5 = (f32[1024,128]{1,0:T(8,128)S(1)}, f32[1024,128]{1,0:T(8,128)}, u32[]{:S(2)}) copy-start(f32[1024,128]{1,0:T(8,128)} %copy.78) | copy-start | bytes 1572868
  304.6 7.6 %copy-start.4 = (f32[1024,192]{0,1:T(8,128)S(1)}, f32[1024,192]{0,1:T(8,128)}, u32[]{:S(2)}) copy-start(f32[1024,192]{0,1:T(8,128)} %all-reduce.6.cloned.1.call-done) | copy-start | bytes 2359300
  305.7 6.9 %collective-permute-start.1 = (f32[2,64,3,64]{1,0,3,2:T(2,128)S(1)}, f32[2,64,3,64]{1,0,3,2:T(2,128)}, u32[]{:S(2)}, u32[]{:S(2)}) collective-permute-start(f32[2,64,3,64]{1,0,3,2:T(2,128)S(1)} %slice.215), channel_id=1, source_target_pairs={{0,1},{1,2},{2,3},{4,5},{5,6},{6,7},{8,9},{9,10},{10,11},{12,13},{... | collective-permute-start | bytes 294920 | tf_op jit(solution)/shard_map/ppermute | solution.py:35
Sparse Core Ops, SparseCore 0:
  261.9 42.6 all-reduce.5
where the time goes:
time: 327 us; the launch traced here: 323 us
  local copies, waits for them, and re-layouts  140 us (43%)
  blocking collectives  49.8 us (15%)
  waiting for transfers between devices  31.6 us (10%)
  other arithmetic  29.4 us (9%)
  matrix products  28.9 us (9%)
  starting transfers between devices  28.2 us (9%)
  between operations  14.5 us (4%)
    unnamed x50, local copies, waits for them, and re-layouts  51.3 us
    psum x1, waiting for transfers between devices, local(): upper_band = lax.psum(band_of(right_window, TILE, BMAX + 1), 'smp')  30.7 us
    psum x3, blocking collectives, squares(): return lax.psum(jnp.sum(residual * residual, axis=0), 'smp')  28 us
    slice x16, local copies, waits for them, and re-layouts, band_product(): stacked[offset:offset + tile_count]  27.4 us
    psum x2, blocking collectives, local(): curve = lax.psum(jnp.sum(direction * image, axis=0), 'smp')  21.8 us
    ppermute x4, starting transfers between devices, extended_2(): lax.ppermute(tail, axis, [(i, (i + 1) % count) for i in range(ends)])  19.8 us
    dot_general x4, matrix products, band_product(): jnp.einsum('uio,uot->uit', band_tiles, windows, precision=lax.Precision.H...  17.4 us
    slice x1, local copies, waits for them, and re-layouts, band_of(): blocks[:, :, offset:offset + tile_count, :]  17.3 us
  transfers between devices with their start and end apart: 11, of which 2 were waited for; matrix products, arithmetic and copies ran while one was open for 58% of the time, Pallas kernels for 0%

commit v1 on v0

v1 whole, which is shorter than its diff:
```python
import functools
import jax
import jax.numpy as jnp
from jax import lax
from jax.experimental import pallas as pl
from jax.experimental.pallas import tpu as pltpu
from jax.sharding import PartitionSpec as P

TILE = 64
BMAX = 2
TBLK = 64
ITERS = 3
RIDGE = 1.0
SPAN = 2 * BMAX + 1
REACH = TILE * BMAX
LANE = 128
QW = 256
HZ = ITERS * REACH
HB = (ITERS - 1) * REACH
TINY = 1e-6
VMEM_LIMIT = 60 * 1024 * 1024
VMEM = pl.BlockSpec(memory_space=pltpu.VMEM)
SMEM = pl.BlockSpec(memory_space=pltpu.SMEM)


def params(**kw):
    return pltpu.CompilerParams(vmem_limit_bytes=VMEM_LIMIT, **kw)


def mask_rows(band_ref, first_tile, total):
    def width(t):
        inside = (t >= 0) & (t < total)
        return jnp.where(inside, band_ref[jnp.clip(t, 0, total - 1)], 0)

    widths = [width(first_tile + d) for d in range(-BMAX, BMAX + 2)]
    low = lax.broadcasted_iota(jnp.int32, (1, LANE), 1) < TILE
    rows = []
    for q in range(-BMAX, BMAX + 1):
        flags = [
            (abs(q) <= jnp.minimum(widths[BMAX + t], widths[BMAX + t + q])).astype(jnp.float32)
            for t in range(2)
        ]
        rows.append(jnp.where(low, flags[0], flags[1]))
    return rows


def low_lanes(shape):
    return lax.broadcasted_iota(jnp.int32, shape, 1) < TILE


def tdot(left, right):
    return lax.dot_general(
        left, right, (((0,), (0,)), ((), ())), preferred_element_type=jnp.float32
    )


def dot(left, right):
    return lax.dot_general(
        left, right, (((1,), (0,)), ((), ())), preferred_element_type=jnp.float32
    )


def gram_kernel(
    parts, rot, inv, meta, own, ahead, right, left, first, mean, scale, *rest
):
    outs = rest[:parts]
    normed, cross = rest[parts:]
    g = pl.program_id(0)
    quarter = lax.rem(g + meta[0], parts) if rot else g
    blocks = QW // LANE
    base = meta[1]
    lanes_total = mean.shape[0]

    def standard(values, block):
        row = jnp.clip(block, 0, lanes_total - 1)
        m = mean[pl.ds(row, 1), :]
        s = scale[pl.ds(row, 1), :]
        return ((values.astype(jnp.float32) - m) * s).astype(jnp.bfloat16)

    for b in range(blocks):
        cols = slice(b * LANE, (b + 1) * LANE)
        normed[:, cols] = standard(own[:, cols], base + quarter * blocks + b)
    beyond = base + (quarter + 1) * blocks
    tail = slice(QW, QW + LANE)

    @pl.when(quarter == parts - 1)
    def _():
        normed[:, tail] = standard(right[...], beyond)

    @pl.when(quarter != parts - 1)
    def _():
        normed[:, tail] = standard(ahead[...], beyond)

    @pl.when(g == 0)
    def _():
        cross[...] = inv * tdot(standard(left[...], base - 1), standard(first[...], base))

    full = tdot(normed[...], normed[:, :QW])
    rows = (BMAX + 1) * TILE
    low = low_lanes((rows, LANE))
    pieces = []
    for b in range(blocks):
        cols = slice(b * LANE, (b + 1) * LANE)
        pieces.append(
            inv
            * jnp.where(
                low,
                full[b * LANE : b * LANE + rows, cols],
                full[b * LANE + TILE : b * LANE + TILE + rows, cols],
            )
        )
    share = LANE // parts // blocks
    start = pl.multiple_of(quarter * (share * blocks), 8)
    shares = [cross[pl.ds(pl.multiple_of(start + b * share, 8), share), :] for b in range(blocks)]
    for i in range(parts):

        @pl.when(g == i)
        def _(i=i):
            for b in range(blocks):
                cols = slice(b * LANE, (b + 1) * LANE)
                outs[i][0:rows, cols] = pieces[b]
                outs[i][rows : rows + share, cols] = shares[b]


def gram_parts(dosage, left, right, mean, scale, k, column_place, rot, inv):
    samples, cols = dosage.shape
    parts = cols // QW
    blocks = QW // LANE
    total = cols // LANE
    height = (BMAX + 1) * TILE + LANE // parts // blocks
    meta = jnp.stack([k, column_place * total]).astype(jnp.int32)

    def quarter(g, m):
        return lax.rem(g + m[0], parts) if rot else g

    fixed = lambda g, m: (0, 0)
    grid_spec = pltpu.PrefetchScalarGridSpec(
        num_scalar_prefetch=1,
        grid=(parts,),
        in_specs=[
            pl.BlockSpec((samples, QW), lambda g, m: (0, quarter(g, m))),
            pl.BlockSpec(
                (samples, LANE),
                lambda g, m: (0, jnp.minimum((quarter(g, m) + 1) * blocks, total - 1)),
            ),
            pl.BlockSpec((samples, LANE), fixed),
            pl.BlockSpec((samples, LANE), fixed),
            pl.BlockSpec((samples, LANE), fixed),
            pl.BlockSpec((mean.shape[0] // LANE, LANE), fixed),
            pl.BlockSpec((mean.shape[0] // LANE, LANE), fixed),
        ],
        out_specs=[pl.BlockSpec((height, QW), fixed) for _ in range(parts)],
        scratch_shapes=[
            pltpu.VMEM((samples, QW + LANE), jnp.bfloat16),
            pltpu.VMEM((LANE, LANE), jnp.float32),
        ],
    )
    return pl.pallas_call(
        functools.partial(gram_kernel, parts, rot, inv),
        grid_spec=grid_spec,
        out_shape=[jax.ShapeDtypeStruct((height, QW), jnp.float32) for _ in range(parts)],
        compiler_params=params(dimension_semantics=("arbitrary",)),
        cost_estimate=pl.CostEstimate(
            flops=2 * samples * cols * (QW + LANE), bytes_accessed=dosage.size * 4, transcendentals=0
        ),
        name="gram",
    )(
        meta,
        dosage,
        dosage,
        right,
        left,
        dosage,
        mean.reshape(-1, LANE),
        scale.reshape(-1, LANE),
    )


def assemble_kernel(parts, rot, tile_total, meta, band, *rest):
    ins = rest[:parts]
    out = rest[parts]
    blocks = QW // LANE
    rows = (BMAX + 1) * TILE
    low = low_lanes((TILE, LANE))
    share = LANE // parts // blocks
    for quarter in range(parts):

        def fetch(row, count, b, quarter=quarter):
            cols = slice(b * LANE, (b + 1) * LANE)
            return ins[quarter][row : row + count, cols]

        for b in range(blocks):
            a = quarter * blocks + b
            cols = slice(a * LANE, (a + 1) * LANE)
            masks = mask_rows(band, meta[1] + 2 * a, tile_total)
            for q in range(BMAX + 1):
                out[(BMAX + q) * TILE : (BMAX + q + 1) * TILE, cols] = (
                    fetch(q * TILE, TILE, b) * masks[BMAX + q]
                )
            turned = fetch(TILE, 2 * TILE, b).T
            rolled = pltpu.roll(turned, TILE, axis=1)
            if a == 0:
                count = LANE // share
                cross = [
                    ins[j // blocks][
                        rows : rows + share, (j % blocks) * LANE : (j % blocks + 1) * LANE
                    ]
                    for j in range(count)
                ]
                cross = jnp.concatenate(cross, axis=0)
                one_low, two_low, two_high = cross[TILE:], cross[:TILE], cross[TILE:]
            else:
                one_low, two_low, two_high = last_turned[TILE:], last_rolled[:TILE], last_turned[TILE:]
            out[TILE : 2 * TILE, cols] = jnp.where(low, one_low, rolled[:TILE]) * masks[1]
            out[0:TILE, cols] = jnp.where(low, two_low, two_high) * masks[0]
            last_turned, last_rolled = turned, rolled


def assemble(pieces, band_next, first_tile, cols):
    parts = len(pieces)
    meta = jnp.stack([first_tile * 0, first_tile]).astype(jnp.int32)
    return pl.pallas_call(
        functools.partial(assemble_kernel, parts, False, band_next.shape[0]),
        in_specs=[SMEM, SMEM] + [VMEM] * parts,
        out_specs=VMEM,
        out_shape=jax.ShapeDtypeStruct((SPAN * TILE, cols), jnp.float32),
        compiler_params=params(),
        name="assemble",
    )(meta, band_next, *pieces)


def krylov_kernel(
    tile_total, sb, meta, band, ldt, z, obs, halo_l, halo_r, w_out, mom_out,
    dh, dl, ucat, seen, u_prev, y
):
    rows = ldt.shape[1]
    traits = z.shape[1]
    own_blocks = rows // LANE
    zb = HZ // LANE
    bb = HB // LANE
    first_tile = meta[0]
    nb = obs.shape[0]
    ld_rows = SPAN * TILE
    total_blocks = own_blocks + 2 * zb

    for c in range(total_blocks):
        if c < zb:
            vec = halo_l[c * LANE : (c + 1) * LANE, :traits]
            flags = [
                halo_l[HZ + bb * ld_rows + c * nb + i : HZ + bb * ld_rows + c * nb + i + 1, :]
                for i in range(nb)
            ]
        elif c < zb + own_blocks:
            o = c - zb
            vec = z[o * LANE : (o + 1) * LANE, :]
            flags = [
                obs[i : i + 1, o * LANE : (o + 1) * LANE].astype(jnp.float32) for i in range(nb)
            ]
        else:
            o = c - zb - own_blocks
            vec = halo_r[o * LANE : (o + 1) * LANE, :traits]
            flags = [
                halo_r[HZ + bb * ld_rows + o * nb + i : HZ + bb * ld_rows + o * nb + i + 1, :]
                for i in range(nb)
            ]
        wide = jnp.concatenate(
            [jnp.broadcast_to(f, (TBLK, LANE)) for f in flags], axis=0
        )
        mask = wide.T
        here = slice(c * LANE, (c + 1) * LANE)
        seen[here, :] = mask
        start = mask * vec
        high = start.astype(jnp.bfloat16)
        u_prev[here, :] = start
        ucat[here, :traits] = high
        ucat[here, traits:] = (start - high.astype(jnp.float32)).astype(jnp.bfloat16)

    per = sb // LANE
    low = low_lanes((TILE, LANE))
    sub = lax.broadcasted_iota(jnp.int32, (TILE, LANE), 0)
    lane = lax.broadcasted_iota(jnp.int32, (TILE, LANE), 1)
    chunks = SPAN + 1
    for c in range(own_blocks + 2 * bb):
        if c < bb:
            get = lambda q, c=c: halo_l[HZ + c * ld_rows + q * TILE : HZ + c * ld_rows + (q + 1) * TILE, :]
        elif c < bb + own_blocks:
            get = lambda q, c=c: ldt[q * TILE : (q + 1) * TILE, (c - bb) * LANE : (c - bb + 1) * LANE]
        else:
            o = c - bb - own_blocks
            get = lambda q, o=o: halo_r[HZ + o * ld_rows + q * TILE : HZ + o * ld_rows + (q + 1) * TILE, :]
        masks = mask_rows(band, first_tile + 2 * (c - bb), tile_total)
        s, h = c // per, c % per
        cols = slice(h * LANE, (h + 1) * LANE)
        parts = [get(q) * masks[q] for q in range(SPAN)]
        zero = jnp.zeros((TILE, LANE), jnp.float32)
        for j in range(chunks):
            left = parts[j] if j < SPAN else zero
            right = parts[j - 1] if j >= 1 else zero
            value = jnp.where(low, left, right)
            if BMAX <= j < BMAX + 2:
                value = value - (sub + TILE * (j - BMAX) == lane).astype(jnp.float32)
            high = value.astype(jnp.bfloat16)
            at = slice(h * LANE + j * TILE, h * LANE + (j + 1) * TILE)
            dh[s, at, cols] = high
            dl[s, at, cols] = (value - high.astype(jnp.float32)).astype(jnp.bfloat16)
        for x in range(per):
            if x < h:
                at = slice(x * LANE, (x + 1) * LANE)
            elif x > h:
                at = slice((x + 2) * LANE, (x + 3) * LANE)
            else:
                continue
            blank = jnp.zeros((LANE, LANE), jnp.bfloat16)
            dh[s, at, cols] = blank
            dl[s, at, cols] = blank

    supers = (rows + 2 * HB) // sb
    window = sb + 2 * REACH

    def product(both, rest):
        return both[:, :traits] + both[:, traits:] + rest

    def apply():
        for s in range(supers):
            vec = ucat[REACH + s * sb : REACH + (s + 1) * sb, :]
            part = product(dot(dh[s], vec), dot(dl[s], vec[:, :traits]))
            at = s * sb
            if s == 0:
                y[at : at + window, :] = part
            else:
                y[at : at + 2 * REACH, :] += part[: 2 * REACH]
                y[at + 2 * REACH : at + window, :] = part[2 * REACH :]

    own = slice(HZ, HZ + rows)
    sums = []
    for step in range(ITERS):
        apply()
        if step == 0:
            for edge_rows, edge_cols, s, target, source in (
                (slice(0, LANE), slice(0, LANE), 0, 1, 0),
                (
                    slice(window - LANE, window),
                    slice(sb - LANE, sb),
                    supers - 1,
                    total_blocks - 2,
                    total_blocks - 1,
                ),
            ):
                vec = ucat[source * LANE : (source + 1) * LANE, :]
                part = product(
                    tdot(dh[s, edge_rows, edge_cols], vec),
                    tdot(dl[s, edge_rows, edge_cols], vec[:, :traits]),
                )
                y[target * LANE : (target + 1) * LANE, :] += part
        u_own = u_prev[own, :]
        y_own = y[own, :]
        w_out[step] = u_own + y_own
        sums.append(jnp.sum(u_own * u_own, axis=0, keepdims=True))
        sums.append(jnp.sum(u_own * y_own, axis=0, keepdims=True))
        if step < ITERS - 1:
            edge = (step + 1) * REACH
            here = slice(edge, total_blocks * LANE - edge)
            nxt = seen[here, :] * y[here, :]
            high = nxt.astype(jnp.bfloat16)
            u_prev[here, :] = nxt
            ucat[here, :traits] = high
            ucat[here, traits:] = (nxt - high.astype(jnp.float32)).astype(jnp.bfloat16)
    mom_out[...] = jnp.concatenate(
        sums + [jnp.zeros((8 - len(sums), traits), jnp.float32)], axis=0
    )


def krylov(ldt, z, obs, halo_l, halo_r, band_prev, first_tile):
    rows, traits = z.shape
    wide = rows + 2 * HB
    sb = 2 * LANE if wide % (2 * LANE) == 0 else LANE
    ext = rows + 2 * HZ
    supers = wide // sb
    meta = first_tile.reshape(1).astype(jnp.int32)
    return pl.pallas_call(
        functools.partial(krylov_kernel, band_prev.shape[0], sb),
        in_specs=[SMEM, SMEM] + [VMEM] * 5,
        out_specs=[VMEM, VMEM],
        out_shape=[
            jax.ShapeDtypeStruct((ITERS, rows, traits), jnp.float32),
            jax.ShapeDtypeStruct((8, traits), jnp.float32),
        ],
        scratch_shapes=[
            pltpu.VMEM((supers, sb + 2 * REACH, sb), jnp.bfloat16),
            pltpu.VMEM((supers, sb + 2 * REACH, sb), jnp.bfloat16),
            pltpu.VMEM((ext, 2 * traits), jnp.bfloat16),
            pltpu.VMEM((ext, traits), jnp.float32),
            pltpu.VMEM((ext, traits), jnp.float32),
            pltpu.VMEM((ext, traits), jnp.float32),
        ],
        compiler_params=params(),
        cost_estimate=pl.CostEstimate(
            flops=ITERS * 6 * ext * SPAN * TILE * traits, bytes_accessed=ldt.size * 4, transcendentals=0
        ),
        name="krylov",
    )(meta, band_prev, ldt, z, obs, halo_l, halo_r)


def combine_kernel(w, mom, out):
    m = [mom[i : i + 1, :] for i in range(2 * ITERS)]
    shift = 1.0 + RIDGE
    h = [shift * m[i] + m[i + 1] for i in range(2 * ITERS - 1)]
    d0 = h[0]
    l10 = h[1] / d0
    l20 = h[2] / d0
    d1 = h[2] - l10 * h[1]
    t12 = h[3] - l20 * h[1]
    ok1 = d1 > TINY * h[2]
    r1 = jnp.where(ok1, 1.0 / jnp.where(ok1, d1, 1.0), 0.0)
    l21 = t12 * r1
    d2 = h[4] - l20 * h[2] - l21 * t12
    ok2 = ok1 & (d2 > TINY * h[4])
    r2 = jnp.where(ok2, 1.0 / jnp.where(ok2, d2, 1.0), 0.0)
    z0 = m[0]
    z1 = m[1] - l10 * z0
    z2 = m[2] - l20 * z0 - l21 * z1
    c2 = z2 * r2
    c1 = z1 * r1 - l21 * c2
    c0 = z0 / d0 - l10 * c1 - l20 * c2
    out[...] = c0 * w[0] + c1 * w[1] + c2 * w[2]


def combine(w, mom):
    return pl.pallas_call(
        combine_kernel,
        in_specs=[VMEM, VMEM],
        out_specs=VMEM,
        out_shape=jax.ShapeDtypeStruct(w.shape[1:], jnp.float32),
        compiler_params=params(),
        name="combine",
    )(w, mom)


def packed(z, ldt, obs):
    z = jnp.pad(z, ((0, 0), (0, LANE - z.shape[1])))
    obs = obs.astype(jnp.float32)
    parts = [z]
    parts += [ldt[:, i : i + LANE] for i in range(0, ldt.shape[1], LANE)]
    parts += [obs[:, i : i + LANE] for i in range(0, obs.shape[1], LANE)]
    height = sum(p.shape[0] for p in parts)
    parts.append(jnp.zeros((-height % 8, LANE), jnp.float32))
    return jnp.concatenate(parts, axis=0)


def halos(z, ldt, obs, axis):
    count = lax.axis_size(axis)
    rows = z.shape[0]

    def shifted(value, by):
        pairs = [(i, i + by) for i in range(count) if 0 <= i + by < count]
        return lax.ppermute(value, axis, pairs)

    if rows >= HZ:
        last = packed(z[rows - HZ :], ldt[:, rows - HB :], obs[:, rows - HZ :])
        head = packed(z[:HZ], ldt[:, :HB], obs[:, :HZ])
        return shifted(last, 1), shifted(head, -1)

    def gather(value, width, dim):
        lefts, rights = [], []
        hop, have = 1, 0
        while have < width:
            take = min(rows, width - have)
            lefts.insert(0, shifted(lax.slice_in_dim(value, rows - take, rows, axis=dim), hop))
            rights.append(shifted(lax.slice_in_dim(value, 0, take, axis=dim), -hop))
            have += take
            hop += 1
        return jnp.concatenate(lefts, dim), jnp.concatenate(rights, dim)

    zs = gather(z, HZ, 0)
    lds = gather(ldt, HB, 1)
    seens = gather(obs, HZ, 1)
    return packed(zs[0], lds[0], seens[0]), packed(zs[1], lds[1], seens[1])


def local(dosage, allele_mean, snp_scale, band_next, ld_prev, band_prev, zscores, observed):
    samples, cols = dosage.shape
    rows = ld_prev.shape[0]
    n_smp = lax.axis_size("smp")
    k = lax.axis_index("smp")
    snp, pair = lax.axis_index("snp"), lax.axis_index("pair")
    n_snp, n_pair = lax.axis_size("snp"), lax.axis_size("pair")
    place = snp * n_pair + pair
    count = n_snp * n_pair

    ldt = ld_prev.T
    obs = observed.T
    halo_l, halo_r = halos(zscores, ldt, obs, "smp")

    line = ("snp", "pair")
    right = lax.ppermute(dosage[:, :LANE], line, [(i + 1, i) for i in range(count - 1)])
    left = lax.ppermute(dosage[:, cols - LANE :], line, [(i, i + 1) for i in range(count - 1)])

    parts = cols // QW
    rot = parts == n_smp
    inv = 1.0 / (samples * n_smp)
    blocks = gram_parts(dosage, left, right, allele_mean, snp_scale, k, place, rot, inv)
    if rot:
        cycle = lambda value, by: lax.ppermute(
            value, "smp", [(i, (i + by) % n_smp) for i in range(n_smp)]
        )
        total = blocks[0]
        for by in range(1, n_smp):
            total = total + cycle(blocks[by].astype(jnp.float16), by).astype(jnp.float32)
        total = total.astype(jnp.float16)
        ring = [total] + [cycle(total, by) for by in range(1, n_smp)]
        stacked = jnp.stack(ring)
        pieces = [
            lax.dynamic_index_in_dim(stacked, lax.rem(k + n_smp - q, n_smp), 0, keepdims=False).astype(
                jnp.float32
            )
            for q in range(parts)
        ]
    else:
        pieces = lax.psum(tuple(blocks), "smp")
    ldn = assemble(pieces, band_next, place * (cols // TILE), cols)

    w, mom = krylov(ldt, zscores, obs, halo_l, halo_r, band_prev, k * (rows // TILE))
    imputed = combine(w, lax.psum(mom, "smp"))
    return ldn.T, imputed


def solution(mesh):
    return jax.shard_map(
        local,
        mesh=mesh,
        in_specs=(
            P(("grp", "smp"), ("snp", "pair")),
            P("grp"),
            P("grp"),
            P("grp"),
            P(("grp", "smp"), None),
            P("grp"),
            P(("grp", "smp"), ("snp", "pair")),
            P(("grp", "smp"), ("snp", "pair")),
        ),
        out_specs=(P(("grp", "snp", "pair"), None), P(("grp", "smp"), ("snp", "pair"))),
        check_vma=False,
    )
```

time: 327 us -> 68.9 us (0.21); the launches traced: 323 us -> 68.4 us
  local copies, waits for them, and re-layouts: 140 us -> 1.64 us
  blocking collectives: 49.8 us -> 10.9 us
  matrix products: 28.9 us -> 0 us
  other arithmetic: 29.4 us -> 6.14 us
  waiting for transfers between devices: 31.6 us -> 8.99 us
  Pallas kernels: 0 us -> 19.8 us
  between operations: 14.5 us -> 0.78 us
  starting transfers between devices: 28.2 us -> 20.1 us
    unnamed x50 -> x6, local copies, waits for them, and re-layouts: 51.3 us -> 0.02 us
    slice x24 -> x4, local copies, waits for them, and re-layouts: 48.4 us -> 1.5 us  [the longest x1 1.42 us: local(): dosage[:, cols - LANE:]]
    psum x5 -> x1, blocking collectives: 49.8 us -> 10.9 us  [local(): imputed = combine(w, lax.psum(mom, 'smp'))]
    psum x1 -> x0, waiting for transfers between devices: 30.7 us -> none  [local(): upper_band = lax.psum(band_of(right_window, TILE, BMAX + 1), 'smp')]
    dot_general x6 -> x0, matrix products: 28.9 us -> none  [the longest x4 17.4 us: band_product(): jnp.einsum('uio,uot->uit', band_tiles, windows, precision=lax.Precision.H...]
    pallas_call x0 -> x4, Pallas kernels: none -> 19.8 us  [the longest x1 8.68 us: gram_parts(): pl.pallas_call(functools.partial(gram_kernel, parts, rot, inv), grid_spec...]
    reshape x8 -> x0, local copies, waits for them, and re-layouts: 15.6 us -> none  [the longest x1 8.15 us: band_of(): window.reshape(tile_count, tile_size, tile_count + span - 1, tile_size)]
    concatenate x7 -> x0, other arithmetic: 14.5 us -> none  [the longest x4 8.14 us: extended_2(): jnp.concatenate([lax.ppermute(tail, axis, [(i, (i + 1) % count) for i in...]
  transfers between devices with their start and end apart: 11 -> 10, of which waited for: 2 -> 2; matrix products, arithmetic and copies ran while one was open for 58% -> 8% of each run, Pallas kernels for 0% -> 25%
where the time goes in v1:
time: 68.9 us; the launch traced here: 68.4 us
  starting transfers between devices  20.1 us (29%)
  Pallas kernels  19.8 us (29%)
  blocking collectives  10.9 us (16%)
  waiting for transfers between devices  8.99 us (13%)
  other arithmetic  6.14 us (9%)
  local copies, waits for them, and re-layouts  1.64 us (2%)
  between operations  0.78 us (1%)
    psum x1, blocking collectives, local(): imputed = combine(w, lax.psum(mom, 'smp'))  10.9 us
    ppermute x6, starting transfers between devices, local(): lax.ppermute(value, 'smp', [(i, (i + by) % n_smp) for i in range(n_smp)])  9.21 us
    ppermute x6, waiting for transfers between devices, local(): lax.ppermute(value, 'smp', [(i, (i + by) % n_smp) for i in range(n_smp)])  8.98 us
    pallas_call x1, Pallas kernels, gram_parts(): pl.pallas_call(functools.partial(gram_kernel, parts, rot, inv), grid_spec...  8.68 us
    ppermute x2, starting transfers between devices, shifted(): return lax.ppermute(value, axis, pairs)  6.4 us
    pallas_call x1, Pallas kernels, krylov(): pl.pallas_call(functools.partial(krylov_kernel, band_prev.shape[0], sb),...  6.15 us
    ppermute x1, starting transfers between devices, local(): lax.ppermute(dosage[:, cols - LANE:], line, [(i, i + 1) for i in range(co...  3.21 us
    convert_element_type x3, other arithmetic, local(): blocks[by].astype(jnp.float16)  2.84 us
  transfers between devices with their start and end apart: 10, of which 2 were waited for; matrix products, arithmetic and copies ran while one was open for 8% of the time, Pallas kernels for 25%

profile of v1, /device:TPU:0, one launch (start us, length us, event | category | flops | bytes accessed | tf_op | source)
XLA Modules:
  0.0 68.4 jit_solution(5106540491459051093)
XLA Ops:
  0.6 0.0 copy-start.2
  0.6 0.0 copy-start.1
  0.7 0.0 copy-start
  0.7 1.4 %fusion = (bf16[2048,128]{1,0:T(8,128)(2,1)S(1)}, bf16[2048,128]{1,0:T(8,128)(2,1)S(1)}) fusion(bf16[2048,1024]{1,0:T(8,128)(2,1)} %first.1), kind=kLoop, calls=%fused_computation.10 | loop fusion | bytes 2097152 | tf_op jit(solution)/shard_map/slice | solution.py:496
  2.1 3.2 %collective-permute-start.1 = (bf16[2048,128]{1,0:T(8,128)(2,1)S(1)}, bf16[2048,128]{1,0:T(8,128)(2,1)}, u32[]{:S(2)}, u32[]{:S(2)}) collective-permute-start(bf16[2048,128]{1,0:T(8,128)(2,1)S(1)} %get-tuple-element.14), channel_id=1, source_target_pairs={{0,1},{1,2},{2,3},{4,5},{5,6},{6,7},{8,9},{9,10},{10,11},{12,13},{... | collective-permute-start | bytes 1572872 | tf_op jit(solution)/shard_map/ppermute | solution.py:496
  5.3 1.3 %collective-permute-start = (bf16[2048,128]{1,0:T(8,128)(2,1)S(1)}, bf16[2048,128]{1,0:T(8,128)(2,1)}, u32[]{:S(2)}, u32[]{:S(2)}) collective-permute-start(bf16[2048,128]{1,0:T(8,128)(2,1)S(1)} %get-tuple-element.15), channel_id=1, source_target_pairs={{1,0},{2,1},{3,2},{5,4},{6,5},{7,6},{9,8},{10,9},{11,10},{13,12},{... | collective-permute-start | bytes 1572872 | tf_op jit(solution)/shard_map/ppermute | solution.py:495
  6.6 0.0 copy-done.2
  6.6 0.0 copy-done.1
  6.7 0.0 copy-done
  6.7 0.1 concatenate.6
  6.8 5.1 %collective-permute-start.8 = (f32[1032,128]{1,0:T(8,128)S(1)}, f32[1032,128]{1,0:T(8,128)}, u32[]{:S(2)}, u32[]{:S(2)}) collective-permute-start(f32[1032,128]{1,0:T(8,128)S(1)} %concatenate.6), channel_id=1, source_target_pairs={{0,4},{4,8},{8,12},{1,5},{5,9},{9,13},{2,6},{6,10},{10,14},{3,7},{... | collective-permute-start | bytes 1585160 | tf_op jit(solution)/shard_map/ppermute | solution.py:456
  11.9 0.1 concatenate.7
  12.0 1.3 %collective-permute-start.9 = (f32[1032,128]{1,0:T(8,128)S(1)}, f32[1032,128]{1,0:T(8,128)}, u32[]{:S(2)}, u32[]{:S(2)}) collective-permute-start(f32[1032,128]{1,0:T(8,128)S(1)} %concatenate.7), channel_id=1, source_target_pairs={{4,0},{8,4},{12,8},{5,1},{9,5},{13,9},{6,2},{10,6},{14,10},{7,3},{... | collective-permute-start | bytes 1585160 | tf_op jit(solution)/shard_map/ppermute | solution.py:456
  13.3 0.7 pad_add_fusion.1.meta
  13.9 0.0 collective-permute-done.1.left
  13.9 0.0 collective-permute-done.right
  14.0 8.7 %gram.1 = (f32[208,256]{1,0:T(8,128)}, f32[208,256]{1,0:T(8,128)}, f32[208,256]{1,0:T(8,128)}, f32[208,256]{1,0:T(8,128)}) custom-call(s32[2]{0:T(128)} %pad_add_fusion.1.meta, bf16[2048,1024]{1,0:T(8,128)(2,1)} %first.1, bf16[2048,1024]{1,0:T(8,128)(2,1)} %first.1, bf16[2048,128]{1,0:T(8,128)(2,1)} %collective-permute-done.right, ...), custom_call_target="tpu_custom_call" | custom-call | flops 1610612736 | bytes 8388608 | tf_op jit(solution)/shard_map/gram/pallas_call | solution.py:158
  22.6 0.9 %convert_element_type.47 = f16[208,256]{1,0:T(8,128)(2,1)S(1)} convert(f32[208,256]{1,0:T(8,128)} %get-tuple-element.9) | non-fusion elementwise | flops 53248 | bytes 319488 | tf_op jit(solution)/shard_map/convert_element_type | solution.py:508
  23.6 0.9 %convert_element_type.49 = f16[208,256]{1,0:T(8,128)(2,1)S(1)} convert(f32[208,256]{1,0:T(8,128)} %get-tuple-element.10) | non-fusion elementwise | flops 53248 | bytes 319488 | tf_op jit(solution)/shard_map/convert_element_type | solution.py:508
  24.5 0.9 %convert_element_type.51 = f16[208,256]{1,0:T(8,128)(2,1)S(1)} convert(f32[208,256]{1,0:T(8,128)} %get-tuple-element.11) | non-fusion elementwise | flops 53248 | bytes 319488 | tf_op jit(solution)/shard_map/convert_element_type | solution.py:508
  25.5 4.8 %collective-permute-start.4 = (f16[208,256]{1,0:T(8,128)(2,1)S(1)}, f16[208,256]{1,0:T(8,128)(2,1)S(1)}, u32[]{:S(2)}, u32[]{:S(2)}) collective-permute-start(f16[208,256]{1,0:T(8,128)(2,1)S(1)} %convert_element_type.51), channel_id=1, source_target_pairs={{0,12},{4,0},{8,4},{12,8},{1,13},{5,1},{9,5},{13,9},{2,14},{6,2},{... | collective-permute-start | bytes 319496 | tf_op jit(solution)/shard_map/ppermute | solution.py:503
  30.3 0.0 collective-permute-start.3
  30.3 0.6 collective-permute-start.2
  30.9 0.6 pad_add_fusion.meta
  31.5 1.1 %collective-permute-done.4 = f16[208,256]{1,0:T(8,128)(2,1)S(1)} collective-permute-done((f16[208,256]{1,0:T(8,128)(2,1)S(1)}, f16[208,256]{1,0:T(8,128)(2,1)S(1)}, u32[]{:S(2)}, u32[]{:S(2)}) %collective-permute-start.4) | collective-permute-done | bytes 106528 | tf_op jit(solution)/shard_map/ppermute | solution.py:503
  32.6 7.9 %collective-permute-done.3 = f16[208,256]{1,0:T(8,128)(2,1)S(1)} collective-permute-done((f16[208,256]{1,0:T(8,128)(2,1)S(1)}, f16[208,256]{1,0:T(8,128)(2,1)S(1)}, u32[]{:S(2)}, u32[]{:S(2)}) %collective-permute-start.3) | collective-permute-done | bytes 106528 | tf_op jit(solution)/shard_map/ppermute | solution.py:503
  40.4 0.0 collective-permute-done.2
  40.4 1.0 %add_convert_fusion = f16[208,256]{1,0:T(8,128)(2,1)S(1)} fusion(f16[208,256]{1,0:T(8,128)(2,1)S(1)} %collective-permute-done.4, f16[208,256]{1,0:T(8,128)(2,1)S(1)} %collective-permute-done.3, f32[208,256]{1,0:T(8,128)} %get-tuple-element.8, f16[208,256]{1,0:T(8,128)(2,1)S(1)} %collective-permute-done.2), kind=kLoop, calls=%fused_computation.1 | loop fusion | flops 372736 | bytes 638976 | tf_op jit(solution)/shard_map/convert_element_type | solution.py:509
  41.4 0.1 collective-permute-start.7
  41.5 1.8 %collective-permute-start.6 = (f16[208,256]{1,0:T(8,128)(2,1)S(1)}, f16[208,256]{1,0:T(8,128)(2,1)S(1)}, u32[]{:S(2)}, u32[]{:S(2)}) collective-permute-start(f16[208,256]{1,0:T(8,128)(2,1)S(1)} %add_convert_fusion), channel_id=1, source_target_pairs={{0,8},{4,12},{8,0},{12,4},{1,9},{5,13},{9,1},{13,5},{2,10},{6,14},... | collective-permute-start | bytes 319496 | tf_op jit(solution)/shard_map/ppermute | solution.py:503
  43.3 1.9 %collective-permute-start.5 = (f16[208,256]{1,0:T(8,128)(2,1)S(1)}, f16[208,256]{1,0:T(8,128)(2,1)S(1)}, u32[]{:S(2)}, u32[]{:S(2)}) collective-permute-start(f16[208,256]{1,0:T(8,128)(2,1)S(1)} %add_convert_fusion), channel_id=1, source_target_pairs={{0,4},{4,8},{8,12},{12,0},{1,5},{5,9},{9,13},{13,1},{2,6},{6,10},{... | collective-permute-start | bytes 319496 | tf_op jit(solution)/shard_map/ppermute | solution.py:503
  45.2 0.0 collective-permute-done.8.halo_l
  45.2 0.0 collective-permute-done.9.halo_r
  45.2 6.1 %krylov.1 = (f32[3,1024,128]{2,1,0:T(8,128)}, f32[8,128]{1,0:T(8,128)}) custom-call(s32[1]{0:T(128)} %bitcast.14.meta, s32[64]{0:T(128)} %band.3, f32[320,1024]{1,0:T(8,128)} %bitcast.27, f32[1024,128]{1,0:T(8,128)} %z.1, s32[2,1024]{1,0:T(2,128)} %bitcast.34, f32[1032,128]{1,0:T(8,128)} %collective-permute-done.8.halo_l, ...), custom_call_target="tpu_custom_call" | custom-call | flops 1321205760 | bytes 1310720 | tf_op jit(solution)/shard_map/krylov/pallas_call | solution.py:380
  51.4 10.9 %psum.7.mom = f32[8,128]{1,0:T(8,128)} all-reduce(f32[8,128]{1,0:T(8,128)} %get-tuple-element.13), channel_id=1, replica_groups=mesh['grp'=2,'smp'=4,'snp'=2,'pair'=2] {'smp'}, use_global_device_ids=true, to_apply=%region_0.1 | all-reduce | flops 1024 | bytes 8192 | tf_op jit(solution)/shard_map/psum | solution.py:523
  62.3 2.3 %combine.1 = f32[1024,128]{1,0:T(8,128)} custom-call(f32[3,1024,128]{2,1,0:T(8,128)} %get-tuple-element.12.w, f32[8,128]{1,0:T(8,128)} %psum.7.mom), custom_call_target="tpu_custom_call" | custom-call | tf_op jit(solution)/shard_map/combine/pallas_call | solution.py:429
  64.6 0.0 collective-permute-done.7
  64.6 0.0 collective-permute-done.6
  64.6 0.0 collective-permute-done.5
  64.7 0.1 pad_maximum_fusion
  64.8 0.9 %bitcast_convert_fusion = (f32[208,256]{1,0:T(8,128)}, f32[208,256]{1,0:T(8,128)}, f32[208,256]{1,0:T(8,128)}, f32[208,256]{1,0:T(8,128)}) fusion(f16[4,208,256]{2,1,0:T(8,128)(2,1)S(1)} %pad_maximum_fusion, s32[]{:T(128)S(6)} %select_n.16, s32[]{:T(128)S(6)} %select_n.15, s32[]{:T(128)S(6)} %select_n.14, s32[]{:T(128)S(6)} %select_n.13), kind=kLoop, calls=%fused_computation.2 | loop fusion | flops 212992 | bytes 1277968 | tf_op jit(solution)/shard_map/convert_element_type | solution.py:513
  65.7 2.7 %assemble.1 = f32[320,1024]{1,0:T(8,128)} custom-call(s32[2]{0:T(128)} %pad_add_fusion.meta, s32[64]{0:T(128)} %band.2, f32[208,256]{1,0:T(8,128)} %get-tuple-element.25.rest_0_, f32[208,256]{1,0:T(8,128)} %get-tuple-element.24.rest_1_, f32[208,256]{1,0:T(8,128)} %get-tuple-element.23.rest_2_, f32[208,256]{1,0:T(8,128)} %get-tuple-element.22.rest_3_), custom_call_target="tpu_custom_call" | custom-call | tf_op jit(solution)/shard_map/assemble/pallas_call | solution.py:222
  (5 shorter events, 0.1 us)
Async XLA Ops:
  0.6 6.0 %copy-start.2 = (s32[1024,2]{0,1:T(2,128)S(1)}, s32[1024,2]{0,1:T(2,128)}, u32[]{:S(2)}) copy-start(s32[1024,2]{0,1:T(2,128)} %param.15) | copy-start | bytes 24580
  0.6 6.0 %copy-start.1 = (f32[1024,128]{1,0:T(8,128)S(1)}, f32[1024,128]{1,0:T(8,128)}, u32[]{:S(2)}) copy-start(f32[1024,128]{1,0:T(8,128)} %z.1) | copy-start | bytes 1572868
  0.7 6.0 %copy-start = (f32[1024,320]{0,1:T(8,128)S(1)}, f32[1024,320]{0,1:T(8,128)}, u32[]{:S(2)}) copy-start(f32[1024,320]{0,1:T(8,128)} %param.12) | copy-start | bytes 3932164
  2.1 11.9 %collective-permute-start.1 = (bf16[2048,128]{1,0:T(8,128)(2,1)S(1)}, bf16[2048,128]{1,0:T(8,128)(2,1)}, u32[]{:S(2)}, u32[]{:S(2)}) collective-permute-start(bf16[2048,128]{1,0:T(8,128)(2,1)S(1)} %get-tuple-element.14), channel_id=1, source_target_pairs={{0,1},{1,2},{2,3},{4,5},{5,6},{6,7},{8,9},{9,10},{10,11},{12,13},{... | collective-permute-start | bytes 1572872 | tf_op jit(solution)/shard_map/ppermute | solution.py:496
  5.3 8.7 %collective-permute-start = (bf16[2048,128]{1,0:T(8,128)(2,1)S(1)}, bf16[2048,128]{1,0:T(8,128)(2,1)}, u32[]{:S(2)}, u32[]{:S(2)}) collective-permute-start(bf16[2048,128]{1,0:T(8,128)(2,1)S(1)} %get-tuple-element.15), channel_id=1, source_target_pairs={{1,0},{2,1},{3,2},{5,4},{6,5},{7,6},{9,8},{10,9},{11,10},{13,12},{... | collective-permute-start | bytes 1572872 | tf_op jit(solution)/shard_map/ppermute | solution.py:495
  6.8 38.4 %collective-permute-start.8 = (f32[1032,128]{1,0:T(8,128)S(1)}, f32[1032,128]{1,0:T(8,128)}, u32[]{:S(2)}, u32[]{:S(2)}) collective-permute-start(f32[1032,128]{1,0:T(8,128)S(1)} %concatenate.6), channel_id=1, source_target_pairs={{0,4},{4,8},{8,12},{1,5},{5,9},{9,13},{2,6},{6,10},{10,14},{3,7},{... | collective-permute-start | bytes 1585160 | tf_op jit(solution)/shard_map/ppermute | solution.py:456
  12.0 33.3 %collective-permute-start.9 = (f32[1032,128]{1,0:T(8,128)S(1)}, f32[1032,128]{1,0:T(8,128)}, u32[]{:S(2)}, u32[]{:S(2)}) collective-permute-start(f32[1032,128]{1,0:T(8,128)S(1)} %concatenate.7), channel_id=1, source_target_pairs={{4,0},{8,4},{12,8},{5,1},{9,5},{13,9},{6,2},{10,6},{14,10},{7,3},{... | collective-permute-start | bytes 1585160 | tf_op jit(solution)/shard_map/ppermute | solution.py:456
  25.5 7.1 %collective-permute-start.4 = (f16[208,256]{1,0:T(8,128)(2,1)S(1)}, f16[208,256]{1,0:T(8,128)(2,1)S(1)}, u32[]{:S(2)}, u32[]{:S(2)}) collective-permute-start(f16[208,256]{1,0:T(8,128)(2,1)S(1)} %convert_element_type.51), channel_id=1, source_target_pairs={{0,12},{4,0},{8,4},{12,8},{1,13},{5,1},{9,5},{13,9},{2,14},{6,2},{... | collective-permute-start | bytes 319496 | tf_op jit(solution)/shard_map/ppermute | solution.py:503
  30.3 10.2 %collective-permute-start.3 = (f16[208,256]{1,0:T(8,128)(2,1)S(1)}, f16[208,256]{1,0:T(8,128)(2,1)S(1)}, u32[]{:S(2)}, u32[]{:S(2)}) collective-permute-start(f16[208,256]{1,0:T(8,128)(2,1)S(1)} %convert_element_type.49), channel_id=1, source_target_pairs={{0,8},{4,12},{8,0},{12,4},{1,9},{5,13},{9,1},{13,5},{2,10},{6,14},... | collective-permute-start | bytes 319496 | tf_op jit(solution)/shard_map/ppermute | solution.py:503
  30.3 10.2 %collective-permute-start.2 = (f16[208,256]{1,0:T(8,128)(2,1)S(1)}, f16[208,256]{1,0:T(8,128)(2,1)S(1)}, u32[]{:S(2)}, u32[]{:S(2)}) collective-permute-start(f16[208,256]{1,0:T(8,128)(2,1)S(1)} %convert_element_type.47), channel_id=1, source_target_pairs={{0,4},{4,8},{8,12},{12,0},{1,5},{5,9},{9,13},{13,1},{2,6},{6,10},{... | collective-permute-start | bytes 319496 | tf_op jit(solution)/shard_map/ppermute | solution.py:503
  41.4 23.2 %collective-permute-start.7 = (f16[208,256]{1,0:T(8,128)(2,1)S(1)}, f16[208,256]{1,0:T(8,128)(2,1)S(1)}, u32[]{:S(2)}, u32[]{:S(2)}) collective-permute-start(f16[208,256]{1,0:T(8,128)(2,1)S(1)} %add_convert_fusion), channel_id=1, source_target_pairs={{0,12},{4,0},{8,4},{12,8},{1,13},{5,1},{9,5},{13,9},{2,14},{6,2},{... | collective-permute-start | bytes 319496 | tf_op jit(solution)/shard_map/ppermute | solution.py:503
  41.5 23.1 %collective-permute-start.6 = (f16[208,256]{1,0:T(8,128)(2,1)S(1)}, f16[208,256]{1,0:T(8,128)(2,1)S(1)}, u32[]{:S(2)}, u32[]{:S(2)}) collective-permute-start(f16[208,256]{1,0:T(8,128)(2,1)S(1)} %add_convert_fusion), channel_id=1, source_target_pairs={{0,8},{4,12},{8,0},{12,4},{1,9},{5,13},{9,1},{13,5},{2,10},{6,14},... | collective-permute-start | bytes 319496 | tf_op jit(solution)/shard_map/ppermute | solution.py:503
  43.3 21.4 %collective-permute-start.5 = (f16[208,256]{1,0:T(8,128)(2,1)S(1)}, f16[208,256]{1,0:T(8,128)(2,1)S(1)}, u32[]{:S(2)}, u32[]{:S(2)}) collective-permute-start(f16[208,256]{1,0:T(8,128)(2,1)S(1)} %add_convert_fusion), channel_id=1, source_target_pairs={{0,4},{4,8},{8,12},{12,0},{1,5},{5,9},{9,13},{13,1},{2,6},{6,10},{... | collective-permute-start | bytes 319496 | tf_op jit(solution)/shard_map/ppermute | solution.py:503

commit v2 on v1

--- a/solution.py
+++ b/solution.py
@@ -18,7 +18,7 @@
 HZ = ITERS * REACH
 HB = (ITERS - 1) * REACH
 TINY = 1e-6
-VMEM_LIMIT = 60 * 1024 * 1024
+VMEM_LIMIT = 28 * 1024 * 1024
 VMEM = pl.BlockSpec(memory_space=pltpu.VMEM)
 SMEM = pl.BlockSpec(memory_space=pltpu.SMEM)
 
@@ -401,7 +401,11 @@
     )(meta, band_prev, ldt, z, obs, halo_l, halo_r)
 
 
-def combine_kernel(w, mom, out):
+def combine_kernel(w, *rest):
+    out = rest[-1]
+    mom = rest[0][...]
+    for other in rest[1:-1]:
+        mom = mom + other[...]
     m = [mom[i : i + 1, :] for i in range(2 * ITERS)]
     shift = 1.0 + RIDGE
     h = [shift * m[i] + m[i + 1] for i in range(2 * ITERS - 1)]
@@ -425,15 +429,15 @@
     out[...] = c0 * w[0] + c1 * w[1] + c2 * w[2]
 
 
-def combine(w, mom):
+def combine(w, moments):
     return pl.pallas_call(
         combine_kernel,
-        in_specs=[VMEM, VMEM],
+        in_specs=[VMEM] * (1 + len(moments)),
         out_specs=VMEM,
         out_shape=jax.ShapeDtypeStruct(w.shape[1:], jnp.float32),
         compiler_params=params(),
         name="combine",
-    )(w, mom)
+    )(w, *moments)
 
 
 def packed(z, ldt, obs):
@@ -495,6 +499,8 @@
     right = lax.ppermute(dosage[:, :LANE], line, [(i + 1, i) for i in range(count - 1)])
     left = lax.ppermute(dosage[:, cols - LANE :], line, [(i, i + 1) for i in range(count - 1)])
 
+    w, mom = krylov(ldt, zscores, obs, halo_l, halo_r, band_prev, k * (rows // TILE))
+
     parts = cols // QW
     rot = parts == n_smp
     inv = 1.0 / (samples * n_smp)
@@ -503,9 +509,12 @@
         cycle = lambda value, by: lax.ppermute(
             value, "smp", [(i, (i + by) % n_smp) for i in range(n_smp)]
         )
+        moments = [mom] + [cycle(mom, by) for by in range(1, n_smp)]
+        got = [cycle(blocks[by].astype(jnp.float16), by) for by in range(1, n_smp)]
+        got, moments = lax.optimization_barrier((got, moments))
         total = blocks[0]
-        for by in range(1, n_smp):
-            total = total + cycle(blocks[by].astype(jnp.float16), by).astype(jnp.float32)
+        for g in got:
+            total = total + g.astype(jnp.float32)
         total = total.astype(jnp.float16)
         ring = [total] + [cycle(total, by) for by in range(1, n_smp)]
         stacked = jnp.stack(ring)
@@ -517,10 +526,9 @@
         ]
     else:
         pieces = lax.psum(tuple(blocks), "smp")
+        moments = [lax.psum(mom, "smp")]
+    imputed = combine(w, moments)
     ldn = assemble(pieces, band_next, place * (cols // TILE), cols)
-
-    w, mom = krylov(ldt, zscores, obs, halo_l, halo_r, band_prev, k * (rows // TILE))
-    imputed = combine(w, lax.psum(mom, "smp"))
     return ldn.T, imputed
 
 

time: 68.9 us -> 66.4 us (0.964)
  local copies, waits for them, and re-layouts: 1.64 us -> 13.5 us
  blocking collectives: 10.9 us -> 0 us
  Pallas kernels: 19.8 us -> 14.2 us
  waiting for transfers between devices: 8.99 us -> 12.5 us
  other arithmetic: 6.14 us -> 3.49 us
  starting transfers between devices: 20.1 us -> 21.5 us
    psum x1 -> x0, blocking collectives: 10.9 us -> none  [local(): imputed = combine(w, lax.psum(mom, 'smp'))]
    concatenate x2, local copies, waits for them, and re-layouts: 0.12 us -> 8.07 us  [packed(): return jnp.concatenate(parts, axis=0)]
    ppermute x6 -> x9, waiting for transfers between devices: 8.98 us -> 12.5 us  [local(): lax.ppermute(value, 'smp', [(i, (i + by) % n_smp) for i in range(n_smp)])]
    unnamed x6 -> x18, local copies, waits for them, and re-layouts: 0.02 us -> 2.22 us
    pallas_call x1, Pallas kernels: 8.68 us -> 6.69 us  [gram_parts(): pl.pallas_call(functools.partial(gram_kernel, parts, rot, inv), grid_spec...]
    pallas_call x1, Pallas kernels: 6.15 us -> 4.58 us  [krylov(): pl.pallas_call(functools.partial(krylov_kernel, band_prev.shape[0], sb),...]
    pallas_call x1, Pallas kernels: 2.32 us -> 0.93 us  [combine(): pl.pallas_call(combine_kernel, in_specs=[VMEM] * (1 + len(moments)), out_...]
    slice x1, local copies, waits for them, and re-layouts: 1.42 us -> 2.39 us  [local(): dosage[:, cols - LANE:]]
  transfers between devices with their start and end apart: 10 -> 13, of which waited for: 2 -> 5; matrix products, arithmetic and copies ran while one was open for 8% -> 17% of each run, Pallas kernels for 25% -> 18%
where the time goes in v2:
time: 66.4 us; the launch traced here: 66 us
  starting transfers between devices  21.5 us (32%)
  Pallas kernels  14.2 us (21%)
  local copies, waits for them, and re-layouts  13.5 us (20%)
  waiting for transfers between devices  12.5 us (19%)
  other arithmetic  3.49 us (5%)
  between operations  0.84 us (1%)
    ppermute x9, waiting for transfers between devices, local(): lax.ppermute(value, 'smp', [(i, (i + by) % n_smp) for i in range(n_smp)])  12.5 us
    ppermute x9, starting transfers between devices, local(): lax.ppermute(value, 'smp', [(i, (i + by) % n_smp) for i in range(n_smp)])  10.1 us
    concatenate x2, local copies, waits for them, and re-layouts, packed(): return jnp.concatenate(parts, axis=0)  8.07 us
    ppermute x2, starting transfers between devices, shifted(): return lax.ppermute(value, axis, pairs)  7.04 us
    pallas_call x1, Pallas kernels, gram_parts(): pl.pallas_call(functools.partial(gram_kernel, parts, rot, inv), grid_spec...  6.69 us
    pallas_call x1, Pallas kernels, krylov(): pl.pallas_call(functools.partial(krylov_kernel, band_prev.shape[0], sb),...  4.58 us
    ppermute x1, starting transfers between devices, local(): lax.ppermute(dosage[:, cols - LANE:], line, [(i, i + 1) for i in range(co...  3.06 us
    slice x1, local copies, waits for them, and re-layouts, local(): dosage[:, cols - LANE:]  2.39 us
  transfers between devices with their start and end apart: 13, of which 5 were waited for; matrix products, arithmetic and copies ran while one was open for 17% of the time, Pallas kernels for 18%

profile of v2, /device:TPU:0, one launch (start us, length us, event | category | flops | bytes accessed | tf_op | source)
XLA Modules:
  0.0 66.0 jit_solution(3615963451765692022)
XLA Ops:
  0.7 2.4 %fusion = (bf16[2048,128]{1,0:T(8,128)(2,1)}, bf16[2048,128]{1,0:T(8,128)(2,1)}) fusion(bf16[2048,1024]{1,0:T(8,128)(2,1)} %first.1), kind=kLoop, calls=%fused_computation.10 | loop fusion | bytes 2097152 | tf_op jit(solution)/shard_map/slice | solution.py:500
  3.0 1.3 %collective-permute-start = (bf16[2048,128]{1,0:T(8,128)(2,1)}, bf16[2048,128]{1,0:T(8,128)(2,1)S(1)}, u32[]{:S(2)}, u32[]{:S(2)}) collective-permute-start(bf16[2048,128]{1,0:T(8,128)(2,1)} %get-tuple-element.29), channel_id=1, source_target_pairs={{1,0},{2,1},{3,2},{5,4},{6,5},{7,6},{9,8},{10,9},{11,10},{13,12},{... | collective-permute-start | bytes 1572872 | tf_op jit(solution)/shard_map/ppermute | solution.py:499
  4.3 3.1 %collective-permute-start.1 = (bf16[2048,128]{1,0:T(8,128)(2,1)}, bf16[2048,128]{1,0:T(8,128)(2,1)S(1)}, u32[]{:S(2)}, u32[]{:S(2)}) collective-permute-start(bf16[2048,128]{1,0:T(8,128)(2,1)} %get-tuple-element.28), channel_id=1, source_target_pairs={{0,1},{1,2},{2,3},{4,5},{5,6},{6,7},{8,9},{9,10},{10,11},{12,13},{... | collective-permute-start | bytes 1572872 | tf_op jit(solution)/shard_map/ppermute | solution.py:500
  7.4 0.0 copy-done.6
  7.4 0.0 copy-done.1
  7.4 0.8 %fusion.1 = (f32[320,128]{1,0:T(8,128)S(1)}, f32[320,128]{1,0:T(8,128)}, f32[320,128]{1,0:T(8,128)}, f32[320,128]{1,0:T(8,128)}) fusion(f32[320,1024]{1,0:T(8,128)S(1)} %bitcast.25), kind=kLoop, calls=%fused_computation.11 | loop fusion | bytes 1310720 | tf_op jit(solution)/shard_map/slice | solution.py:447
  8.3 4.5 %concatenate.6 = f32[1032,128]{1,0:T(8,128)} concatenate(f32[384,128]{1,0:T(8,128)S(1)} %get-tuple-element.35, f32[320,128]{1,0:T(8,128)} %get-tuple-element.33, f32[320,128]{1,0:T(8,128)} %get-tuple-element.32, f32[2,128]{1,0:T(2,128)S(1)} %get-tuple-element.48, f32[2,128]{1,0:T(2,128)S(1)} %get-tuple-element.49, f32[2,128]{1,0:T(2,128)S(1)} %get-tuple-element.50, ...), dimensions={0} | concatenate | bytes 1056768 | tf_op jit(solution)/shard_map/concatenate | solution.py:451
  12.8 5.8 %collective-permute-start.5 = (f32[1032,128]{1,0:T(8,128)}, f32[1032,128]{1,0:T(8,128)}, u32[]{:S(2)}, u32[]{:S(2)}) collective-permute-start(f32[1032,128]{1,0:T(8,128)} %concatenate.6), channel_id=1, source_target_pairs={{0,4},{4,8},{8,12},{1,5},{5,9},{9,13},{2,6},{6,10},{10,14},{3,7},{... | collective-permute-start | bytes 1585160 | tf_op jit(solution)/shard_map/ppermute | solution.py:460
  18.6 3.6 %concatenate.7 = f32[1032,128]{1,0:T(8,128)} concatenate(f32[384,128]{1,0:T(8,128)S(1)} %get-tuple-element.34, f32[320,128]{1,0:T(8,128)} %get-tuple-element.31, f32[320,128]{1,0:T(8,128)S(1)} %get-tuple-element.30, f32[2,128]{1,0:T(2,128)S(1)} %get-tuple-element.44, f32[2,128]{1,0:T(2,128)S(1)} %get-tuple-element.43, f32[2,128]{1,0:T(2,128)S(1)} %get-tuple-element.42, ...), dimensions={0} | concatenate | bytes 1056768 | tf_op jit(solution)/shard_map/concatenate | solution.py:451
  22.2 1.3 %collective-permute-start.6 = (f32[1032,128]{1,0:T(8,128)}, f32[1032,128]{1,0:T(8,128)}, u32[]{:S(2)}, u32[]{:S(2)}) collective-permute-start(f32[1032,128]{1,0:T(8,128)} %concatenate.7), channel_id=1, source_target_pairs={{4,0},{8,4},{12,8},{5,1},{9,5},{13,9},{6,2},{10,6},{14,10},{7,3},{... | collective-permute-start | bytes 1585160 | tf_op jit(solution)/shard_map/ppermute | solution.py:460
  23.5 0.1 pad_add_fusion.1.meta
  23.5 0.0 collective-permute-done.right
  23.5 0.0 collective-permute-done.1.left
  23.6 0.0 copy-start
  23.6 2.2 %copy-done = bf16[2048,1024]{1,0:T(8,128)(2,1)S(1)} copy-done((bf16[2048,1024]{1,0:T(8,128)(2,1)S(1)}, bf16[2048,1024]{1,0:T(8,128)(2,1)}, u32[]{:S(2)}) %copy-start) | copy-done | bytes 4194328
  25.7 6.7 %gram.1 = (f32[208,256]{1,0:T(8,128)S(1)}, f32[208,256]{1,0:T(8,128)S(1)}, f32[208,256]{1,0:T(8,128)S(1)}, f32[208,256]{1,0:T(8,128)S(1)}) custom-call(s32[2]{0:T(128)S(1)} %pad_add_fusion.1.meta, bf16[2048,1024]{1,0:T(8,128)(2,1)S(1)} %copy-done, bf16[2048,1024]{1,0:T(8,128)(2,1)S(1)} %copy-done, bf16[2048,128]{1,0:T(8,128)(2,1)S(1)} %collective-permute-done.right, ...), custom_call_target="tpu_custom_call" | custom-call | flops 1610612736 | bytes 8388608 | tf_op jit(solution)/shard_map/gram/pallas_call | solution.py:158
  32.5 0.0 copy-start.3
  32.5 0.7 %convert_element_type.47 = f16[208,256]{1,0:T(8,128)(2,1)} convert(f32[208,256]{1,0:T(8,128)S(1)} %get-tuple-element.16) | non-fusion elementwise | flops 53248 | bytes 319488 | tf_op jit(solution)/shard_map/convert_element_type | solution.py:513
  33.2 2.6 %collective-permute-start.2 = (f16[208,256]{1,0:T(8,128)(2,1)}, f16[208,256]{1,0:T(8,128)(2,1)S(1)}, u32[]{:S(2)}, u32[]{:S(2)}) collective-permute-start(f16[208,256]{1,0:T(8,128)(2,1)} %convert_element_type.47), channel_id=1, source_target_pairs={{0,4},{4,8},{8,12},{12,0},{1,5},{5,9},{9,13},{13,1},{2,6},{6,10},{... | collective-permute-start | bytes 319496 | tf_op jit(solution)/shard_map/ppermute | solution.py:509
  35.8 0.7 convert_element_type.48
  36.5 2.6 %collective-permute-start.3 = (f16[208,256]{1,0:T(8,128)(2,1)}, f16[208,256]{1,0:T(8,128)(2,1)}, u32[]{:S(2)}, u32[]{:S(2)}) collective-permute-start(f16[208,256]{1,0:T(8,128)(2,1)} %convert_element_type.48), channel_id=1, source_target_pairs={{0,8},{4,12},{8,0},{12,4},{1,9},{5,13},{9,1},{13,5},{2,10},{6,14},... | collective-permute-start | bytes 319496 | tf_op jit(solution)/shard_map/ppermute | solution.py:509
  39.1 0.6 convert_element_type.49
  39.7 0.5 collective-permute-start.4
  40.3 0.0 collective-permute-done.5.halo_l
  40.3 0.0 collective-permute-done.6.halo_r
  40.3 4.6 %krylov.1 = (f32[3,1024,128]{2,1,0:T(8,128)S(1)}, f32[8,128]{1,0:T(8,128)S(1)}) custom-call(s32[1]{0:T(128)} %bitcast.5.meta, s32[64]{0:T(128)S(1)} %copy-done.8, f32[320,1024]{1,0:T(8,128)S(1)} %bitcast.26, f32[1024,128]{1,0:T(8,128)S(1)} %copy-done.2, s32[2,1024]{1,0:T(2,128)S(1)} %bitcast.30, f32[1032,128]{1,0:T(8,128)} %collective-permute-done.5.halo_l, ...), custom_call_target="tpu_custom_call" | custom-call | flops 1321205760 | bytes 1310720 | tf_op jit(solution)/shard_map/krylov/pallas_call | solution.py:380
  44.9 1.5 %collective-permute-start.7 = (f32[8,128]{1,0:T(8,128)S(1)}, f32[8,128]{1,0:T(8,128)S(1)}, u32[]{:S(2)}, u32[]{:S(2)}) collective-permute-start(f32[8,128]{1,0:T(8,128)S(1)} %get-tuple-element.24.rest_0_), channel_id=1, source_target_pairs={{0,4},{4,8},{8,12},{12,0},{1,5},{5,9},{9,13},{13,1},{2,6},{6,10},{... | collective-permute-start | bytes 12296 | tf_op jit(solution)/shard_map/ppermute | solution.py:509
  46.4 0.3 collective-permute-start.8
  46.7 3.6 %collective-permute-done.7.rest_1_ = f32[8,128]{1,0:T(8,128)S(1)} collective-permute-done((f32[8,128]{1,0:T(8,128)S(1)}, f32[8,128]{1,0:T(8,128)S(1)}, u32[]{:S(2)}, u32[]{:S(2)}) %collective-permute-start.7) | collective-permute-done | bytes 4128 | tf_op jit(solution)/shard_map/ppermute | solution.py:509
  50.3 0.0 collective-permute-start.9
  50.3 0.6 collective-permute-done.8.rest_2_
  50.9 3.0 %collective-permute-done.9.rest_3_ = f32[8,128]{1,0:T(8,128)S(1)} collective-permute-done((f32[8,128]{1,0:T(8,128)S(1)}, f32[8,128]{1,0:T(8,128)S(1)}, u32[]{:S(2)}, u32[]{:S(2)}) %collective-permute-start.9) | collective-permute-done | bytes 4128 | tf_op jit(solution)/shard_map/ppermute | solution.py:509
  53.9 0.0 collective-permute-done.2
  53.9 0.0 collective-permute-done.3
  53.9 0.0 collective-permute-done.4
  53.9 1.1 %add_convert_fusion = f16[208,256]{1,0:T(8,128)(2,1)S(1)} fusion(f16[208,256]{1,0:T(8,128)(2,1)} %collective-permute-done.4, f16[208,256]{1,0:T(8,128)(2,1)} %collective-permute-done.3, f32[208,256]{1,0:T(8,128)} %copy-done.3, f16[208,256]{1,0:T(8,128)(2,1)S(1)} %collective-permute-done.2), kind=kLoop, calls=%fused_computation.1 | loop fusion | flops 372736 | bytes 638976 | tf_op jit(solution)/shard_map/convert_element_type | solution.py:518
  55.1 0.1 collective-permute-start.11
  55.1 2.1 %collective-permute-start.12 = (f16[208,256]{1,0:T(8,128)(2,1)S(1)}, f16[208,256]{1,0:T(8,128)(2,1)S(1)}, u32[]{:S(2)}, u32[]{:S(2)}) collective-permute-start(f16[208,256]{1,0:T(8,128)(2,1)S(1)} %add_convert_fusion), channel_id=1, source_target_pairs={{0,12},{4,0},{8,4},{12,8},{1,13},{5,1},{9,5},{13,9},{2,14},{6,2},{... | collective-permute-start | bytes 319496 | tf_op jit(solution)/shard_map/ppermute | solution.py:509
  57.2 0.3 collective-permute-start.10
  57.5 0.1 pad_add_fusion.meta
  57.6 0.9 %combine.1 = f32[1024,128]{1,0:T(8,128)} custom-call(f32[3,1024,128]{2,1,0:T(8,128)S(1)} %get-tuple-element.23.w, f32[8,128]{1,0:T(8,128)S(1)} %get-tuple-element.24.rest_0_, f32[8,128]{1,0:T(8,128)S(1)} %collective-permute-done.7.rest_1_, f32[8,128]{1,0:T(8,128)S(1)} %collective-permute-done.8.rest_2_, f32[8,128]{1,0:T(8,128)S(1)} %collective-permute-done.9.rest_3_), custom_call_target="tpu_custom_call" | custom-call | tf_op jit(solution)/shard_map/combine/pallas_call | solution.py:433
  58.5 4.0 %collective-permute-done.11 = f16[208,256]{1,0:T(8,128)(2,1)S(1)} collective-permute-done((f16[208,256]{1,0:T(8,128)(2,1)S(1)}, f16[208,256]{1,0:T(8,128)(2,1)S(1)}, u32[]{:S(2)}, u32[]{:S(2)}) %collective-permute-start.11) | collective-permute-done | bytes 106528 | tf_op jit(solution)/shard_map/ppermute | solution.py:509
  62.5 0.0 collective-permute-done.12
  62.5 1.4 %collective-permute-done.10 = f16[208,256]{1,0:T(8,128)(2,1)S(1)} collective-permute-done((f16[208,256]{1,0:T(8,128)(2,1)S(1)}, f16[208,256]{1,0:T(8,128)(2,1)S(1)}, u32[]{:S(2)}, u32[]{:S(2)}) %collective-permute-start.10) | collective-permute-done | bytes 106528 | tf_op jit(solution)/shard_map/ppermute | solution.py:509
  63.8 0.1 pad_maximum_fusion
  64.0 0.1 bitcast_convert_fusion
  64.1 0.0 copy-done.7
  64.1 2.0 %assemble.1 = f32[320,1024]{1,0:T(8,128)} custom-call(s32[2]{0:T(128)S(1)} %pad_add_fusion.meta, s32[64]{0:T(128)S(1)} %copy-done.7, f32[208,256]{1,0:T(8,128)S(1)} %get-tuple-element.39.rest_0_, f32[208,256]{1,0:T(8,128)S(1)} %get-tuple-element.38.rest_1_, f32[208,256]{1,0:T(8,128)S(1)} %get-tuple-element.37.rest_2_, f32[208,256]{1,0:T(8,128)S(1)} %get-tuple-element.36.rest_3_), custom_call_target="tpu_custom_call" | custom-call | tf_op jit(solution)/shard_map/assemble/pallas_call | solution.py:222
  (16 shorter events, 0.1 us)
Async XLA Ops:
  0.6 6.8 %copy-start.6 = (s32[1024,2]{0,1:T(2,128)S(1)}, s32[1024,2]{0,1:T(2,128)}, u32[]{:S(2)}) copy-start(s32[1024,2]{0,1:T(2,128)} %param.15) | copy-start | bytes 24580
  0.6 6.8 %copy-start.1 = (f32[1024,320]{0,1:T(8,128)S(1)}, f32[1024,320]{0,1:T(8,128)}, u32[]{:S(2)}) copy-start(f32[1024,320]{0,1:T(8,128)} %param.12) | copy-start | bytes 3932164
  0.7 7.6 %copy-start.2 = (f32[1024,128]{1,0:T(8,128)S(1)}, f32[1024,128]{1,0:T(8,128)}, u32[]{:S(2)}) copy-start(f32[1024,128]{1,0:T(8,128)} %z.1) | copy-start | bytes 1572868
  3.0 20.5 %collective-permute-start = (bf16[2048,128]{1,0:T(8,128)(2,1)}, bf16[2048,128]{1,0:T(8,128)(2,1)S(1)}, u32[]{:S(2)}, u32[]{:S(2)}) collective-permute-start(bf16[2048,128]{1,0:T(8,128)(2,1)} %get-tuple-element.29), channel_id=1, source_target_pairs={{1,0},{2,1},{3,2},{5,4},{6,5},{7,6},{9,8},{10,9},{11,10},{13,12},{... | collective-permute-start | bytes 1572872 | tf_op jit(solution)/shard_map/ppermute | solution.py:499
  4.3 19.2 %collective-permute-start.1 = (bf16[2048,128]{1,0:T(8,128)(2,1)}, bf16[2048,128]{1,0:T(8,128)(2,1)S(1)}, u32[]{:S(2)}, u32[]{:S(2)}) collective-permute-start(bf16[2048,128]{1,0:T(8,128)(2,1)} %get-tuple-element.28), channel_id=1, source_target_pairs={{0,1},{1,2},{2,3},{4,5},{5,6},{6,7},{8,9},{9,10},{10,11},{12,13},{... | collective-permute-start | bytes 1572872 | tf_op jit(solution)/shard_map/ppermute | solution.py:500
  8.3 15.3 %copy-start.4 = (f32[4096]{0:T(1024)S(1)}, f32[4096]{0:T(1024)}, u32[]{:S(2)}) copy-start(f32[4096]{0:T(1024)} %param.9) | copy-start | bytes 49156
  8.3 15.3 %copy-start.5 = (f32[4096]{0:T(1024)S(1)}, f32[4096]{0:T(1024)}, u32[]{:S(2)}) copy-start(f32[4096]{0:T(1024)} %param.10) | copy-start | bytes 49156
  12.8 27.4 %collective-permute-start.5 = (f32[1032,128]{1,0:T(8,128)}, f32[1032,128]{1,0:T(8,128)}, u32[]{:S(2)}, u32[]{:S(2)}) collective-permute-start(f32[1032,128]{1,0:T(8,128)} %concatenate.6), channel_id=1, source_target_pairs={{0,4},{4,8},{8,12},{1,5},{5,9},{9,13},{2,6},{6,10},{10,14},{3,7},{... | collective-permute-start | bytes 1585160 | tf_op jit(solution)/shard_map/ppermute | solution.py:460
  22.2 18.1 %collective-permute-start.6 = (f32[1032,128]{1,0:T(8,128)}, f32[1032,128]{1,0:T(8,128)}, u32[]{:S(2)}, u32[]{:S(2)}) collective-permute-start(f32[1032,128]{1,0:T(8,128)} %concatenate.7), channel_id=1, source_target_pairs={{4,0},{8,4},{12,8},{5,1},{9,5},{13,9},{6,2},{10,6},{14,10},{7,3},{... | collective-permute-start | bytes 1585160 | tf_op jit(solution)/shard_map/ppermute | solution.py:460
  23.6 2.2 %copy-start = (bf16[2048,1024]{1,0:T(8,128)(2,1)S(1)}, bf16[2048,1024]{1,0:T(8,128)(2,1)}, u32[]{:S(2)}) copy-start(bf16[2048,1024]{1,0:T(8,128)(2,1)} %first.1) | copy-start | bytes 12582916
  25.7 14.5 %copy-start.8 = (s32[64]{0:T(128)S(1)}, s32[64]{0:T(128)}, u32[]{:S(2)}) copy-start(s32[64]{0:T(128)} %band.2) | copy-start | bytes 772
  32.5 12.4 %copy-start.3 = (f32[208,256]{1,0:T(8,128)}, f32[208,256]{1,0:T(8,128)S(1)}, u32[]{:S(2)}) copy-start(f32[208,256]{1,0:T(8,128)S(1)} %get-tuple-element.15) | copy-start | bytes 638980
  33.2 20.8 %collective-permute-start.2 = (f16[208,256]{1,0:T(8,128)(2,1)}, f16[208,256]{1,0:T(8,128)(2,1)S(1)}, u32[]{:S(2)}, u32[]{:S(2)}) collective-permute-start(f16[208,256]{1,0:T(8,128)(2,1)} %convert_element_type.47), channel_id=1, source_target_pairs={{0,4},{4,8},{8,12},{12,0},{1,5},{5,9},{9,13},{13,1},{2,6},{6,10},{... | collective-permute-start | bytes 319496 | tf_op jit(solution)/shard_map/ppermute | solution.py:509
  36.5 17.5 %collective-permute-start.3 = (f16[208,256]{1,0:T(8,128)(2,1)}, f16[208,256]{1,0:T(8,128)(2,1)}, u32[]{:S(2)}, u32[]{:S(2)}) collective-permute-start(f16[208,256]{1,0:T(8,128)(2,1)} %convert_element_type.48), channel_id=1, source_target_pairs={{0,8},{4,12},{8,0},{12,4},{1,9},{5,13},{9,1},{13,5},{2,10},{6,14},... | collective-permute-start | bytes 319496 | tf_op jit(solution)/shard_map/ppermute | solution.py:509
  39.7 14.2 %collective-permute-start.4 = (f16[208,256]{1,0:T(8,128)(2,1)}, f16[208,256]{1,0:T(8,128)(2,1)}, u32[]{:S(2)}, u32[]{:S(2)}) collective-permute-start(f16[208,256]{1,0:T(8,128)(2,1)} %convert_element_type.49), channel_id=1, source_target_pairs={{0,12},{4,0},{8,4},{12,8},{1,13},{5,1},{9,5},{13,9},{2,14},{6,2},{... | collective-permute-start | bytes 319496 | tf_op jit(solution)/shard_map/ppermute | solution.py:509
  44.9 5.5 %collective-permute-start.7 = (f32[8,128]{1,0:T(8,128)S(1)}, f32[8,128]{1,0:T(8,128)S(1)}, u32[]{:S(2)}, u32[]{:S(2)}) collective-permute-start(f32[8,128]{1,0:T(8,128)S(1)} %get-tuple-element.24.rest_0_), channel_id=1, source_target_pairs={{0,4},{4,8},{8,12},{12,0},{1,5},{5,9},{9,13},{13,1},{2,6},{6,10},{... | collective-permute-start | bytes 12296 | tf_op jit(solution)/shard_map/ppermute | solution.py:509
  46.4 4.5 %collective-permute-start.8 = (f32[8,128]{1,0:T(8,128)S(1)}, f32[8,128]{1,0:T(8,128)S(1)}, u32[]{:S(2)}, u32[]{:S(2)}) collective-permute-start(f32[8,128]{1,0:T(8,128)S(1)} %get-tuple-element.24.rest_0_), channel_id=1, source_target_pairs={{0,8},{4,12},{8,0},{12,4},{1,9},{5,13},{9,1},{13,5},{2,10},{6,14},... | collective-permute-start | bytes 12296 | tf_op jit(solution)/shard_map/ppermute | solution.py:509
  50.3 3.6 %collective-permute-start.9 = (f32[8,128]{1,0:T(8,128)S(1)}, f32[8,128]{1,0:T(8,128)S(1)}, u32[]{:S(2)}, u32[]{:S(2)}) collective-permute-start(f32[8,128]{1,0:T(8,128)S(1)} %get-tuple-element.24.rest_0_), channel_id=1, source_target_pairs={{0,12},{4,0},{8,4},{12,8},{1,13},{5,1},{9,5},{13,9},{2,14},{6,2},{... | collective-permute-start | bytes 12296 | tf_op jit(solution)/shard_map/ppermute | solution.py:509
  55.1 7.4 %collective-permute-start.11 = (f16[208,256]{1,0:T(8,128)(2,1)S(1)}, f16[208,256]{1,0:T(8,128)(2,1)S(1)}, u32[]{:S(2)}, u32[]{:S(2)}) collective-permute-start(f16[208,256]{1,0:T(8,128)(2,1)S(1)} %add_convert_fusion), channel_id=1, source_target_pairs={{0,8},{4,12},{8,0},{12,4},{1,9},{5,13},{9,1},{13,5},{2,10},{6,14},... | collective-permute-start | bytes 319496 | tf_op jit(solution)/shard_map/ppermute | solution.py:509
  55.1 7.3 %collective-permute-start.12 = (f16[208,256]{1,0:T(8,128)(2,1)S(1)}, f16[208,256]{1,0:T(8,128)(2,1)S(1)}, u32[]{:S(2)}, u32[]{:S(2)}) collective-permute-start(f16[208,256]{1,0:T(8,128)(2,1)S(1)} %add_convert_fusion), channel_id=1, source_target_pairs={{0,12},{4,0},{8,4},{12,8},{1,13},{5,1},{9,5},{13,9},{2,14},{6,2},{... | collective-permute-start | bytes 319496 | tf_op jit(solution)/shard_map/ppermute | solution.py:509
  57.2 6.6 %collective-permute-start.10 = (f16[208,256]{1,0:T(8,128)(2,1)S(1)}, f16[208,256]{1,0:T(8,128)(2,1)S(1)}, u32[]{:S(2)}, u32[]{:S(2)}) collective-permute-start(f16[208,256]{1,0:T(8,128)(2,1)S(1)} %add_convert_fusion), channel_id=1, source_target_pairs={{0,4},{4,8},{8,12},{12,0},{1,5},{5,9},{9,13},{13,1},{2,6},{6,10},{... | collective-permute-start | bytes 319496 | tf_op jit(solution)/shard_map/ppermute | solution.py:509
  58.5 5.6 %copy-start.7 = (s32[64]{0:T(128)S(1)}, s32[64]{0:T(128)}, u32[]{:S(2)}) copy-start(s32[64]{0:T(128)} %band.3) | copy-start | bytes 772

commit v3 on v1

--- a/solution.py
+++ b/solution.py
@@ -18,13 +18,12 @@
 HZ = ITERS * REACH
 HB = (ITERS - 1) * REACH
 TINY = 1e-6
-VMEM_LIMIT = 60 * 1024 * 1024
 VMEM = pl.BlockSpec(memory_space=pltpu.VMEM)
 SMEM = pl.BlockSpec(memory_space=pltpu.SMEM)
 
 
-def params(**kw):
-    return pltpu.CompilerParams(vmem_limit_bytes=VMEM_LIMIT, **kw)
+def params(mib):
+    return pltpu.CompilerParams(vmem_limit_bytes=mib * 1024 * 1024)
 
 
 def mask_rows(band_ref, first_tile, total):
@@ -60,16 +59,149 @@
     )
 
 
-def gram_kernel(
-    parts, rot, inv, meta, own, ahead, right, left, first, mean, scale, *rest
-):
+LEVELS = 32000.0
+LARGEST = 36.0
+
+
+def encode(value):
+    size = jnp.minimum(jnp.abs(value) * (1.0 / LARGEST), 1.0) + 1e-30
+    for _ in range(3):
+        size = size * lax.rsqrt(size)
+    code = size * LEVELS + 0.5
+    return jnp.where(value < 0, -code, code).astype(jnp.int32).astype(jnp.int16)
+
+
+def decode(code):
+    value = code.astype(jnp.int32).astype(jnp.float32)
+    power = value * (1.0 / LEVELS)
+    square = power * power
+    fourth = square * square
+    eighth = fourth * fourth * LARGEST
+    return jnp.where(value < 0, -eighth, eighth)
+
+
+def encode_exact(value):
+    size = jnp.maximum(jnp.abs(value), 1e-30)
+    power = jnp.clip(jnp.floor(jnp.log2(size)), -100.0, 120.0)
+    scaled = value * jnp.exp2(-power) * 2.0**13
+    high = jnp.round(scaled)
+    low = jnp.round((scaled - high) * 2.0**14)
+    return power, high, low
+
+
+def decode_exact(power, high, low):
+    return (high * 2.0**-13 + low * 2.0**-27) * jnp.exp2(power)
+
+
+def to_code(value):
+    return value.astype(jnp.int32).astype(jnp.int16)
+
+
+def from_code(code):
+    return code.astype(jnp.int32).astype(jnp.float32)
+
+
+def line_index(axes):
+    place = lax.axis_index(axes[0])
+    for axis in axes[1:]:
+        place = place * lax.axis_size(axis) + lax.axis_index(axis)
+    return place
+
+
+def pack_kernel(dos, z, ldt, obs, dos_e, dos_o, *rest):
+    halo, sem = rest[:-1], rest[-1]
+    cols = dos.shape[1]
+    rows = z.shape[0]
+    copies = []
+
+    def start(source, target):
+        copy = pltpu.make_async_copy(source, target, sem.at[len(copies)])
+        copy.start()
+        copies.append(copy)
+
+    even = lax.rem(line_index(("snp", "pair")), 2) == 0
+    to_e = pl.multiple_of(jnp.where(even, cols - LANE, 0), LANE)
+    to_o = pl.multiple_of(jnp.where(even, 0, cols - LANE), LANE)
+    start(dos.at[:, pl.ds(to_e, LANE)], dos_e)
+    start(dos.at[:, pl.ds(to_o, LANE)], dos_o)
+    if halo:
+        even = lax.rem(lax.axis_index("smp"), 2) == 0
+        spots = []
+        for out, last in ((halo[0], even), (halo[1], jnp.logical_not(even))):
+            row = pl.multiple_of(jnp.where(last, rows - HZ, 0), LANE)
+            col = pl.multiple_of(jnp.where(last, rows - HB, 0), LANE)
+            spots.append(row)
+            start(z.at[pl.ds(row, HZ), :], out.at[0:HZ, :])
+            for i in range(HB // LANE):
+                start(
+                    ldt.at[:, pl.ds(pl.multiple_of(col + i * LANE, LANE), LANE)],
+                    out.at[HZ + i * SPAN * TILE : HZ + (i + 1) * SPAN * TILE, :],
+                )
+        nb = obs.shape[0]
+        base = HZ + HB // LANE * SPAN * TILE
+        for out, row in zip(halo, spots):
+            for i in range(HZ // LANE):
+                flags = obs[:, pl.ds(pl.multiple_of(row + i * LANE, LANE), LANE)]
+                out[base + i * nb : base + (i + 1) * nb, :] = flags.astype(jnp.float32)
+            used = base + HZ // LANE * nb
+            if used < out.shape[0]:
+                out[used:, :] = jnp.zeros((out.shape[0] - used, LANE), jnp.float32)
+    for copy in copies:
+        copy.wait()
+
+
+def pack(dosage, z, ldt, obs, with_halo):
+    samples = dosage.shape[0]
+    shapes = [jax.ShapeDtypeStruct((samples, LANE), dosage.dtype)] * 2
+    copies = 2
+    if with_halo:
+        height = HZ + HB // LANE * SPAN * TILE + HZ // LANE * obs.shape[0]
+        shapes += [jax.ShapeDtypeStruct((height + -height % 8, LANE), jnp.float32)] * 2
+        copies += 2 * (1 + HB // LANE)
+    far = pl.BlockSpec(memory_space=pltpu.HBM)
+    return pl.pallas_call(
+        pack_kernel,
+        in_specs=[far, far, far, VMEM],
+        out_specs=[VMEM] * len(shapes),
+        out_shape=shapes,
+        scratch_shapes=[pltpu.SemaphoreType.DMA((copies,))],
+        compiler_params=params(8),
+        name="pack",
+    )(dosage, z, ldt, obs)
+
+
+def exchange(value, axes, phase):
+    count = 1
+    for axis in axes:
+        count *= lax.axis_size(axis)
+    if phase == 0 and lax.axis_size(axes[-1]) == 2 and len(axes) > 1:
+        return lax.ppermute(value, axes[-1], [(0, 1), (1, 0)])
+    pairs = []
+    for i in range(phase, count - 1, 2):
+        pairs += [(i, i + 1), (i + 1, i)]
+    return lax.ppermute(value, axes, pairs)
+
+
+def gram_kernel(parts, rot, samples_total, dos, got_e, got_o, mean, scale, *rest):
     outs = rest[:parts]
-    normed, cross = rest[parts:]
-    g = pl.program_id(0)
-    quarter = lax.rem(g + meta[0], parts) if rot else g
+    raw, normed, cross, sem = rest[parts:]
     blocks = QW // LANE
-    base = meta[1]
+    samples, cols = dos.shape
+    place = line_index(("snp", "pair"))
+    base = place * (cols // LANE)
     lanes_total = mean.shape[0]
+    first = lax.axis_index("smp") if rot else 0
+    inv = 1.0 / (samples if rot else samples_total)
+
+    def quarter_of(g):
+        return lax.rem(g + first, parts)
+
+    def fetch(g):
+        at = pl.multiple_of(quarter_of(g) * QW, QW)
+        return pltpu.make_async_copy(dos.at[:, pl.ds(at, QW)], raw.at[g], sem.at[g])
+
+    for g in range(parts):
+        fetch(g).start()
 
     def standard(values, block):
         row = jnp.clip(block, 0, lanes_total - 1)
@@ -77,160 +209,200 @@
         s = scale[pl.ds(row, 1), :]
         return ((values.astype(jnp.float32) - m) * s).astype(jnp.bfloat16)
 
-    for b in range(blocks):
-        cols = slice(b * LANE, (b + 1) * LANE)
-        normed[:, cols] = standard(own[:, cols], base + quarter * blocks + b)
-    beyond = base + (quarter + 1) * blocks
-    tail = slice(QW, QW + LANE)
-
-    @pl.when(quarter == parts - 1)
-    def _():
-        normed[:, tail] = standard(right[...], beyond)
-
-    @pl.when(quarter != parts - 1)
-    def _():
-        normed[:, tail] = standard(ahead[...], beyond)
-
-    @pl.when(g == 0)
-    def _():
-        cross[...] = inv * tdot(standard(left[...], base - 1), standard(first[...], base))
-
-    full = tdot(normed[...], normed[:, :QW])
+    def settle(g):
+        fetch(g).wait()
+        block = quarter_of(g) * blocks
+        for b in range(blocks):
+            at = pl.multiple_of((block + b) * LANE, LANE)
+            normed[:, pl.ds(at, LANE)] = standard(
+                raw[g, :, b * LANE : (b + 1) * LANE], base + block + b
+            )
+
+    even = lax.rem(place, 2) == 0
+    got = [got_e[...], got_o[...]]
+    right = jnp.where(even, got[0], got[1])
+    left = jnp.where(even, got[1], got[0])
+    normed[:, cols:] = standard(right, base + cols // LANE)
+    raw_left = standard(left, base - 1)
+    settle(0)
     rows = (BMAX + 1) * TILE
     low = low_lanes((rows, LANE))
-    pieces = []
-    for b in range(blocks):
-        cols = slice(b * LANE, (b + 1) * LANE)
-        pieces.append(
-            inv
-            * jnp.where(
-                low,
-                full[b * LANE : b * LANE + rows, cols],
-                full[b * LANE + TILE : b * LANE + TILE + rows, cols],
+    share = LANE // parts // blocks
+
+    fetch0 = pltpu.make_async_copy(dos.at[:, 0:LANE], raw.at[parts, :, 0:LANE], sem.at[parts])
+    fetch0.start()
+    fetch0.wait()
+    cross[...] = inv * tdot(raw_left, standard(raw[parts, :, 0:LANE], base))
+
+    def step(g, _):
+        @pl.when(g < parts - 1)
+        def _():
+            settle(jnp.minimum(g + 1, parts - 1))
+
+        quarter = quarter_of(g)
+        at = pl.multiple_of(quarter * QW, QW)
+        full = tdot(normed[:, pl.ds(at, QW + LANE)], normed[:, pl.ds(at, QW)])
+        pieces = []
+        for b in range(blocks):
+            cut = slice(b * LANE, (b + 1) * LANE)
+            pieces.append(
+                inv
+                * jnp.where(
+                    low,
+                    full[b * LANE : b * LANE + rows, cut],
+                    full[b * LANE + TILE : b * LANE + TILE + rows, cut],
+                )
             )
-        )
-    share = LANE // parts // blocks
-    start = pl.multiple_of(quarter * (share * blocks), 8)
-    shares = [cross[pl.ds(pl.multiple_of(start + b * share, 8), share), :] for b in range(blocks)]
-    for i in range(parts):
-
-        @pl.when(g == i)
-        def _(i=i):
-            for b in range(blocks):
-                cols = slice(b * LANE, (b + 1) * LANE)
-                outs[i][0:rows, cols] = pieces[b]
-                outs[i][rows : rows + share, cols] = shares[b]
-
-
-def gram_parts(dosage, left, right, mean, scale, k, column_place, rot, inv):
+        start = quarter * (share * blocks)
+        shares = [
+            cross[pl.ds(pl.multiple_of(start + b * share, 8), share), :] for b in range(blocks)
+        ]
+        for i in range(parts):
+
+            @pl.when(g == i)
+            def _(i=i):
+                for b in range(blocks):
+                    cut = slice(b * LANE, (b + 1) * LANE)
+                    send = encode if rot and i > 0 else (lambda v: v)
+                    outs[i][0:rows, cut] = send(pieces[b])
+                    outs[i][rows : rows + share, cut] = send(shares[b])
+
+        return 0
+
+    lax.fori_loop(0, parts, step, 0)
+
+
+def gram_parts(dosage, got_e, got_o, mean, scale, rot, samples_total):
     samples, cols = dosage.shape
     parts = cols // QW
-    blocks = QW // LANE
-    total = cols // LANE
-    height = (BMAX + 1) * TILE + LANE // parts // blocks
-    meta = jnp.stack([k, column_place * total]).astype(jnp.int32)
-
-    def quarter(g, m):
-        return lax.rem(g + m[0], parts) if rot else g
-
-    fixed = lambda g, m: (0, 0)
-    grid_spec = pltpu.PrefetchScalarGridSpec(
-        num_scalar_prefetch=1,
-        grid=(parts,),
-        in_specs=[
-            pl.BlockSpec((samples, QW), lambda g, m: (0, quarter(g, m))),
-            pl.BlockSpec(
-                (samples, LANE),
-                lambda g, m: (0, jnp.minimum((quarter(g, m) + 1) * blocks, total - 1)),
-            ),
-            pl.BlockSpec((samples, LANE), fixed),
-            pl.BlockSpec((samples, LANE), fixed),
-            pl.BlockSpec((samples, LANE), fixed),
-            pl.BlockSpec((mean.shape[0] // LANE, LANE), fixed),
-            pl.BlockSpec((mean.shape[0] // LANE, LANE), fixed),
+    height = (BMAX + 1) * TILE + LANE // parts // (QW // LANE)
+    kinds = [jnp.float32] + [jnp.int16 if rot else jnp.float32] * (parts - 1)
+    return pl.pallas_call(
+        functools.partial(gram_kernel, parts, rot, samples_total),
+        in_specs=[pl.BlockSpec(memory_space=pltpu.HBM)] + [VMEM] * 4,
+        out_specs=[VMEM] * parts,
+        out_shape=[jax.ShapeDtypeStruct((height, QW), kind) for kind in kinds],
+        scratch_shapes=[
+            pltpu.VMEM((parts + 1, samples, QW), jnp.bfloat16),
+            pltpu.VMEM((samples, cols + LANE), jnp.bfloat16),
+            pltpu.VMEM((LANE, LANE), jnp.float32),
+            pltpu.SemaphoreType.DMA((parts + 1,)),
         ],
-        out_specs=[pl.BlockSpec((height, QW), fixed) for _ in range(parts)],
-        scratch_shapes=[
-            pltpu.VMEM((samples, QW + LANE), jnp.bfloat16),
-            pltpu.VMEM((LANE, LANE), jnp.float32),
-        ],
-    )
-    return pl.pallas_call(
-        functools.partial(gram_kernel, parts, rot, inv),
-        grid_spec=grid_spec,
-        out_shape=[jax.ShapeDtypeStruct((height, QW), jnp.float32) for _ in range(parts)],
-        compiler_params=params(dimension_semantics=("arbitrary",)),
+        compiler_params=params(24),
         cost_estimate=pl.CostEstimate(
             flops=2 * samples * cols * (QW + LANE), bytes_accessed=dosage.size * 4, transcendentals=0
         ),
         name="gram",
-    )(
-        meta,
-        dosage,
-        dosage,
-        right,
-        left,
-        dosage,
-        mean.reshape(-1, LANE),
-        scale.reshape(-1, LANE),
-    )
-
-
-def assemble_kernel(parts, rot, tile_total, meta, band, *rest):
-    ins = rest[:parts]
-    out = rest[parts]
+    )(dosage, got_e, got_o, mean.reshape(-1, LANE), scale.reshape(-1, LANE))
+
+
+def total_kernel(count, own, *rest):
+    others, mom, out = rest[:-2], rest[-2], rest[-1]
+    height = own.shape[0]
+    total = own[...]
+    for other in others:
+        total = total + decode(other[...])
+    out[0:height, :] = encode(total * (1.0 / count))
+    power, high, low = encode_exact(mom[...])
+    lanes = mom.shape[1]
+    top = jnp.concatenate([power, low], axis=1)
+    bottom = jnp.concatenate([high, jnp.zeros_like(low)], axis=1)
+    out[height : height + 16, :] = to_code(jnp.concatenate([top, bottom], axis=0))
+
+
+def total_of(own, others, mom):
+    count = 1 + len(others)
+    return pl.pallas_call(
+        functools.partial(total_kernel, count),
+        in_specs=[VMEM] * (count + 1),
+        out_specs=VMEM,
+        out_shape=jax.ShapeDtypeStruct((own.shape[0] + 16, own.shape[1]), jnp.int16),
+        compiler_params=params(8),
+        name="total",
+    )(own, *others, mom)
+
+
+def final_kernel(parts, rot, moments, tile_total, band, w, *rest):
+    ring = rest[:parts]
+    moms = rest[parts : parts + moments]
+    out, imputed, held = rest[parts + moments :]
     blocks = QW // LANE
     rows = (BMAX + 1) * TILE
     low = low_lanes((TILE, LANE))
     share = LANE // parts // blocks
-    for quarter in range(parts):
-
-        def fetch(row, count, b, quarter=quarter):
-            cols = slice(b * LANE, (b + 1) * LANE)
-            return ins[quarter][row : row + count, cols]
-
-        for b in range(blocks):
-            a = quarter * blocks + b
-            cols = slice(a * LANE, (a + 1) * LANE)
-            masks = mask_rows(band, meta[1] + 2 * a, tile_total)
-            for q in range(BMAX + 1):
-                out[(BMAX + q) * TILE : (BMAX + q + 1) * TILE, cols] = (
-                    fetch(q * TILE, TILE, b) * masks[BMAX + q]
-                )
-            turned = fetch(TILE, 2 * TILE, b).T
-            rolled = pltpu.roll(turned, TILE, axis=1)
-            if a == 0:
-                count = LANE // share
-                cross = [
-                    ins[j // blocks][
-                        rows : rows + share, (j % blocks) * LANE : (j % blocks + 1) * LANE
-                    ]
-                    for j in range(count)
-                ]
-                cross = jnp.concatenate(cross, axis=0)
-                one_low, two_low, two_high = cross[TILE:], cross[:TILE], cross[TILE:]
-            else:
-                one_low, two_low, two_high = last_turned[TILE:], last_rolled[:TILE], last_turned[TILE:]
-            out[TILE : 2 * TILE, cols] = jnp.where(low, one_low, rolled[:TILE]) * masks[1]
-            out[0:TILE, cols] = jnp.where(low, two_low, two_high) * masks[0]
-            last_turned, last_rolled = turned, rolled
-
-
-def assemble(pieces, band_next, first_tile, cols):
-    parts = len(pieces)
-    meta = jnp.stack([first_tile * 0, first_tile]).astype(jnp.int32)
+    height = rows + share
+    cols = out.shape[1]
+    first_tile = line_index(("snp", "pair")) * (cols // TILE)
+    if rot:
+        k = lax.axis_index("smp")
+        total = None
+        for by in range(parts):
+            held[lax.rem(k - by + parts, parts)] = decode(ring[by][0:height, :])
+            code = from_code(ring[by][height : height + 16, :])
+            lanes = code.shape[1] // 2
+            mom = decode_exact(code[:8, :lanes], code[8:, :lanes], code[:8, lanes:])
+            total = mom if total is None else total + mom
+    else:
+        for by in range(parts):
+            held[by] = ring[by][...]
+        total = moms[0][...]
+    solve(w, total, imputed)
+    for a in range(parts * blocks):
+        quarter, b = a // blocks, a % blocks
+        cut = slice(b * LANE, (b + 1) * LANE)
+        cols_here = slice(a * LANE, (a + 1) * LANE)
+        masks = mask_rows(band, first_tile + 2 * a, tile_total)
+        for q in range(BMAX + 1):
+            out[(BMAX + q) * TILE : (BMAX + q + 1) * TILE, cols_here] = (
+                held[quarter, q * TILE : (q + 1) * TILE, cut] * masks[BMAX + q]
+            )
+        turned = held[quarter, TILE : 3 * TILE, cut].T
+        rolled = pltpu.roll(turned, TILE, axis=1)
+        if a == 0:
+            cross = jnp.concatenate(
+                [
+                    held[j // blocks, rows:height, (j % blocks) * LANE : (j % blocks + 1) * LANE]
+                    for j in range(LANE // share)
+                ],
+                axis=0,
+            )
+            one_low, two_low, two_high = cross[TILE:], cross[:TILE], cross[TILE:]
+        else:
+            one_low, two_low, two_high = last_turned[TILE:], last_rolled[:TILE], last_turned[TILE:]
+        out[TILE : 2 * TILE, cols_here] = jnp.where(low, one_low, rolled[:TILE]) * masks[1]
+        out[0:TILE, cols_here] = jnp.where(low, two_low, two_high) * masks[0]
+        last_turned, last_rolled = turned, rolled
+
+
+def final(ring, moms, w, band_next, cols, rot):
+    parts = len(ring)
+    height = (BMAX + 1) * TILE + LANE // parts // (QW // LANE)
     return pl.pallas_call(
-        functools.partial(assemble_kernel, parts, False, band_next.shape[0]),
-        in_specs=[SMEM, SMEM] + [VMEM] * parts,
-        out_specs=VMEM,
-        out_shape=jax.ShapeDtypeStruct((SPAN * TILE, cols), jnp.float32),
-        compiler_params=params(),
-        name="assemble",
-    )(meta, band_next, *pieces)
+        functools.partial(final_kernel, parts, rot, len(moms), band_next.shape[0]),
+        in_specs=[SMEM] + [VMEM] * (1 + parts + len(moms)),
+        out_specs=[VMEM, VMEM],
+        out_shape=[
+            jax.ShapeDtypeStruct((SPAN * TILE, cols), jnp.float32),
+            jax.ShapeDtypeStruct(w.shape[1:], jnp.float32),
+        ],
+        scratch_shapes=[pltpu.VMEM((parts, height, QW), jnp.float32)],
+        compiler_params=params(16),
+        name="final",
+    )(band_next, w, *ring, *moms)
+
+
+class Side:
+    def __init__(self, flag, one, two):
+        self.flag, self.one, self.two = flag, one, two
+
+    def __getitem__(self, at):
+        if self.flag is None:
+            return self.one[at]
+        return jnp.where(self.flag, self.one[at], self.two[at])
 
 
 def krylov_kernel(
-    tile_total, sb, meta, band, ldt, z, obs, halo_l, halo_r, w_out, mom_out,
+    tile_total, sb, paired, band, ldt, z, obs, got_e, got_o, w_out, mom_out,
     dh, dl, ucat, seen, u_prev, y
 ):
     rows = ldt.shape[1]
@@ -238,7 +410,10 @@
     own_blocks = rows // LANE
     zb = HZ // LANE
     bb = HB // LANE
-    first_tile = meta[0]
+    first_tile = lax.axis_index("smp") * (rows // TILE)
+    even = lax.rem(lax.axis_index("smp"), 2) == 0 if paired else None
+    halo_r = Side(even, got_e, got_o)
+    halo_l = Side(even, got_o, got_e)
     nb = obs.shape[0]
     ld_rows = SPAN * TILE
     total_blocks = own_blocks + 2 * zb
@@ -370,16 +545,15 @@
     )
 
 
-def krylov(ldt, z, obs, halo_l, halo_r, band_prev, first_tile):
+def krylov(ldt, z, obs, got_e, got_o, band_prev, paired):
     rows, traits = z.shape
     wide = rows + 2 * HB
     sb = 2 * LANE if wide % (2 * LANE) == 0 else LANE
     ext = rows + 2 * HZ
     supers = wide // sb
-    meta = first_tile.reshape(1).astype(jnp.int32)
     return pl.pallas_call(
-        functools.partial(krylov_kernel, band_prev.shape[0], sb),
-        in_specs=[SMEM, SMEM] + [VMEM] * 5,
+        functools.partial(krylov_kernel, band_prev.shape[0], sb, paired),
+        in_specs=[SMEM] + [VMEM] * 5,
         out_specs=[VMEM, VMEM],
         out_shape=[
             jax.ShapeDtypeStruct((ITERS, rows, traits), jnp.float32),
@@ -393,15 +567,15 @@
             pltpu.VMEM((ext, traits), jnp.float32),
             pltpu.VMEM((ext, traits), jnp.float32),
         ],
-        compiler_params=params(),
+        compiler_params=params(28),
         cost_estimate=pl.CostEstimate(
             flops=ITERS * 6 * ext * SPAN * TILE * traits, bytes_accessed=ldt.size * 4, transcendentals=0
         ),
         name="krylov",
-    )(meta, band_prev, ldt, z, obs, halo_l, halo_r)
-
-
-def combine_kernel(w, mom, out):
+    )(band_prev, ldt, z, obs, got_e, got_o)
+
+
+def solve(w, mom, out):
     m = [mom[i : i + 1, :] for i in range(2 * ITERS)]
     shift = 1.0 + RIDGE
     h = [shift * m[i] + m[i + 1] for i in range(2 * ITERS - 1)]
@@ -425,17 +599,6 @@
     out[...] = c0 * w[0] + c1 * w[1] + c2 * w[2]
 
 
-def combine(w, mom):
-    return pl.pallas_call(
-        combine_kernel,
-        in_specs=[VMEM, VMEM],
-        out_specs=VMEM,
-        out_shape=jax.ShapeDtypeStruct(w.shape[1:], jnp.float32),
-        compiler_params=params(),
-        name="combine",
-    )(w, mom)
-
-
 def packed(z, ldt, obs):
     z = jnp.pad(z, ((0, 0), (0, LANE - z.shape[1])))
     obs = obs.astype(jnp.float32)
@@ -454,11 +617,6 @@
     def shifted(value, by):
         pairs = [(i, i + by) for i in range(count) if 0 <= i + by < count]
         return lax.ppermute(value, axis, pairs)
-
-    if rows >= HZ:
-        last = packed(z[rows - HZ :], ldt[:, rows - HB :], obs[:, rows - HZ :])
-        head = packed(z[:HZ], ldt[:, :HB], obs[:, :HZ])
-        return shifted(last, 1), shifted(head, -1)
 
     def gather(value, width, dim):
         lefts, rights = [], []
@@ -481,46 +639,38 @@
     samples, cols = dosage.shape
     rows = ld_prev.shape[0]
     n_smp = lax.axis_size("smp")
-    k = lax.axis_index("smp")
-    snp, pair = lax.axis_index("snp"), lax.axis_index("pair")
-    n_snp, n_pair = lax.axis_size("snp"), lax.axis_size("pair")
-    place = snp * n_pair + pair
-    count = n_snp * n_pair
-
     ldt = ld_prev.T
     obs = observed.T
-    halo_l, halo_r = halos(zscores, ldt, obs, "smp")
-
     line = ("snp", "pair")
-    right = lax.ppermute(dosage[:, :LANE], line, [(i + 1, i) for i in range(count - 1)])
-    left = lax.ppermute(dosage[:, cols - LANE :], line, [(i, i + 1) for i in range(count - 1)])
+    paired = rows >= HZ
+
+    sent = pack(dosage, zscores, ldt, obs, paired)
+    dos_e = exchange(sent[0], line, 0)
+    dos_o = exchange(sent[1], line, 1)
+    if paired:
+        got_e = exchange(sent[2], ("smp",), 0)
+        got_o = exchange(sent[3], ("smp",), 1)
+    else:
+        got_o, got_e = halos(zscores, ldt, obs, "smp")
 
     parts = cols // QW
-    rot = parts == n_smp
-    inv = 1.0 / (samples * n_smp)
-    blocks = gram_parts(dosage, left, right, allele_mean, snp_scale, k, place, rot, inv)
+    rot = parts == n_smp and zscores.shape[1] == LANE
+    blocks = gram_parts(dosage, dos_e, dos_o, allele_mean, snp_scale, rot, samples * n_smp)
     if rot:
-        cycle = lambda value, by: lax.ppermute(
-            value, "smp", [(i, (i + by) % n_smp) for i in range(n_smp)]
-        )
-        total = blocks[0]
-        for by in range(1, n_smp):
-            total = total + cycle(blocks[by].astype(jnp.float16), by).astype(jnp.float32)
-        total = total.astype(jnp.float16)
-        ring = [total] + [cycle(total, by) for by in range(1, n_smp)]
-        stacked = jnp.stack(ring)
-        pieces = [
-            lax.dynamic_index_in_dim(stacked, lax.rem(k + n_smp - q, n_smp), 0, keepdims=False).astype(
-                jnp.float32
-            )
-            for q in range(parts)
-        ]
+
+        def cycle(value, by):
+            return lax.ppermute(value, "smp", [(i, (i + by) % n_smp) for i in range(n_smp)])
+
+        got = [cycle(blocks[by], by) for by in range(1, n_smp)]
+    w, mom = krylov(ldt, zscores, obs, got_e, got_o, band_prev, paired)
+    if rot:
+        mine = total_of(blocks[0], got, mom)
+        ring = [mine] + [cycle(mine, by) for by in range(1, n_smp)]
+        moms = []
     else:
-        pieces = lax.psum(tuple(blocks), "smp")
-    ldn = assemble(pieces, band_next, place * (cols // TILE), cols)
-
-    w, mom = krylov(ldt, zscores, obs, halo_l, halo_r, band_prev, k * (rows // TILE))
-    imputed = combine(w, lax.psum(mom, "smp"))
+        ring = list(lax.psum(tuple(blocks), "smp"))
+        moms = [lax.psum(mom, "smp")]
+    ldn, imputed = final(ring, moms, w, band_next, cols, rot)
     return ldn.T, imputed
 
 

time: 68.9 us -> 52.4 us (0.76)
  blocking collectives: 10.9 us -> 0 us
  Pallas kernels: 19.8 us -> 13.2 us
  other arithmetic: 6.14 us -> 0 us
  waiting for transfers between devices: 8.99 us -> 15.1 us
  local copies, waits for them, and re-layouts: 1.64 us -> 5.27 us
  starting transfers between devices: 20.1 us -> 17.7 us
    psum x1 -> x0, blocking collectives: 10.9 us -> none  [local(): imputed = combine(w, lax.psum(mom, 'smp'))]
    pallas_call x4 -> x5, Pallas kernels: 19.8 us -> 13.2 us  [the longest x1 5.51 us: gram_parts(): pl.pallas_call(functools.partial(gram_kernel, parts, rot, samples_total),...]
    ppermute x10, waiting for transfers between devices: 8.99 us -> 15.1 us  [the longest x6 15.1 us: cycle(): lax.ppermute(value, 'smp', [(i, (i + by) % n_smp) for i in range(n_smp)])]
    unnamed x6 -> x24, local copies, waits for them, and re-layouts: 0.02 us -> 5.27 us
    convert_element_type x6 -> x0, other arithmetic: 4.78 us -> none  [the longest x3 2.84 us: local(): blocks[by].astype(jnp.float16)]
    ppermute x10, starting transfers between devices: 20.1 us -> 17.7 us  [the longest x6 13 us: cycle(): lax.ppermute(value, 'smp', [(i, (i + by) % n_smp) for i in range(n_smp)])]
    slice x4 -> x0, local copies, waits for them, and re-layouts: 1.5 us -> none  [the longest x1 1.42 us: local(): dosage[:, cols - LANE:]]
    another operation x3 -> x0, other arithmetic: 1.36 us -> none  [the longest x1 0.67 us: gram_parts(): meta = jnp.stack([k, column_place * total]).astype(jnp.int32)]
  transfers between devices with their start and end apart: 10 -> 10, of which waited for: 2 -> 3; matrix products, arithmetic and copies ran while one was open for 8% -> 0% of each run, Pallas kernels for 25% -> 18%
where the time goes in v3:
time: 52.4 us; the launch traced here: 52.1 us
  starting transfers between devices  17.7 us (34%)
  waiting for transfers between devices  15.1 us (29%)
  Pallas kernels  13.2 us (25%)
  local copies, waits for them, and re-layouts  5.27 us (10%)
  between operations  0.8 us (2%)
    ppermute x6, waiting for transfers between devices, cycle(): lax.ppermute(value, 'smp', [(i, (i + by) % n_smp) for i in range(n_smp)])  15.1 us
    ppermute x6, starting transfers between devices, cycle(): lax.ppermute(value, 'smp', [(i, (i + by) % n_smp) for i in range(n_smp)])  13 us
    pallas_call x1, Pallas kernels, gram_parts(): pl.pallas_call(functools.partial(gram_kernel, parts, rot, samples_total),...  5.51 us
    unnamed x24, local copies, waits for them, and re-layouts  5.27 us
    ppermute x3, starting transfers between devices, exchange(): return lax.ppermute(value, axes, pairs)  4.15 us
    pallas_call x1, Pallas kernels, krylov(): pl.pallas_call(functools.partial(krylov_kernel, band_prev.shape[0], sb, p...  3.98 us
    pallas_call x1, Pallas kernels, final(): pl.pallas_call(functools.partial(final_kernel, parts, rot, len(moms), ban...  2.35 us
  transfers between devices with their start and end apart: 10, of which 3 were waited for; matrix products, arithmetic and copies ran while one was open for 0% of the time, Pallas kernels for 18%

profile of v3, /device:TPU:0, one launch (start us, length us, event | category | flops | bytes accessed | tf_op | source)
XLA Modules:
  0.0 52.1 jit_solution(17455436573110840205)
XLA Ops:
  0.6 0.0 copy-start
  0.6 2.2 %copy-done = bf16[2048,1024]{1,0:T(8,128)(2,1)S(1)} copy-done((bf16[2048,1024]{1,0:T(8,128)(2,1)S(1)}, bf16[2048,1024]{1,0:T(8,128)(2,1)}, u32[]{:S(2)}) %copy-start) | copy-done | bytes 4194328
  2.8 0.0 copy-start.2
  2.8 1.3 %copy-done.2 = f32[1024,320]{0,1:T(8,128)S(1)} copy-done((f32[1024,320]{0,1:T(8,128)S(1)}, f32[1024,320]{0,1:T(8,128)}, u32[]{:S(2)}) %copy-start.2) | copy-done | bytes 1310744
  4.1 0.0 copy-start.4
  4.1 1.0 %copy-done.4 = f32[1024,128]{1,0:T(8,128)S(1)} copy-done((f32[1024,128]{1,0:T(8,128)S(1)}, f32[1024,128]{1,0:T(8,128)}, u32[]{:S(2)}) %copy-start.4) | copy-done | bytes 524312
  5.2 0.0 copy-start.6
  5.2 0.7 %copy-done.6 = s32[1024,2]{0,1:T(2,128)S(1)} copy-done((s32[1024,2]{0,1:T(2,128)S(1)}, s32[1024,2]{0,1:T(2,128)}, u32[]{:S(2)}) %copy-start.6) | copy-done | bytes 8216
  5.9 0.0 copy-start.1
  5.9 0.0 copy-start.9
  5.9 0.0 copy-start.10
  5.9 1.0 %pack.1 = (bf16[2048,128]{1,0:T(8,128)(2,1)S(1)}, bf16[2048,128]{1,0:T(8,128)(2,1)S(1)}, f32[1032,128]{1,0:T(8,128)S(1)}, f32[1032,128]{1,0:T(8,128)S(1)}) custom-call(bf16[2048,1024]{1,0:T(8,128)(2,1)S(1)} %copy-done, f32[1024,128]{1,0:T(8,128)S(1)} %copy-done.4, f32[320,1024]{1,0:T(8,128)S(1)} %bitcast.5, s32[2,1024]{1,0:T(2,128)S(1)} %bitcast.7), custom_call_target="tpu_custom_call" | custom-call | tf_op jit(solution)/shard_map/pack/pallas_call | solution.py:162
  6.9 0.6 %collective-permute-start.2 = (bf16[2048,128]{1,0:T(8,128)(2,1)S(1)}, bf16[2048,128]{1,0:T(8,128)(2,1)S(1)}, u32[]{:S(2)}, u32[]{:S(2)}) collective-permute-start(bf16[2048,128]{1,0:T(8,128)(2,1)S(1)} %get-tuple-element.17), channel_id=1, source_target_pairs={{0,1},{1,0},{2,3},{3,2},{4,5},{5,4},{6,7},{7,6},{8,9},{9,8},{10,11... | collective-permute-start | bytes 1572872 | tf_op jit(solution)/shard_map/ppermute | solution.py:178
  7.4 0.7 %collective-permute-start.3 = (bf16[2048,128]{1,0:T(8,128)(2,1)S(1)}, bf16[2048,128]{1,0:T(8,128)(2,1)S(1)}, u32[]{:S(2)}, u32[]{:S(2)}) collective-permute-start(bf16[2048,128]{1,0:T(8,128)(2,1)S(1)} %get-tuple-element.18), channel_id=1, source_target_pairs={{1,2},{2,1},{5,6},{6,5},{9,10},{10,9},{13,14},{14,13},{17,18},{18,... | collective-permute-start | bytes 1572872 | tf_op jit(solution)/shard_map/ppermute | solution.py:182
  8.1 2.8 %collective-permute-start = (f32[1032,128]{1,0:T(8,128)S(1)}, f32[1032,128]{1,0:T(8,128)S(1)}, u32[]{:S(2)}, u32[]{:S(2)}) collective-permute-start(f32[1032,128]{1,0:T(8,128)S(1)} %get-tuple-element.14), channel_id=1, source_target_pairs={{0,4},{4,0},{8,12},{12,8},{1,5},{5,1},{9,13},{13,9},{2,6},{6,2},{1... | collective-permute-start | bytes 1585160 | tf_op jit(solution)/shard_map/ppermute | solution.py:182
  10.9 0.7 %collective-permute-start.1 = (f32[1032,128]{1,0:T(8,128)S(1)}, f32[1032,128]{1,0:T(8,128)S(1)}, u32[]{:S(2)}, u32[]{:S(2)}) collective-permute-start(f32[1032,128]{1,0:T(8,128)S(1)} %get-tuple-element.15), channel_id=1, source_target_pairs={{4,8},{8,4},{5,9},{9,5},{6,10},{10,6},{7,11},{11,7},{20,24},{24,20... | collective-permute-start | bytes 1585160 | tf_op jit(solution)/shard_map/ppermute | solution.py:182
  11.6 0.0 collective-permute-done.2.got_e
  11.6 0.0 collective-permute-done.3.got_o
  11.6 0.0 copy-done.1
  11.6 0.0 copy-done.9
  11.6 0.0 copy-done.10
  11.6 0.0 copy-start.3
  11.6 0.0 copy-start.5
  11.7 0.0 copy-start.7
  11.7 0.0 copy-start.11
  11.7 5.5 %gram.1 = (f32[208,256]{1,0:T(8,128)S(1)}, s16[208,256]{1,0:T(8,128)(2,1)S(1)}, s16[208,256]{1,0:T(8,128)(2,1)S(1)}, s16[208,256]{1,0:T(8,128)(2,1)S(1)}) custom-call(bf16[2048,1024]{1,0:T(8,128)(2,1)S(1)} %copy-done.1, bf16[2048,128]{1,0:T(8,128)(2,1)S(1)} %collective-permute-done.2.got_e, bf16[2048,128]{1,0:T(8,128)(2,1)S(1)} %collective-permute-done.3.got_o, ...), custom_call_target="tpu_custom_call" | custom-call | flops 1610612736 | bytes 8388608 | tf_op jit(solution)/shard_map/gram/pallas_call | solution.py:280
  17.2 4.4 %collective-permute-start.4 = (s16[208,256]{1,0:T(8,128)(2,1)S(1)}, s16[208,256]{1,0:T(8,128)(2,1)S(1)}, u32[]{:S(2)}, u32[]{:S(2)}) collective-permute-start(s16[208,256]{1,0:T(8,128)(2,1)S(1)} %get-tuple-element.20), channel_id=1, source_target_pairs={{0,4},{4,8},{8,12},{12,0},{1,5},{5,9},{9,13},{13,1},{2,6},{6,10},{... | collective-permute-start | bytes 319496 | tf_op jit(solution)/shard_map/ppermute | solution.py:662
  21.6 0.0 collective-permute-start.5
  21.6 2.4 %collective-permute-start.6 = (s16[208,256]{1,0:T(8,128)(2,1)S(1)}, s16[208,256]{1,0:T(8,128)(2,1)S(1)}, u32[]{:S(2)}, u32[]{:S(2)}) collective-permute-start(s16[208,256]{1,0:T(8,128)(2,1)S(1)} %get-tuple-element.22), channel_id=1, source_target_pairs={{0,12},{4,0},{8,4},{12,8},{1,13},{5,1},{9,5},{13,9},{2,14},{6,2},{... | collective-permute-start | bytes 319496 | tf_op jit(solution)/shard_map/ppermute | solution.py:662
  24.1 0.0 collective-permute-done.got_e
  24.1 0.0 collective-permute-done.1.got_o
  24.1 0.0 copy-done.3
  24.1 0.0 copy-done.5
  24.1 0.0 copy-done.7
  24.1 0.0 copy-done.11
  24.1 4.0 %krylov.1 = (f32[3,1024,128]{2,1,0:T(8,128)S(1)}, f32[8,128]{1,0:T(8,128)S(1)}) custom-call(s32[64]{0:T(128)S(1)} %copy-done.11, f32[320,1024]{1,0:T(8,128)S(1)} %bitcast.6, f32[1024,128]{1,0:T(8,128)S(1)} %copy-done.5, s32[2,1024]{1,0:T(2,128)S(1)} %bitcast.8, f32[1032,128]{1,0:T(8,128)S(1)} %collective-permute-done.got_e, ...), custom_call_target="tpu_custom_call" | custom-call | flops 1321205760 | bytes 1310720 | tf_op jit(solution)/shard_map/krylov/pallas_call | solution.py:554
  28.1 0.0 collective-permute-done.4.rest_0_
  28.1 5.1 %collective-permute-done.5.rest_1_ = s16[208,256]{1,0:T(8,128)(2,1)S(1)} collective-permute-done((s16[208,256]{1,0:T(8,128)(2,1)S(1)}, s16[208,256]{1,0:T(8,128)(2,1)S(1)}, u32[]{:S(2)}, u32[]{:S(2)}) %collective-permute-start.5) | collective-permute-done | bytes 106528 | tf_op jit(solution)/shard_map/ppermute | solution.py:662
  33.2 0.0 collective-permute-done.6.rest_2_
  33.2 0.4 total.1.rest_0_
  33.6 5.5 %collective-permute-start.9 = (s16[224,256]{1,0:T(8,128)(2,1)S(1)}, s16[224,256]{1,0:T(8,128)(2,1)S(1)}, u32[]{:S(2)}, u32[]{:S(2)}) collective-permute-start(s16[224,256]{1,0:T(8,128)(2,1)S(1)} %total.1.rest_0_), channel_id=1, source_target_pairs={{0,12},{4,0},{8,4},{12,8},{1,13},{5,1},{9,5},{13,9},{2,14},{6,2},{... | collective-permute-start | bytes 344072 | tf_op jit(solution)/shard_map/ppermute | solution.py:662
  39.1 0.0 collective-permute-start.8
  39.1 0.6 %collective-permute-start.7 = (s16[224,256]{1,0:T(8,128)(2,1)S(1)}, s16[224,256]{1,0:T(8,128)(2,1)S(1)}, u32[]{:S(2)}, u32[]{:S(2)}) collective-permute-start(s16[224,256]{1,0:T(8,128)(2,1)S(1)} %total.1.rest_0_), channel_id=1, source_target_pairs={{0,4},{4,8},{8,12},{12,0},{1,5},{5,9},{9,13},{13,1},{2,6},{6,10},{... | collective-permute-start | bytes 344072 | tf_op jit(solution)/shard_map/ppermute | solution.py:662
  39.8 2.5 %collective-permute-done.9.rest_3_ = s16[224,256]{1,0:T(8,128)(2,1)S(1)} collective-permute-done((s16[224,256]{1,0:T(8,128)(2,1)S(1)}, s16[224,256]{1,0:T(8,128)(2,1)S(1)}, u32[]{:S(2)}, u32[]{:S(2)}) %collective-permute-start.9) | collective-permute-done | bytes 114720 | tf_op jit(solution)/shard_map/ppermute | solution.py:662
  42.3 7.4 %collective-permute-done.8.rest_2_ = s16[224,256]{1,0:T(8,128)(2,1)S(1)} collective-permute-done((s16[224,256]{1,0:T(8,128)(2,1)S(1)}, s16[224,256]{1,0:T(8,128)(2,1)S(1)}, u32[]{:S(2)}, u32[]{:S(2)}) %collective-permute-start.8) | collective-permute-done | bytes 114720 | tf_op jit(solution)/shard_map/ppermute | solution.py:662
  49.7 0.0 collective-permute-done.7.rest_1_
  49.7 0.0 copy-done.8
  49.8 2.3 %final.1 = (f32[320,1024]{1,0:T(8,128)}, f32[1024,128]{1,0:T(8,128)}) custom-call(s32[64]{0:T(128)S(1)} %copy-done.8, f32[3,1024,128]{2,1,0:T(8,128)S(1)} %get-tuple-element.16.w, s16[224,256]{1,0:T(8,128)(2,1)S(1)} %total.1.rest_0_, s16[224,256]{1,0:T(8,128)(2,1)S(1)} %collective-permute-done.7.rest_1_, s16[224,256]{1,0:T(8,128)(2,1)S(1)} %collective-permute-done.8.rest_2_, ...), custom_call_target="tpu_custom_call" | custom-call | tf_op jit(solution)/shard_map/final/pallas_call | solution.py:380
  (1 shorter events, 0.0 us)
Async XLA Ops:
  0.6 2.2 %copy-start = (bf16[2048,1024]{1,0:T(8,128)(2,1)S(1)}, bf16[2048,1024]{1,0:T(8,128)(2,1)}, u32[]{:S(2)}) copy-start(bf16[2048,1024]{1,0:T(8,128)(2,1)} %dos.3) | copy-start | bytes 12582916
  2.8 1.3 %copy-start.2 = (f32[1024,320]{0,1:T(8,128)S(1)}, f32[1024,320]{0,1:T(8,128)}, u32[]{:S(2)}) copy-start(f32[1024,320]{0,1:T(8,128)} %param.12) | copy-start | bytes 3932164
  4.1 1.0 %copy-start.4 = (f32[1024,128]{1,0:T(8,128)S(1)}, f32[1024,128]{1,0:T(8,128)}, u32[]{:S(2)}) copy-start(f32[1024,128]{1,0:T(8,128)} %z.3) | copy-start | bytes 1572868
  5.2 0.7 %copy-start.6 = (s32[1024,2]{0,1:T(2,128)S(1)}, s32[1024,2]{0,1:T(2,128)}, u32[]{:S(2)}) copy-start(s32[1024,2]{0,1:T(2,128)} %param.15) | copy-start | bytes 24580
  5.9 5.7 %copy-start.1 = (bf16[2048,1024]{1,0:T(8,128)(2,1)S(1)}, bf16[2048,1024]{1,0:T(8,128)(2,1)}, u32[]{:S(2)}) copy-start(bf16[2048,1024]{1,0:T(8,128)(2,1)} %dos.3) | copy-start | bytes 12582916
  5.9 5.7 %copy-start.9 = (f32[4096]{0:T(1024)S(1)}, f32[4096]{0:T(1024)}, u32[]{:S(2)}) copy-start(f32[4096]{0:T(1024)} %param.9) | copy-start | bytes 49156
  5.9 5.7 %copy-start.10 = (f32[4096]{0:T(1024)S(1)}, f32[4096]{0:T(1024)}, u32[]{:S(2)}) copy-start(f32[4096]{0:T(1024)} %param.10) | copy-start | bytes 49156
  6.9 4.7 %collective-permute-start.2 = (bf16[2048,128]{1,0:T(8,128)(2,1)S(1)}, bf16[2048,128]{1,0:T(8,128)(2,1)S(1)}, u32[]{:S(2)}, u32[]{:S(2)}) collective-permute-start(bf16[2048,128]{1,0:T(8,128)(2,1)S(1)} %get-tuple-element.17), channel_id=1, source_target_pairs={{0,1},{1,0},{2,3},{3,2},{4,5},{5,4},{6,7},{7,6},{8,9},{9,8},{10,11... | collective-permute-start | bytes 1572872 | tf_op jit(solution)/shard_map/ppermute | solution.py:178
  7.4 4.2 %collective-permute-start.3 = (bf16[2048,128]{1,0:T(8,128)(2,1)S(1)}, bf16[2048,128]{1,0:T(8,128)(2,1)S(1)}, u32[]{:S(2)}, u32[]{:S(2)}) collective-permute-start(bf16[2048,128]{1,0:T(8,128)(2,1)S(1)} %get-tuple-element.18), channel_id=1, source_target_pairs={{1,2},{2,1},{5,6},{6,5},{9,10},{10,9},{13,14},{14,13},{17,18},{18,... | collective-permute-start | bytes 1572872 | tf_op jit(solution)/shard_map/ppermute | solution.py:182
  8.1 16.0 %collective-permute-start = (f32[1032,128]{1,0:T(8,128)S(1)}, f32[1032,128]{1,0:T(8,128)S(1)}, u32[]{:S(2)}, u32[]{:S(2)}) collective-permute-start(f32[1032,128]{1,0:T(8,128)S(1)} %get-tuple-element.14), channel_id=1, source_target_pairs={{0,4},{4,0},{8,12},{12,8},{1,5},{5,1},{9,13},{13,9},{2,6},{6,2},{1... | collective-permute-start | bytes 1585160 | tf_op jit(solution)/shard_map/ppermute | solution.py:182
  10.9 13.2 %collective-permute-start.1 = (f32[1032,128]{1,0:T(8,128)S(1)}, f32[1032,128]{1,0:T(8,128)S(1)}, u32[]{:S(2)}, u32[]{:S(2)}) collective-permute-start(f32[1032,128]{1,0:T(8,128)S(1)} %get-tuple-element.15), channel_id=1, source_target_pairs={{4,8},{8,4},{5,9},{9,5},{6,10},{10,6},{7,11},{11,7},{20,24},{24,20... | collective-permute-start | bytes 1585160 | tf_op jit(solution)/shard_map/ppermute | solution.py:182
  11.6 12.4 %copy-start.3 = (f32[1024,320]{0,1:T(8,128)S(1)}, f32[1024,320]{0,1:T(8,128)}, u32[]{:S(2)}) copy-start(f32[1024,320]{0,1:T(8,128)} %param.12) | copy-start | bytes 3932164
  11.6 12.4 %copy-start.5 = (f32[1024,128]{1,0:T(8,128)S(1)}, f32[1024,128]{1,0:T(8,128)}, u32[]{:S(2)}) copy-start(f32[1024,128]{1,0:T(8,128)} %z.3) | copy-start | bytes 1572868
  11.7 12.4 %copy-start.7 = (s32[1024,2]{0,1:T(2,128)S(1)}, s32[1024,2]{0,1:T(2,128)}, u32[]{:S(2)}) copy-start(s32[1024,2]{0,1:T(2,128)} %param.15) | copy-start | bytes 24580
  11.7 12.4 %copy-start.11 = (s32[64]{0:T(128)S(1)}, s32[64]{0:T(128)}, u32[]{:S(2)}) copy-start(s32[64]{0:T(128)} %band.2) | copy-start | bytes 772
  17.2 10.9 %collective-permute-start.4 = (s16[208,256]{1,0:T(8,128)(2,1)S(1)}, s16[208,256]{1,0:T(8,128)(2,1)S(1)}, u32[]{:S(2)}, u32[]{:S(2)}) collective-permute-start(s16[208,256]{1,0:T(8,128)(2,1)S(1)} %get-tuple-element.20), channel_id=1, source_target_pairs={{0,4},{4,8},{8,12},{12,0},{1,5},{5,9},{9,13},{13,1},{2,6},{6,10},{... | collective-permute-start | bytes 319496 | tf_op jit(solution)/shard_map/ppermute | solution.py:662
  21.6 11.6 %collective-permute-start.5 = (s16[208,256]{1,0:T(8,128)(2,1)S(1)}, s16[208,256]{1,0:T(8,128)(2,1)S(1)}, u32[]{:S(2)}, u32[]{:S(2)}) collective-permute-start(s16[208,256]{1,0:T(8,128)(2,1)S(1)} %get-tuple-element.21), channel_id=1, source_target_pairs={{0,8},{4,12},{8,0},{12,4},{1,9},{5,13},{9,1},{13,5},{2,10},{6,14},... | collective-permute-start | bytes 319496 | tf_op jit(solution)/shard_map/ppermute | solution.py:662
  21.6 28.1 %copy-start.8 = (s32[64]{0:T(128)S(1)}, s32[64]{0:T(128)}, u32[]{:S(2)}) copy-start(s32[64]{0:T(128)} %band.3) | copy-start | bytes 772
  21.6 11.6 %collective-permute-start.6 = (s16[208,256]{1,0:T(8,128)(2,1)S(1)}, s16[208,256]{1,0:T(8,128)(2,1)S(1)}, u32[]{:S(2)}, u32[]{:S(2)}) collective-permute-start(s16[208,256]{1,0:T(8,128)(2,1)S(1)} %get-tuple-element.22), channel_id=1, source_target_pairs={{0,12},{4,0},{8,4},{12,8},{1,13},{5,1},{9,5},{13,9},{2,14},{6,2},{... | collective-permute-start | bytes 319496 | tf_op jit(solution)/shard_map/ppermute | solution.py:662
  33.6 8.7 %collective-permute-start.9 = (s16[224,256]{1,0:T(8,128)(2,1)S(1)}, s16[224,256]{1,0:T(8,128)(2,1)S(1)}, u32[]{:S(2)}, u32[]{:S(2)}) collective-permute-start(s16[224,256]{1,0:T(8,128)(2,1)S(1)} %total.1.rest_0_), channel_id=1, source_target_pairs={{0,12},{4,0},{8,4},{12,8},{1,13},{5,1},{9,5},{13,9},{2,14},{6,2},{... | collective-permute-start | bytes 344072 | tf_op jit(solution)/shard_map/ppermute | solution.py:662
  39.1 10.6 %collective-permute-start.8 = (s16[224,256]{1,0:T(8,128)(2,1)S(1)}, s16[224,256]{1,0:T(8,128)(2,1)S(1)}, u32[]{:S(2)}, u32[]{:S(2)}) collective-permute-start(s16[224,256]{1,0:T(8,128)(2,1)S(1)} %total.1.rest_0_), channel_id=1, source_target_pairs={{0,8},{4,12},{8,0},{12,4},{1,9},{5,13},{9,1},{13,5},{2,10},{6,14},... | collective-permute-start | bytes 344072 | tf_op jit(solution)/shard_map/ppermute | solution.py:662
  39.1 10.6 %collective-permute-start.7 = (s16[224,256]{1,0:T(8,128)(2,1)S(1)}, s16[224,256]{1,0:T(8,128)(2,1)S(1)}, u32[]{:S(2)}, u32[]{:S(2)}) collective-permute-start(s16[224,256]{1,0:T(8,128)(2,1)S(1)} %total.1.rest_0_), channel_id=1, source_target_pairs={{0,4},{4,8},{8,12},{12,0},{1,5},{5,9},{9,13},{13,1},{2,6},{6,10},{... | collective-permute-start | bytes 344072 | tf_op jit(solution)/shard_map/ppermute | solution.py:662

commit v4 on v3

--- a/solution.py
+++ b/solution.py
@@ -60,24 +60,26 @@
 
 
 LEVELS = 32000.0
+Z_LARGEST = 22.0
+Z_ROOTS = 2
 LARGEST = 36.0
 
 
-def encode(value):
-    size = jnp.minimum(jnp.abs(value) * (1.0 / LARGEST), 1.0) + 1e-30
-    for _ in range(3):
+def encode(value, largest=LARGEST, roots=3):
+    size = jnp.minimum(jnp.abs(value) * (1.0 / largest), 1.0) + 1e-30
+    for _ in range(roots):
         size = size * lax.rsqrt(size)
     code = size * LEVELS + 0.5
-    return jnp.where(value < 0, -code, code).astype(jnp.int32).astype(jnp.int16)
-
-
-def decode(code):
-    value = code.astype(jnp.int32).astype(jnp.float32)
-    power = value * (1.0 / LEVELS)
-    square = power * power
-    fourth = square * square
-    eighth = fourth * fourth * LARGEST
-    return jnp.where(value < 0, -eighth, eighth)
+    return to_code(jnp.where(value < 0, -code, code))
+
+
+def decode(code, largest=LARGEST, roots=3):
+    value = from_code(code)
+    size = value * (1.0 / LEVELS)
+    for _ in range(roots):
+        size = size * size
+    size = size * largest
+    return jnp.where(value < 0, -size, size)
 
 
 def encode_exact(value):
@@ -108,10 +110,19 @@
     return place
 
 
+def in_hbm(value):
+    return pltpu.with_memory_space_constraint(value, pltpu.HBM)
+
+
+def halo_height(nb):
+    height = HZ + HB // LANE * SPAN * TILE + HZ // LANE * nb
+    return height + -height % 16
+
+
 def pack_kernel(dos, z, ldt, obs, dos_e, dos_o, *rest):
-    halo, sem = rest[:-1], rest[-1]
     cols = dos.shape[1]
     rows = z.shape[0]
+    sem = rest[-1]
     copies = []
 
     def start(source, target):
@@ -122,31 +133,34 @@
     even = lax.rem(line_index(("snp", "pair")), 2) == 0
     to_e = pl.multiple_of(jnp.where(even, cols - LANE, 0), LANE)
     to_o = pl.multiple_of(jnp.where(even, 0, cols - LANE), LANE)
+    halo = ()
+    if len(rest) > 1:
+        halo, (zs, lds, flags) = rest[:2], rest[2:5]
+        even = lax.rem(lax.axis_index("smp"), 2) == 0
+        for i, last in enumerate((even, jnp.logical_not(even))):
+            row = pl.multiple_of(jnp.where(last, rows - HZ, 0), LANE)
+            col = pl.multiple_of(jnp.where(last, rows - HB, 0), LANE)
+            start(z.at[pl.ds(row, HZ), :], zs.at[i])
+            start(ldt.at[:, pl.ds(col, HB)], lds.at[i])
+            start(obs.at[:, pl.ds(row, HZ)], flags.at[i])
     start(dos.at[:, pl.ds(to_e, LANE)], dos_e)
     start(dos.at[:, pl.ds(to_o, LANE)], dos_o)
-    if halo:
-        even = lax.rem(lax.axis_index("smp"), 2) == 0
-        spots = []
-        for out, last in ((halo[0], even), (halo[1], jnp.logical_not(even))):
-            row = pl.multiple_of(jnp.where(last, rows - HZ, 0), LANE)
-            col = pl.multiple_of(jnp.where(last, rows - HB, 0), LANE)
-            spots.append(row)
-            start(z.at[pl.ds(row, HZ), :], out.at[0:HZ, :])
-            for i in range(HB // LANE):
-                start(
-                    ldt.at[:, pl.ds(pl.multiple_of(col + i * LANE, LANE), LANE)],
-                    out.at[HZ + i * SPAN * TILE : HZ + (i + 1) * SPAN * TILE, :],
-                )
+    for i, out in enumerate(halo):
         nb = obs.shape[0]
-        base = HZ + HB // LANE * SPAN * TILE
-        for out, row in zip(halo, spots):
-            for i in range(HZ // LANE):
-                flags = obs[:, pl.ds(pl.multiple_of(row + i * LANE, LANE), LANE)]
-                out[base + i * nb : base + (i + 1) * nb, :] = flags.astype(jnp.float32)
-            used = base + HZ // LANE * nb
-            if used < out.shape[0]:
-                out[used:, :] = jnp.zeros((out.shape[0] - used, LANE), jnp.float32)
-    for copy in copies:
+        for copy in copies[3 * i : 3 * i + 3]:
+            copy.wait()
+        out[0:HZ, : z.shape[1]] = encode(zs[i], Z_LARGEST, Z_ROOTS)
+        base = HZ
+        for j in range(HB // LANE):
+            out[base : base + SPAN * TILE, :] = to_code(
+                jnp.round(lds[i, :, j * LANE : (j + 1) * LANE] * LEVELS)
+            )
+            base += SPAN * TILE
+        bits = [flags[i, :, j * LANE : (j + 1) * LANE] for j in range(HZ // LANE)]
+        blank = out.shape[0] - base - nb * len(bits)
+        bits.append(jnp.zeros((blank, LANE), jnp.int32))
+        out[base:, :] = jnp.concatenate(bits, axis=0).astype(jnp.int16)
+    for copy in copies[3 * len(halo) :]:
         copy.wait()
 
 
@@ -154,20 +168,25 @@
     samples = dosage.shape[0]
     shapes = [jax.ShapeDtypeStruct((samples, LANE), dosage.dtype)] * 2
     copies = 2
+    scratch = []
     if with_halo:
-        height = HZ + HB // LANE * SPAN * TILE + HZ // LANE * obs.shape[0]
-        shapes += [jax.ShapeDtypeStruct((height + -height % 8, LANE), jnp.float32)] * 2
-        copies += 2 * (1 + HB // LANE)
+        shapes += [jax.ShapeDtypeStruct((halo_height(obs.shape[0]), LANE), jnp.int16)] * 2
+        copies += 6
+        scratch = [
+            pltpu.VMEM((2, HZ, z.shape[1]), z.dtype),
+            pltpu.VMEM((2, SPAN * TILE, HB), ldt.dtype),
+            pltpu.VMEM((2, obs.shape[0], HZ), obs.dtype),
+        ]
     far = pl.BlockSpec(memory_space=pltpu.HBM)
     return pl.pallas_call(
         pack_kernel,
-        in_specs=[far, far, far, VMEM],
+        in_specs=[far] * 4,
         out_specs=[VMEM] * len(shapes),
         out_shape=shapes,
-        scratch_shapes=[pltpu.SemaphoreType.DMA((copies,))],
+        scratch_shapes=scratch + [pltpu.SemaphoreType.DMA((copies,))],
         compiler_params=params(8),
         name="pack",
-    )(dosage, z, ldt, obs)
+    )(in_hbm(dosage), in_hbm(z), in_hbm(ldt), in_hbm(obs))
 
 
 def exchange(value, axes, phase):
@@ -182,16 +201,20 @@
     return lax.ppermute(value, axes, pairs)
 
 
-def gram_kernel(parts, rot, samples_total, dos, got_e, got_o, mean, scale, *rest):
+def standard(values, mean, scale, block):
+    row = jnp.clip(block, 0, mean.shape[0] - 1)
+    m = mean[pl.ds(row, 1), :]
+    s = scale[pl.ds(row, 1), :]
+    return ((values.astype(jnp.float32) - m) * s).astype(jnp.bfloat16)
+
+
+def gram_kernel(parts, rot, inv, dos, mean, scale, *rest):
     outs = rest[:parts]
-    raw, normed, cross, sem = rest[parts:]
+    raw, normed, sem = rest[parts:]
     blocks = QW // LANE
     samples, cols = dos.shape
-    place = line_index(("snp", "pair"))
-    base = place * (cols // LANE)
-    lanes_total = mean.shape[0]
+    base = line_index(("snp", "pair")) * (cols // LANE)
     first = lax.axis_index("smp") if rot else 0
-    inv = 1.0 / (samples if rot else samples_total)
 
     def quarter_of(g):
         return lax.rem(g + first, parts)
@@ -202,12 +225,6 @@
 
     for g in range(parts):
         fetch(g).start()
-
-    def standard(values, block):
-        row = jnp.clip(block, 0, lanes_total - 1)
-        m = mean[pl.ds(row, 1), :]
-        s = scale[pl.ds(row, 1), :]
-        return ((values.astype(jnp.float32) - m) * s).astype(jnp.bfloat16)
 
     def settle(g):
         fetch(g).wait()
@@ -215,32 +232,20 @@
         for b in range(blocks):
             at = pl.multiple_of((block + b) * LANE, LANE)
             normed[:, pl.ds(at, LANE)] = standard(
-                raw[g, :, b * LANE : (b + 1) * LANE], base + block + b
+                raw[g, :, b * LANE : (b + 1) * LANE], mean, scale, base + block + b
             )
 
-    even = lax.rem(place, 2) == 0
-    got = [got_e[...], got_o[...]]
-    right = jnp.where(even, got[0], got[1])
-    left = jnp.where(even, got[1], got[0])
-    normed[:, cols:] = standard(right, base + cols // LANE)
-    raw_left = standard(left, base - 1)
+    normed[:, cols:] = jnp.zeros((samples, LANE), jnp.bfloat16)
     settle(0)
     rows = (BMAX + 1) * TILE
     low = low_lanes((rows, LANE))
-    share = LANE // parts // blocks
-
-    fetch0 = pltpu.make_async_copy(dos.at[:, 0:LANE], raw.at[parts, :, 0:LANE], sem.at[parts])
-    fetch0.start()
-    fetch0.wait()
-    cross[...] = inv * tdot(raw_left, standard(raw[parts, :, 0:LANE], base))
 
     def step(g, _):
         @pl.when(g < parts - 1)
         def _():
             settle(jnp.minimum(g + 1, parts - 1))
 
-        quarter = quarter_of(g)
-        at = pl.multiple_of(quarter * QW, QW)
+        at = pl.multiple_of(quarter_of(g) * QW, QW)
         full = tdot(normed[:, pl.ds(at, QW + LANE)], normed[:, pl.ds(at, QW)])
         pieces = []
         for b in range(blocks):
@@ -253,47 +258,93 @@
                     full[b * LANE + TILE : b * LANE + TILE + rows, cut],
                 )
             )
-        start = quarter * (share * blocks)
-        shares = [
-            cross[pl.ds(pl.multiple_of(start + b * share, 8), share), :] for b in range(blocks)
-        ]
         for i in range(parts):
 
             @pl.when(g == i)
             def _(i=i):
                 for b in range(blocks):
                     cut = slice(b * LANE, (b + 1) * LANE)
-                    send = encode if rot and i > 0 else (lambda v: v)
-                    outs[i][0:rows, cut] = send(pieces[b])
-                    outs[i][rows : rows + share, cut] = send(shares[b])
+                    outs[i][:, cut] = encode(pieces[b]) if rot and i > 0 else pieces[b]
 
         return 0
 
     lax.fori_loop(0, parts, step, 0)
 
 
-def gram_parts(dosage, got_e, got_o, mean, scale, rot, samples_total):
+def gram_parts(dosage, mean, scale, rot, inv):
     samples, cols = dosage.shape
     parts = cols // QW
-    height = (BMAX + 1) * TILE + LANE // parts // (QW // LANE)
+    rows = (BMAX + 1) * TILE
     kinds = [jnp.float32] + [jnp.int16 if rot else jnp.float32] * (parts - 1)
     return pl.pallas_call(
-        functools.partial(gram_kernel, parts, rot, samples_total),
-        in_specs=[pl.BlockSpec(memory_space=pltpu.HBM)] + [VMEM] * 4,
+        functools.partial(gram_kernel, parts, rot, inv),
+        in_specs=[pl.BlockSpec(memory_space=pltpu.HBM)] + [VMEM] * 2,
         out_specs=[VMEM] * parts,
-        out_shape=[jax.ShapeDtypeStruct((height, QW), kind) for kind in kinds],
+        out_shape=[jax.ShapeDtypeStruct((rows, QW), kind) for kind in kinds],
         scratch_shapes=[
-            pltpu.VMEM((parts + 1, samples, QW), jnp.bfloat16),
+            pltpu.VMEM((parts, samples, QW), jnp.bfloat16),
             pltpu.VMEM((samples, cols + LANE), jnp.bfloat16),
-            pltpu.VMEM((LANE, LANE), jnp.float32),
-            pltpu.SemaphoreType.DMA((parts + 1,)),
+            pltpu.SemaphoreType.DMA((parts,)),
         ],
         compiler_params=params(24),
         cost_estimate=pl.CostEstimate(
             flops=2 * samples * cols * (QW + LANE), bytes_accessed=dosage.size * 4, transcendentals=0
         ),
         name="gram",
-    )(dosage, got_e, got_o, mean.reshape(-1, LANE), scale.reshape(-1, LANE))
+    )(in_hbm(dosage), mean, scale)
+
+
+def cross_kernel(parts, rot, inv, cols, sent_e, sent_o, got_e, got_o, mean, scale, *rest):
+    ins, outs, cross = rest[:parts], rest[parts : 2 * parts], rest[-1]
+    blocks = QW // LANE
+    rows = (BMAX + 1) * TILE
+    share = LANE // parts // blocks
+    place = line_index(("snp", "pair"))
+    base = place * (cols // LANE)
+    end = base + cols // LANE
+    even = lax.rem(place, 2) == 0
+    pick = lambda one, two: jnp.where(even, one[...], two[...])
+    right = standard(pick(got_e, got_o), mean, scale, end)
+    left = standard(pick(got_o, got_e), mean, scale, base - 1)
+    last = standard(pick(sent_e, sent_o), mean, scale, end - 1)
+    head = standard(pick(sent_o, sent_e), mean, scale, base)
+    ahead = inv * tdot(right, last)
+    cross[...] = inv * tdot(left, head)
+    low = low_lanes((TILE, LANE))
+    far = slice((blocks - 1) * LANE, blocks * LANE)
+    first = lax.axis_index("smp") if rot else 0
+    for i in range(parts):
+        send = encode if rot and i > 0 else (lambda v: v)
+        wide = (lambda v: v.astype(jnp.int32)) if rot and i > 0 else (lambda v: v)
+        outs[i][0:rows, :] = ins[i][...]
+        quarter = lax.rem(i + first, parts)
+        for b in range(blocks):
+            at = pl.multiple_of((quarter * blocks + b) * share, 8)
+            outs[i][rows : rows + share, b * LANE : (b + 1) * LANE] = send(
+                cross[pl.ds(at, share), :]
+            )
+
+        @pl.when(quarter == parts - 1)
+        def _(i=i, send=send, wide=wide):
+            old = wide(ins[i][TILE : 2 * TILE, far])
+            outs[i][TILE : 2 * TILE, far] = jnp.where(low, old, wide(send(ahead[:TILE]))).astype(
+                outs[i].dtype
+            )
+            outs[i][2 * TILE : rows, far] = send(jnp.where(low, ahead[:TILE], ahead[TILE:]))
+
+
+def cross_parts(sent_e, sent_o, got_e, got_o, mean, scale, blocks, cols, rot, inv):
+    parts = len(blocks)
+    height = (BMAX + 1) * TILE + LANE // parts // (QW // LANE)
+    return pl.pallas_call(
+        functools.partial(cross_kernel, parts, rot, inv, cols),
+        in_specs=[VMEM] * (6 + parts),
+        out_specs=[VMEM] * parts,
+        out_shape=[jax.ShapeDtypeStruct((height, QW), b.dtype) for b in blocks],
+        scratch_shapes=[pltpu.VMEM((LANE, LANE), jnp.float32)],
+        compiler_params=params(12),
+        name="cross",
+    )(sent_e, sent_o, got_e, got_o, mean, scale, *blocks)
 
 
 def total_kernel(count, own, *rest):
@@ -395,10 +446,19 @@
     def __init__(self, flag, one, two):
         self.flag, self.one, self.two = flag, one, two
 
-    def __getitem__(self, at):
+    def pick(self, at, convert):
         if self.flag is None:
             return self.one[at]
-        return jnp.where(self.flag, self.one[at], self.two[at])
+        return jnp.where(self.flag, convert(self.one[at]), convert(self.two[at]))
+
+    def vector(self, at):
+        return self.pick(at, lambda code: decode(code, Z_LARGEST, Z_ROOTS))
+
+    def band(self, at):
+        return self.pick(at, lambda code: from_code(code) * (1.0 / LEVELS))
+
+    def flags(self, at):
+        return self.pick(at, from_code)
 
 
 def krylov_kernel(
@@ -418,13 +478,13 @@
     ld_rows = SPAN * TILE
     total_blocks = own_blocks + 2 * zb
 
+    tail = (slice(HZ + bb * ld_rows, got_e.shape[0]), slice(None))
+    flags_l, flags_r = halo_l.flags(tail), halo_r.flags(tail)
+
     for c in range(total_blocks):
         if c < zb:
-            vec = halo_l[c * LANE : (c + 1) * LANE, :traits]
-            flags = [
-                halo_l[HZ + bb * ld_rows + c * nb + i : HZ + bb * ld_rows + c * nb + i + 1, :]
-                for i in range(nb)
-            ]
+            vec = halo_l.vector((slice(c * LANE, (c + 1) * LANE), slice(0, traits)))
+            flags = [flags_l[c * nb + i : c * nb + i + 1, :] for i in range(nb)]
         elif c < zb + own_blocks:
             o = c - zb
             vec = z[o * LANE : (o + 1) * LANE, :]
@@ -433,11 +493,8 @@
             ]
         else:
             o = c - zb - own_blocks
-            vec = halo_r[o * LANE : (o + 1) * LANE, :traits]
-            flags = [
-                halo_r[HZ + bb * ld_rows + o * nb + i : HZ + bb * ld_rows + o * nb + i + 1, :]
-                for i in range(nb)
-            ]
+            vec = halo_r.vector((slice(o * LANE, (o + 1) * LANE), slice(0, traits)))
+            flags = [flags_r[o * nb + i : o * nb + i + 1, :] for i in range(nb)]
         wide = jnp.concatenate(
             [jnp.broadcast_to(f, (TBLK, LANE)) for f in flags], axis=0
         )
@@ -457,12 +514,14 @@
     chunks = SPAN + 1
     for c in range(own_blocks + 2 * bb):
         if c < bb:
-            get = lambda q, c=c: halo_l[HZ + c * ld_rows + q * TILE : HZ + c * ld_rows + (q + 1) * TILE, :]
+            full = halo_l.band((slice(HZ + c * ld_rows, HZ + (c + 1) * ld_rows), slice(None)))
+            get = lambda q, full=full: full[q * TILE : (q + 1) * TILE]
         elif c < bb + own_blocks:
             get = lambda q, c=c: ldt[q * TILE : (q + 1) * TILE, (c - bb) * LANE : (c - bb + 1) * LANE]
         else:
             o = c - bb - own_blocks
-            get = lambda q, o=o: halo_r[HZ + o * ld_rows + q * TILE : HZ + o * ld_rows + (q + 1) * TILE, :]
+            full = halo_r.band((slice(HZ + o * ld_rows, HZ + (o + 1) * ld_rows), slice(None)))
+            get = lambda q, full=full: full[q * TILE : (q + 1) * TILE]
         masks = mask_rows(band, first_tile + 2 * (c - bb), tile_total)
         s, h = c // per, c % per
         cols = slice(h * LANE, (h + 1) * LANE)
@@ -606,7 +665,7 @@
     parts += [ldt[:, i : i + LANE] for i in range(0, ldt.shape[1], LANE)]
     parts += [obs[:, i : i + LANE] for i in range(0, obs.shape[1], LANE)]
     height = sum(p.shape[0] for p in parts)
-    parts.append(jnp.zeros((-height % 8, LANE), jnp.float32))
+    parts.append(jnp.zeros((-height % 16, LANE), jnp.float32))
     return jnp.concatenate(parts, axis=0)
 
 
@@ -655,7 +714,11 @@
 
     parts = cols // QW
     rot = parts == n_smp and zscores.shape[1] == LANE
-    blocks = gram_parts(dosage, dos_e, dos_o, allele_mean, snp_scale, rot, samples * n_smp)
+    inv = 1.0 / (samples if rot else samples * n_smp)
+    mean = allele_mean.reshape(-1, LANE)
+    scale = snp_scale.reshape(-1, LANE)
+    blocks = gram_parts(dosage, mean, scale, rot, inv)
+    blocks = cross_parts(sent[0], sent[1], dos_e, dos_o, mean, scale, blocks, cols, rot, inv)
     if rot:
 
         def cycle(value, by):

time: 52.4 us -> 44.1 us (0.84)
  local copies, waits for them, and re-layouts: 5.27 us -> 0.04 us
  waiting for transfers between devices: 15.1 us -> 12.2 us
  Pallas kernels: 13.2 us -> 15.1 us
  starting transfers between devices: 17.7 us -> 15.8 us
    unnamed x24 -> x14, local copies, waits for them, and re-layouts: 5.27 us -> 0.04 us
    ppermute x6, waiting for transfers between devices: 15.1 us -> 12.2 us  [cycle(): lax.ppermute(value, 'smp', [(i, (i + by) % n_smp) for i in range(n_smp)])]
    ppermute x6, starting transfers between devices: 13 us -> 11.2 us  [cycle(): lax.ppermute(value, 'smp', [(i, (i + by) % n_smp) for i in range(n_smp)])]
    pallas_call x2 -> x3, Pallas kernels: 6.48 us -> 8.16 us  [the longest x1 5.42 us: gram_parts(): pl.pallas_call(functools.partial(gram_kernel, parts, rot, inv), in_specs=...]
  transfers between devices with their start and end apart: 10 -> 10, of which waited for: 3 -> 3; matrix products, arithmetic and copies ran while one was open for 0% -> 0% of each run, Pallas kernels for 18% -> 24%
where the time goes in v4:
time: 44.1 us; the launch traced here: 43.9 us
  starting transfers between devices  15.8 us (36%)
  Pallas kernels  15.1 us (34%)
  waiting for transfers between devices  12.2 us (28%)
  between operations  0.8 us (2%)
    ppermute x6, waiting for transfers between devices, cycle(): lax.ppermute(value, 'smp', [(i, (i + by) % n_smp) for i in range(n_smp)])  12.2 us
    ppermute x6, starting transfers between devices, cycle(): lax.ppermute(value, 'smp', [(i, (i + by) % n_smp) for i in range(n_smp)])  11.2 us
    pallas_call x1, Pallas kernels, gram_parts(): pl.pallas_call(functools.partial(gram_kernel, parts, rot, inv), in_specs=...  5.42 us
    pallas_call x1, Pallas kernels, krylov(): pl.pallas_call(functools.partial(krylov_kernel, band_prev.shape[0], sb, p...  4.21 us
    ppermute x3, starting transfers between devices, exchange(): return lax.ppermute(value, axes, pairs)  4 us
    pallas_call x1, Pallas kernels, final(): pl.pallas_call(functools.partial(final_kernel, parts, rot, len(moms), ban...  2.35 us
    pallas_call x1, Pallas kernels, pack(): pl.pallas_call(pack_kernel, in_specs=[far] * 4, out_specs=[VMEM] * len(sh...  1.7 us
    pallas_call x1, Pallas kernels, cross_parts(): pl.pallas_call(functools.partial(cross_kernel, parts, rot, inv, cols), in...  1.03 us
  transfers between devices with their start and end apart: 10, of which 3 were waited for; matrix products, arithmetic and copies ran while one was open for 0% of the time, Pallas kernels for 24%

profile of v4, /device:TPU:0, one launch (start us, length us, event | category | flops | bytes accessed | tf_op | source)
XLA Modules:
  0.0 43.9 jit_solution(17138392998949219907)
XLA Ops:
  0.6 0.0 copy-start.2
  0.6 0.0 copy-start.3
  0.6 1.7 %pack.1 = (bf16[2048,128]{1,0:T(8,128)(2,1)S(1)}, bf16[2048,128]{1,0:T(8,128)(2,1)S(1)}, s16[1040,128]{1,0:T(8,128)(2,1)S(1)}, s16[1040,128]{1,0:T(8,128)(2,1)S(1)}) custom-call(bf16[2048,1024]{1,0:T(8,128)(2,1)} %dos.3, f32[1024,128]{1,0:T(8,128)} %z.3, f32[320,1024]{1,0:T(8,128)} %bitcast.5, s32[2,1024]{1,0:T(2,128)} %bitcast.11), custom_call_target="tpu_custom_call" | custom-call | tf_op jit(solution)/shard_map/pack/pallas_call | solution.py:181
  2.4 0.6 %collective-permute-start.2 = (bf16[2048,128]{1,0:T(8,128)(2,1)S(1)}, bf16[2048,128]{1,0:T(8,128)(2,1)S(1)}, u32[]{:S(2)}, u32[]{:S(2)}) collective-permute-start(bf16[2048,128]{1,0:T(8,128)(2,1)S(1)} %get-tuple-element.21.sent_e), channel_id=1, source_target_pairs={{0,1},{1,0},{2,3},{3,2},{4,5},{5,4},{6,7},{7,6},{8,9},{9,8},{10,11... | collective-permute-start | bytes 1572872 | tf_op jit(solution)/shard_map/ppermute | solution.py:197
  2.9 0.7 %collective-permute-start.3 = (bf16[2048,128]{1,0:T(8,128)(2,1)S(1)}, bf16[2048,128]{1,0:T(8,128)(2,1)S(1)}, u32[]{:S(2)}, u32[]{:S(2)}) collective-permute-start(bf16[2048,128]{1,0:T(8,128)(2,1)S(1)} %get-tuple-element.22.sent_o), channel_id=1, source_target_pairs={{1,2},{2,1},{5,6},{6,5},{9,10},{10,9},{13,14},{14,13},{17,18},{18,... | collective-permute-start | bytes 1572872 | tf_op jit(solution)/shard_map/ppermute | solution.py:201
  3.6 2.6 %collective-permute-start = (s16[1040,128]{1,0:T(8,128)(2,1)S(1)}, s16[1040,128]{1,0:T(8,128)(2,1)S(1)}, u32[]{:S(2)}, u32[]{:S(2)}) collective-permute-start(s16[1040,128]{1,0:T(8,128)(2,1)S(1)} %get-tuple-element.18), channel_id=1, source_target_pairs={{0,4},{4,0},{8,12},{12,8},{1,5},{5,1},{9,13},{13,9},{2,6},{6,2},{1... | collective-permute-start | bytes 798728 | tf_op jit(solution)/shard_map/ppermute | solution.py:201
  6.3 0.7 %collective-permute-start.1 = (s16[1040,128]{1,0:T(8,128)(2,1)S(1)}, s16[1040,128]{1,0:T(8,128)(2,1)S(1)}, u32[]{:S(2)}, u32[]{:S(2)}) collective-permute-start(s16[1040,128]{1,0:T(8,128)(2,1)S(1)} %get-tuple-element.19), channel_id=1, source_target_pairs={{4,8},{8,4},{5,9},{9,5},{6,10},{10,6},{7,11},{11,7},{20,24},{24,20... | collective-permute-start | bytes 798728 | tf_op jit(solution)/shard_map/ppermute | solution.py:201
  6.9 0.0 copy-done.2
  6.9 0.0 copy-done.3
  7.0 5.4 %gram.1 = (f32[192,256]{1,0:T(8,128)S(1)}, s16[192,256]{1,0:T(8,128)(2,1)S(1)}, s16[192,256]{1,0:T(8,128)(2,1)S(1)}, s16[192,256]{1,0:T(8,128)(2,1)S(1)}) custom-call(bf16[2048,1024]{1,0:T(8,128)(2,1)} %dos.3, f32[32,128]{1,0:T(8,128)S(1)} %bitcast.7, f32[32,128]{1,0:T(8,128)S(1)} %bitcast.9), custom_call_target="tpu_custom_call" | custom-call | flops 1610612736 | bytes 8388608 | tf_op jit(solution)/shard_map/gram/pallas_call | solution.py:279
  12.4 0.0 copy-start
  12.4 0.0 copy-start.1
  12.4 0.0 copy-start.4
  12.4 0.0 copy-start.6
  12.4 0.0 collective-permute-done.2.got_e
  12.4 0.0 collective-permute-done.3.got_o
  12.5 1.0 %cross.1 = (f32[208,256]{1,0:T(8,128)S(1)}, s16[208,256]{1,0:T(8,128)(2,1)S(1)}, s16[208,256]{1,0:T(8,128)(2,1)S(1)}, s16[208,256]{1,0:T(8,128)(2,1)S(1)}) custom-call(bf16[2048,128]{1,0:T(8,128)(2,1)S(1)} %get-tuple-element.21.sent_e, bf16[2048,128]{1,0:T(8,128)(2,1)S(1)} %get-tuple-element.22.sent_o, bf16[2048,128]{1,0:T(8,128)(2,1)S(1)} %collective-permute-done.2.got_e, ...), custom_call_target="tpu_custom_call" | custom-call | tf_op jit(solution)/shard_map/cross/pallas_call | solution.py:339
  13.5 4.4 %collective-permute-start.4 = (s16[208,256]{1,0:T(8,128)(2,1)S(1)}, s16[208,256]{1,0:T(8,128)(2,1)S(1)}, u32[]{:S(2)}, u32[]{:S(2)}) collective-permute-start(s16[208,256]{1,0:T(8,128)(2,1)S(1)} %get-tuple-element.28), channel_id=1, source_target_pairs={{0,4},{4,8},{8,12},{12,0},{1,5},{5,9},{9,13},{13,1},{2,6},{6,10},{... | collective-permute-start | bytes 319496 | tf_op jit(solution)/shard_map/ppermute | solution.py:725
  17.9 0.0 collective-permute-start.5
  17.9 0.0 copy-start.5
  17.9 2.4 %collective-permute-start.6 = (s16[208,256]{1,0:T(8,128)(2,1)S(1)}, s16[208,256]{1,0:T(8,128)(2,1)S(1)}, u32[]{:S(2)}, u32[]{:S(2)}) collective-permute-start(s16[208,256]{1,0:T(8,128)(2,1)S(1)} %get-tuple-element.30), channel_id=1, source_target_pairs={{0,12},{4,0},{8,4},{12,8},{1,13},{5,1},{9,5},{13,9},{2,14},{6,2},{... | collective-permute-start | bytes 319496 | tf_op jit(solution)/shard_map/ppermute | solution.py:725
  20.4 0.0 collective-permute-done.got_e
  20.4 0.0 collective-permute-done.1.got_o
  20.4 0.0 copy-done
  20.4 0.0 copy-done.1
  20.4 0.0 copy-done.4
  20.4 0.0 copy-done.6
  20.4 4.2 %krylov.1 = (f32[3,1024,128]{2,1,0:T(8,128)S(1)}, f32[8,128]{1,0:T(8,128)S(1)}) custom-call(s32[64]{0:T(128)S(1)} %copy-done.6, f32[320,1024]{1,0:T(8,128)S(1)} %bitcast.6, f32[1024,128]{1,0:T(8,128)S(1)} %copy-done.1, s32[2,1024]{1,0:T(2,128)S(1)} %bitcast.12, s16[1040,128]{1,0:T(8,128)(2,1)S(1)} %collective-permute-done.got_e, ...), custom_call_target="tpu_custom_call" | custom-call | flops 1321205760 | bytes 1310720 | tf_op jit(solution)/shard_map/krylov/pallas_call | solution.py:613
  24.6 0.0 collective-permute-done.4.rest_0_
  24.6 1.7 %collective-permute-done.5.rest_1_ = s16[208,256]{1,0:T(8,128)(2,1)S(1)} collective-permute-done((s16[208,256]{1,0:T(8,128)(2,1)S(1)}, s16[208,256]{1,0:T(8,128)(2,1)S(1)}, u32[]{:S(2)}, u32[]{:S(2)}) %collective-permute-start.5) | collective-permute-done | bytes 106528 | tf_op jit(solution)/shard_map/ppermute | solution.py:725
  26.3 0.0 collective-permute-done.6.rest_2_
  26.3 0.4 total.1.rest_0_
  26.7 2.6 %collective-permute-start.9 = (s16[224,256]{1,0:T(8,128)(2,1)S(1)}, s16[224,256]{1,0:T(8,128)(2,1)S(1)}, u32[]{:S(2)}, u32[]{:S(2)}) collective-permute-start(s16[224,256]{1,0:T(8,128)(2,1)S(1)} %total.1.rest_0_), channel_id=1, source_target_pairs={{0,12},{4,0},{8,4},{12,8},{1,13},{5,1},{9,5},{13,9},{2,14},{6,2},{... | collective-permute-start | bytes 344072 | tf_op jit(solution)/shard_map/ppermute | solution.py:725
  29.3 1.8 %collective-permute-start.8 = (s16[224,256]{1,0:T(8,128)(2,1)S(1)}, s16[224,256]{1,0:T(8,128)(2,1)S(1)}, u32[]{:S(2)}, u32[]{:S(2)}) collective-permute-start(s16[224,256]{1,0:T(8,128)(2,1)S(1)} %total.1.rest_0_), channel_id=1, source_target_pairs={{0,8},{4,12},{8,0},{12,4},{1,9},{5,13},{9,1},{13,5},{2,10},{6,14},... | collective-permute-start | bytes 344072 | tf_op jit(solution)/shard_map/ppermute | solution.py:725
  31.1 0.0 collective-permute-start.7
  31.1 2.0 %collective-permute-done.9.rest_3_ = s16[224,256]{1,0:T(8,128)(2,1)S(1)} collective-permute-done((s16[224,256]{1,0:T(8,128)(2,1)S(1)}, s16[224,256]{1,0:T(8,128)(2,1)S(1)}, u32[]{:S(2)}, u32[]{:S(2)}) %collective-permute-start.9) | collective-permute-done | bytes 114720 | tf_op jit(solution)/shard_map/ppermute | solution.py:725
  33.0 8.5 %collective-permute-done.8.rest_2_ = s16[224,256]{1,0:T(8,128)(2,1)S(1)} collective-permute-done((s16[224,256]{1,0:T(8,128)(2,1)S(1)}, s16[224,256]{1,0:T(8,128)(2,1)S(1)}, u32[]{:S(2)}, u32[]{:S(2)}) %collective-permute-start.8) | collective-permute-done | bytes 114720 | tf_op jit(solution)/shard_map/ppermute | solution.py:725
  41.6 0.0 collective-permute-done.7.rest_1_
  41.6 0.0 copy-done.5
  41.6 2.3 %final.1 = (f32[320,1024]{1,0:T(8,128)}, f32[1024,128]{1,0:T(8,128)}) custom-call(s32[64]{0:T(128)S(1)} %copy-done.5, f32[3,1024,128]{2,1,0:T(8,128)S(1)} %get-tuple-element.20.w, s16[224,256]{1,0:T(8,128)(2,1)S(1)} %total.1.rest_0_, s16[224,256]{1,0:T(8,128)(2,1)S(1)} %collective-permute-done.7.rest_1_, s16[224,256]{1,0:T(8,128)(2,1)S(1)} %collective-permute-done.8.rest_2_, ...), custom_call_target="tpu_custom_call" | custom-call | tf_op jit(solution)/shard_map/final/pallas_call | solution.py:431
Async XLA Ops:
  0.6 6.3 %copy-start.2 = (f32[4096]{0:T(1024)S(1)}, f32[4096]{0:T(1024)}, u32[]{:S(2)}) copy-start(f32[4096]{0:T(1024)} %param.9) | copy-start | bytes 49156
  0.6 6.3 %copy-start.3 = (f32[4096]{0:T(1024)S(1)}, f32[4096]{0:T(1024)}, u32[]{:S(2)}) copy-start(f32[4096]{0:T(1024)} %param.10) | copy-start | bytes 49156
  2.4 10.1 %collective-permute-start.2 = (bf16[2048,128]{1,0:T(8,128)(2,1)S(1)}, bf16[2048,128]{1,0:T(8,128)(2,1)S(1)}, u32[]{:S(2)}, u32[]{:S(2)}) collective-permute-start(bf16[2048,128]{1,0:T(8,128)(2,1)S(1)} %get-tuple-element.21.sent_e), channel_id=1, source_target_pairs={{0,1},{1,0},{2,3},{3,2},{4,5},{5,4},{6,7},{7,6},{8,9},{9,8},{10,11... | collective-permute-start | bytes 1572872 | tf_op jit(solution)/shard_map/ppermute | solution.py:197
  2.9 9.5 %collective-permute-start.3 = (bf16[2048,128]{1,0:T(8,128)(2,1)S(1)}, bf16[2048,128]{1,0:T(8,128)(2,1)S(1)}, u32[]{:S(2)}, u32[]{:S(2)}) collective-permute-start(bf16[2048,128]{1,0:T(8,128)(2,1)S(1)} %get-tuple-element.22.sent_o), channel_id=1, source_target_pairs={{1,2},{2,1},{5,6},{6,5},{9,10},{10,9},{13,14},{14,13},{17,18},{18,... | collective-permute-start | bytes 1572872 | tf_op jit(solution)/shard_map/ppermute | solution.py:201
  3.6 16.8 %collective-permute-start = (s16[1040,128]{1,0:T(8,128)(2,1)S(1)}, s16[1040,128]{1,0:T(8,128)(2,1)S(1)}, u32[]{:S(2)}, u32[]{:S(2)}) collective-permute-start(s16[1040,128]{1,0:T(8,128)(2,1)S(1)} %get-tuple-element.18), channel_id=1, source_target_pairs={{0,4},{4,0},{8,12},{12,8},{1,5},{5,1},{9,13},{13,9},{2,6},{6,2},{1... | collective-permute-start | bytes 798728 | tf_op jit(solution)/shard_map/ppermute | solution.py:201
  6.3 14.1 %collective-permute-start.1 = (s16[1040,128]{1,0:T(8,128)(2,1)S(1)}, s16[1040,128]{1,0:T(8,128)(2,1)S(1)}, u32[]{:S(2)}, u32[]{:S(2)}) collective-permute-start(s16[1040,128]{1,0:T(8,128)(2,1)S(1)} %get-tuple-element.19), channel_id=1, source_target_pairs={{4,8},{8,4},{5,9},{9,5},{6,10},{10,6},{7,11},{11,7},{20,24},{24,20... | collective-permute-start | bytes 798728 | tf_op jit(solution)/shard_map/ppermute | solution.py:201
  12.4 8.0 %copy-start = (f32[1024,320]{0,1:T(8,128)S(1)}, f32[1024,320]{0,1:T(8,128)}, u32[]{:S(2)}) copy-start(f32[1024,320]{0,1:T(8,128)} %param.12) | copy-start | bytes 3932164
  12.4 8.0 %copy-start.1 = (f32[1024,128]{1,0:T(8,128)S(1)}, f32[1024,128]{1,0:T(8,128)}, u32[]{:S(2)}) copy-start(f32[1024,128]{1,0:T(8,128)} %z.3) | copy-start | bytes 1572868
  12.4 8.0 %copy-start.4 = (s32[1024,2]{0,1:T(2,128)S(1)}, s32[1024,2]{0,1:T(2,128)}, u32[]{:S(2)}) copy-start(s32[1024,2]{0,1:T(2,128)} %param.15) | copy-start | bytes 24580
  12.4 8.0 %copy-start.6 = (s32[64]{0:T(128)S(1)}, s32[64]{0:T(128)}, u32[]{:S(2)}) copy-start(s32[64]{0:T(128)} %band.2) | copy-start | bytes 772
  13.5 11.1 %collective-permute-start.4 = (s16[208,256]{1,0:T(8,128)(2,1)S(1)}, s16[208,256]{1,0:T(8,128)(2,1)S(1)}, u32[]{:S(2)}, u32[]{:S(2)}) collective-permute-start(s16[208,256]{1,0:T(8,128)(2,1)S(1)} %get-tuple-element.28), channel_id=1, source_target_pairs={{0,4},{4,8},{8,12},{12,0},{1,5},{5,9},{9,13},{13,1},{2,6},{6,10},{... | collective-permute-start | bytes 319496 | tf_op jit(solution)/shard_map/ppermute | solution.py:725
  17.9 8.4 %collective-permute-start.5 = (s16[208,256]{1,0:T(8,128)(2,1)S(1)}, s16[208,256]{1,0:T(8,128)(2,1)S(1)}, u32[]{:S(2)}, u32[]{:S(2)}) collective-permute-start(s16[208,256]{1,0:T(8,128)(2,1)S(1)} %get-tuple-element.29), channel_id=1, source_target_pairs={{0,8},{4,12},{8,0},{12,4},{1,9},{5,13},{9,1},{13,5},{2,10},{6,14},... | collective-permute-start | bytes 319496 | tf_op jit(solution)/shard_map/ppermute | solution.py:725
  17.9 23.6 %copy-start.5 = (s32[64]{0:T(128)S(1)}, s32[64]{0:T(128)}, u32[]{:S(2)}) copy-start(s32[64]{0:T(128)} %band.3) | copy-start | bytes 772
  17.9 8.4 %collective-permute-start.6 = (s16[208,256]{1,0:T(8,128)(2,1)S(1)}, s16[208,256]{1,0:T(8,128)(2,1)S(1)}, u32[]{:S(2)}, u32[]{:S(2)}) collective-permute-start(s16[208,256]{1,0:T(8,128)(2,1)S(1)} %get-tuple-element.30), channel_id=1, source_target_pairs={{0,12},{4,0},{8,4},{12,8},{1,13},{5,1},{9,5},{13,9},{2,14},{6,2},{... | collective-permute-start | bytes 319496 | tf_op jit(solution)/shard_map/ppermute | solution.py:725
  26.7 6.3 %collective-permute-start.9 = (s16[224,256]{1,0:T(8,128)(2,1)S(1)}, s16[224,256]{1,0:T(8,128)(2,1)S(1)}, u32[]{:S(2)}, u32[]{:S(2)}) collective-permute-start(s16[224,256]{1,0:T(8,128)(2,1)S(1)} %total.1.rest_0_), channel_id=1, source_target_pairs={{0,12},{4,0},{8,4},{12,8},{1,13},{5,1},{9,5},{13,9},{2,14},{6,2},{... | collective-permute-start | bytes 344072 | tf_op jit(solution)/shard_map/ppermute | solution.py:725
  29.3 12.3 %collective-permute-start.8 = (s16[224,256]{1,0:T(8,128)(2,1)S(1)}, s16[224,256]{1,0:T(8,128)(2,1)S(1)}, u32[]{:S(2)}, u32[]{:S(2)}) collective-permute-start(s16[224,256]{1,0:T(8,128)(2,1)S(1)} %total.1.rest_0_), channel_id=1, source_target_pairs={{0,8},{4,12},{8,0},{12,4},{1,9},{5,13},{9,1},{13,5},{2,10},{6,14},... | collective-permute-start | bytes 344072 | tf_op jit(solution)/shard_map/ppermute | solution.py:725
  31.1 10.5 %collective-permute-start.7 = (s16[224,256]{1,0:T(8,128)(2,1)S(1)}, s16[224,256]{1,0:T(8,128)(2,1)S(1)}, u32[]{:S(2)}, u32[]{:S(2)}) collective-permute-start(s16[224,256]{1,0:T(8,128)(2,1)S(1)} %total.1.rest_0_), channel_id=1, source_target_pairs={{0,4},{4,8},{8,12},{12,0},{1,5},{5,9},{9,13},{13,1},{2,6},{6,10},{... | collective-permute-start | bytes 344072 | tf_op jit(solution)/shard_map/ppermute | solution.py:725

commit v5 on v4

--- a/solution.py
+++ b/solution.py
@@ -201,6 +201,19 @@
     return lax.ppermute(value, axes, pairs)
 
 
+DIAG = TILE // 2
+RING = (0, 2, 3, 1)
+NEAR = DIAG + BMAX * TILE
+
+
+def quarter_at(step, first, parts):
+    return jnp.bitwise_xor(step, first)
+
+
+def tail_rows(parts):
+    return TILE // parts
+
+
 def standard(values, mean, scale, block):
     row = jnp.clip(block, 0, mean.shape[0] - 1)
     m = mean[pl.ds(row, 1), :]
@@ -238,7 +251,11 @@
     normed[:, cols:] = jnp.zeros((samples, LANE), jnp.bfloat16)
     settle(0)
     rows = (BMAX + 1) * TILE
+    tail = tail_rows(parts)
     low = low_lanes((rows, LANE))
+    sub = lax.broadcasted_iota(jnp.int32, (TILE, LANE), 0)
+    lane = lax.broadcasted_iota(jnp.int32, (TILE, LANE), 1)
+    spot = lax.broadcasted_iota(jnp.int32, (tail, LANE), 0)
 
     def step(g, _):
         @pl.when(g < parts - 1)
@@ -258,13 +275,27 @@
                     full[b * LANE + TILE : b * LANE + TILE + rows, cut],
                 )
             )
+        folded = [
+            jnp.where(sub <= lane, p[:TILE], pltpu.roll(p[:TILE], TILE, axis=1)) for p in pieces
+        ]
+        folded = jnp.where(lane < TILE, folded[0], pltpu.roll(folded[1], TILE, axis=1))
+        diagonals = [
+            jnp.sum(jnp.where(sub == lane - TILE, p[:TILE], 0.0), axis=0, keepdims=True)
+            for p in pieces
+        ]
+        ends = jnp.where(spot == 0, diagonals[0], jnp.where(spot == 1, diagonals[1], 0.0))
+        slot = quarter_at(quarter_of(g), first, parts)
         for i in range(parts):
 
-            @pl.when(g == i)
+            @pl.when(slot == i)
             def _(i=i):
+                send = encode if rot and i > 0 else (lambda v: v)
                 for b in range(blocks):
                     cut = slice(b * LANE, (b + 1) * LANE)
-                    outs[i][:, cut] = encode(pieces[b]) if rot and i > 0 else pieces[b]
+                    outs[i][:DIAG, cut] = send(folded[b * DIAG : (b + 1) * DIAG])
+                    outs[i][DIAG:NEAR, cut] = send(pieces[b][TILE:])
+                outs[i][NEAR:, :LANE] = jnp.zeros((tail, LANE), outs[i].dtype)
+                outs[i][NEAR:, LANE:] = send(ends)
 
         return 0
 
@@ -274,7 +305,7 @@
 def gram_parts(dosage, mean, scale, rot, inv):
     samples, cols = dosage.shape
     parts = cols // QW
-    rows = (BMAX + 1) * TILE
+    rows = NEAR + tail_rows(parts)
     kinds = [jnp.float32] + [jnp.int16 if rot else jnp.float32] * (parts - 1)
     return pl.pallas_call(
         functools.partial(gram_kernel, parts, rot, inv),
@@ -295,10 +326,9 @@
 
 
 def cross_kernel(parts, rot, inv, cols, sent_e, sent_o, got_e, got_o, mean, scale, *rest):
-    ins, outs, cross = rest[:parts], rest[parts : 2 * parts], rest[-1]
+    ins, outs, (zero, one) = rest[:parts], rest[parts : 2 * parts], rest[-2:]
     blocks = QW // LANE
-    rows = (BMAX + 1) * TILE
-    share = LANE // parts // blocks
+    tail = tail_rows(parts)
     place = line_index(("snp", "pair"))
     base = place * (cols // LANE)
     end = base + cols // LANE
@@ -309,39 +339,43 @@
     last = standard(pick(sent_e, sent_o), mean, scale, end - 1)
     head = standard(pick(sent_o, sent_e), mean, scale, base)
     ahead = inv * tdot(right, last)
-    cross[...] = inv * tdot(left, head)
+    behind = inv * tdot(left, head)
     low = low_lanes((TILE, LANE))
+    turned = pltpu.roll(behind[TILE:], TILE, axis=1)
+    zero[...] = jnp.where(low, behind[:TILE], turned)
+    one[...] = turned
     far = slice((blocks - 1) * LANE, blocks * LANE)
     first = lax.axis_index("smp") if rot else 0
     for i in range(parts):
         send = encode if rot and i > 0 else (lambda v: v)
         wide = (lambda v: v.astype(jnp.int32)) if rot and i > 0 else (lambda v: v)
-        outs[i][0:rows, :] = ins[i][...]
-        quarter = lax.rem(i + first, parts)
-        for b in range(blocks):
-            at = pl.multiple_of((quarter * blocks + b) * share, 8)
-            outs[i][rows : rows + share, b * LANE : (b + 1) * LANE] = send(
-                cross[pl.ds(at, share), :]
-            )
+        kind = outs[i].dtype
+        outs[i][:NEAR, :] = ins[i][:NEAR, :]
+        quarter = quarter_at(i, first, parts)
+        share = pl.ds(pl.multiple_of(quarter * tail, 8), tail)
+        outs[i][NEAR:, :LANE] = send(zero[share, :])
+        outs[i][NEAR:, LANE:] = jnp.where(
+            low_lanes((tail, LANE)), wide(send(one[share, :])), wide(ins[i][NEAR:, LANE:])
+        ).astype(kind)
 
         @pl.when(quarter == parts - 1)
-        def _(i=i, send=send, wide=wide):
-            old = wide(ins[i][TILE : 2 * TILE, far])
-            outs[i][TILE : 2 * TILE, far] = jnp.where(low, old, wide(send(ahead[:TILE]))).astype(
-                outs[i].dtype
-            )
-            outs[i][2 * TILE : rows, far] = send(jnp.where(low, ahead[:TILE], ahead[TILE:]))
+        def _(i=i, send=send, wide=wide, kind=kind):
+            next_one = slice(DIAG, DIAG + TILE)
+            outs[i][next_one, far] = jnp.where(
+                low, wide(ins[i][next_one, far]), wide(send(ahead[:TILE]))
+            ).astype(kind)
+            outs[i][DIAG + TILE : NEAR, far] = send(jnp.where(low, ahead[:TILE], ahead[TILE:]))
 
 
 def cross_parts(sent_e, sent_o, got_e, got_o, mean, scale, blocks, cols, rot, inv):
     parts = len(blocks)
-    height = (BMAX + 1) * TILE + LANE // parts // (QW // LANE)
+    height = NEAR + tail_rows(parts)
     return pl.pallas_call(
         functools.partial(cross_kernel, parts, rot, inv, cols),
         in_specs=[VMEM] * (6 + parts),
         out_specs=[VMEM] * parts,
         out_shape=[jax.ShapeDtypeStruct((height, QW), b.dtype) for b in blocks],
-        scratch_shapes=[pltpu.VMEM((LANE, LANE), jnp.float32)],
+        scratch_shapes=[pltpu.VMEM((TILE, LANE), jnp.float32)] * 2,
         compiler_params=params(12),
         name="cross",
     )(sent_e, sent_o, got_e, got_o, mean, scale, *blocks)
@@ -376,20 +410,31 @@
 def final_kernel(parts, rot, moments, tile_total, band, w, *rest):
     ring = rest[:parts]
     moms = rest[parts : parts + moments]
-    out, imputed, held = rest[parts + moments :]
+    out_far, imputed_far, held, out, imputed, sem = rest[parts + moments :]
     blocks = QW // LANE
-    rows = (BMAX + 1) * TILE
+    tail = tail_rows(parts)
+    height = NEAR + tail
     low = low_lanes((TILE, LANE))
-    share = LANE // parts // blocks
-    height = rows + share
+    sub = lax.broadcasted_iota(jnp.int32, (TILE, LANE), 0)
+    lane = lax.broadcasted_iota(jnp.int32, (TILE, LANE), 1)
     cols = out.shape[1]
     first_tile = line_index(("snp", "pair")) * (cols // TILE)
+    copies = []
+
+    def ship(source, target):
+        copy = pltpu.make_async_copy(source, target, sem.at[len(copies)])
+        copy.start()
+        copies.append(copy)
+
+    def swap(value):
+        return pltpu.roll(value, TILE, axis=1)
+
     if rot:
         k = lax.axis_index("smp")
         total = None
-        for by in range(parts):
-            held[lax.rem(k - by + parts, parts)] = decode(ring[by][0:height, :])
-            code = from_code(ring[by][height : height + 16, :])
+        for piece, by in zip(ring, RING):
+            held[quarter_at(by, k, parts)] = decode(piece[0:height, :])
+            code = from_code(piece[height : height + 16, :])
             lanes = code.shape[1] // 2
             mom = decode_exact(code[:8, :lanes], code[8:, :lanes], code[:8, lanes:])
             total = mom if total is None else total + mom
@@ -398,45 +443,70 @@
             held[by] = ring[by][...]
         total = moms[0][...]
     solve(w, total, imputed)
-    for a in range(parts * blocks):
-        quarter, b = a // blocks, a % blocks
-        cut = slice(b * LANE, (b + 1) * LANE)
-        cols_here = slice(a * LANE, (a + 1) * LANE)
-        masks = mask_rows(band, first_tile + 2 * a, tile_total)
-        for q in range(BMAX + 1):
-            out[(BMAX + q) * TILE : (BMAX + q + 1) * TILE, cols_here] = (
-                held[quarter, q * TILE : (q + 1) * TILE, cut] * masks[BMAX + q]
+    ship(imputed, imputed_far)
+    for quarter in range(parts):
+        fold = jnp.concatenate(
+            [held[quarter, :DIAG, b * LANE : (b + 1) * LANE] for b in range(blocks)], axis=0
+        )
+        mirror = jnp.concatenate([fold, swap(fold)], axis=0).T[:TILE]
+        for b in range(blocks):
+            a = quarter * blocks + b
+            cut = slice(b * LANE, (b + 1) * LANE)
+            cols_here = slice(a * LANE, (a + 1) * LANE)
+            masks = mask_rows(band, first_tile + 2 * a, tile_total)
+            here, there = (fold, mirror) if b == 0 else (swap(fold), swap(mirror))
+            second = jnp.where(
+                sub == lane - TILE,
+                held[quarter, NEAR + b : NEAR + b + 1, LANE : 2 * LANE],
+                swap(jnp.where(lane < sub, here, there)),
             )
-        turned = held[quarter, TILE : 3 * TILE, cut].T
-        rolled = pltpu.roll(turned, TILE, axis=1)
-        if a == 0:
-            cross = jnp.concatenate(
-                [
-                    held[j // blocks, rows:height, (j % blocks) * LANE : (j % blocks + 1) * LANE]
-                    for j in range(LANE // share)
-                ],
-                axis=0,
-            )
-            one_low, two_low, two_high = cross[TILE:], cross[:TILE], cross[TILE:]
-        else:
-            one_low, two_low, two_high = last_turned[TILE:], last_rolled[:TILE], last_turned[TILE:]
-        out[TILE : 2 * TILE, cols_here] = jnp.where(low, one_low, rolled[:TILE]) * masks[1]
-        out[0:TILE, cols_here] = jnp.where(low, two_low, two_high) * masks[0]
-        last_turned, last_rolled = turned, rolled
+            centre = jnp.where(low, jnp.where(sub <= lane, here, there), second)
+            out[BMAX * TILE : (BMAX + 1) * TILE, cols_here] = centre * masks[BMAX]
+            for q in range(1, BMAX + 1):
+                out[(BMAX + q) * TILE : (BMAX + q + 1) * TILE, cols_here] = (
+                    held[quarter, DIAG + (q - 1) * TILE : DIAG + q * TILE, cut] * masks[BMAX + q]
+                )
+            turned = held[quarter, DIAG:NEAR, cut].T
+            rolled = swap(turned)
+            if a == 0:
+                cross = [
+                    jnp.concatenate(
+                        [held[j, NEAR:height, c * LANE : (c + 1) * LANE] for j in range(parts)],
+                        axis=0,
+                    )
+                    for c in range(2)
+                ]
+                one_low, two_low, two_high = swap(cross[0]), cross[0], swap(cross[1])
+            else:
+                one_low, two_low, two_high = (
+                    last_turned[TILE:], last_rolled[:TILE], last_turned[TILE:]
+                )
+            out[TILE : 2 * TILE, cols_here] = jnp.where(low, one_low, rolled[:TILE]) * masks[1]
+            out[0:TILE, cols_here] = jnp.where(low, two_low, two_high) * masks[0]
+            last_turned, last_rolled = turned, rolled
+        block = slice(quarter * QW, (quarter + 1) * QW)
+        ship(out.at[:, block], out_far.at[:, block])
+    for copy in copies:
+        copy.wait()
 
 
 def final(ring, moms, w, band_next, cols, rot):
     parts = len(ring)
-    height = (BMAX + 1) * TILE + LANE // parts // (QW // LANE)
+    shapes = [
+        jax.ShapeDtypeStruct((SPAN * TILE, cols), jnp.float32),
+        jax.ShapeDtypeStruct(w.shape[1:], jnp.float32),
+    ]
     return pl.pallas_call(
         functools.partial(final_kernel, parts, rot, len(moms), band_next.shape[0]),
         in_specs=[SMEM] + [VMEM] * (1 + parts + len(moms)),
-        out_specs=[VMEM, VMEM],
-        out_shape=[
-            jax.ShapeDtypeStruct((SPAN * TILE, cols), jnp.float32),
-            jax.ShapeDtypeStruct(w.shape[1:], jnp.float32),
+        out_specs=[pl.BlockSpec(memory_space=pltpu.HBM)] * 2,
+        out_shape=shapes,
+        scratch_shapes=[
+            pltpu.VMEM((parts, NEAR + tail_rows(parts), QW), jnp.float32),
+            pltpu.VMEM(shapes[0].shape, jnp.float32),
+            pltpu.VMEM(shapes[1].shape, jnp.float32),
+            pltpu.SemaphoreType.DMA((parts + 1,)),
         ],
-        scratch_shapes=[pltpu.VMEM((parts, height, QW), jnp.float32)],
         compiler_params=params(16),
         name="final",
     )(band_next, w, *ring, *moms)
@@ -713,7 +783,7 @@
         got_o, got_e = halos(zscores, ldt, obs, "smp")
 
     parts = cols // QW
-    rot = parts == n_smp and zscores.shape[1] == LANE
+    rot = parts == n_smp == 4 and zscores.shape[1] == LANE
     inv = 1.0 / (samples if rot else samples * n_smp)
     mean = allele_mean.reshape(-1, LANE)
     scale = snp_scale.reshape(-1, LANE)
@@ -721,14 +791,14 @@
     blocks = cross_parts(sent[0], sent[1], dos_e, dos_o, mean, scale, blocks, cols, rot, inv)
     if rot:
 
-        def cycle(value, by):
-            return lax.ppermute(value, "smp", [(i, (i + by) % n_smp) for i in range(n_smp)])
-
-        got = [cycle(blocks[by], by) for by in range(1, n_smp)]
+        def swap(value, by):
+            return lax.ppermute(value, "smp", [(i, i ^ by) for i in range(n_smp)])
+
+        got = [swap(blocks[by], by) for by in (1, 3, 2)]
     w, mom = krylov(ldt, zscores, obs, got_e, got_o, band_prev, paired)
     if rot:
         mine = total_of(blocks[0], got, mom)
-        ring = [mine] + [cycle(mine, by) for by in range(1, n_smp)]
+        ring = [swap(mine, by) if by else mine for by in RING]
         moms = []
     else:
         ring = list(lax.psum(tuple(blocks), "smp"))

time: 44.1 us -> 45 us (1.020)
  waiting for transfers between devices: 12.2 us -> 14.1 us
  starting transfers between devices: 15.8 us -> 14.1 us
  Pallas kernels: 15.1 us -> 15.8 us
    ppermute x6, waiting for transfers between devices: 12.2 us -> 14.1 us  [swap(): return lax.ppermute(value, 'smp', [(i, i ^ by) for i in range(n_smp)])]
    ppermute x6, starting transfers between devices: 11.2 us -> 9.53 us  [swap(): return lax.ppermute(value, 'smp', [(i, i ^ by) for i in range(n_smp)])]
  transfers between devices with their start and end apart: 10 -> 10, of which waited for: 3 -> 5; matrix products, arithmetic and copies ran while one was open for 0% -> 0% of each run, Pallas kernels for 24% -> 25%
where the time goes in v5:
time: 45 us; the launch traced here: 44.8 us
  Pallas kernels  15.8 us (35%)
  starting transfers between devices  14.1 us (31%)
  waiting for transfers between devices  14.1 us (31%)
  between operations  0.81 us (2%)
    ppermute x6, waiting for transfers between devices, swap(): return lax.ppermute(value, 'smp', [(i, i ^ by) for i in range(n_smp)])  14.1 us
    ppermute x6, starting transfers between devices, swap(): return lax.ppermute(value, 'smp', [(i, i ^ by) for i in range(n_smp)])  9.53 us
    pallas_call x1, Pallas kernels, gram_parts(): pl.pallas_call(functools.partial(gram_kernel, parts, rot, inv), in_specs=...  5.76 us
    pallas_call x1, Pallas kernels, krylov(): pl.pallas_call(functools.partial(krylov_kernel, band_prev.shape[0], sb, p...  4.21 us
    ppermute x3, starting transfers between devices, exchange(): return lax.ppermute(value, axes, pairs)  4 us
    pallas_call x1, Pallas kernels, final(): pl.pallas_call(functools.partial(final_kernel, parts, rot, len(moms), ban...  2.69 us
    pallas_call x1, Pallas kernels, pack(): pl.pallas_call(pack_kernel, in_specs=[far] * 4, out_specs=[VMEM] * len(sh...  1.7 us
    pallas_call x1, Pallas kernels, cross_parts(): pl.pallas_call(functools.partial(cross_kernel, parts, rot, inv, cols), in...  1.11 us
  transfers between devices with their start and end apart: 10, of which 5 were waited for; matrix products, arithmetic and copies ran while one was open for 0% of the time, Pallas kernels for 25%

profile of v5, /device:TPU:0, one launch (start us, length us, event | category | flops | bytes accessed | tf_op | source)
XLA Modules:
  0.0 44.8 jit_solution(14925913200161405087)
XLA Ops:
  0.6 0.0 copy-start.2
  0.6 0.0 copy-start.3
  0.6 1.7 %pack.1 = (bf16[2048,128]{1,0:T(8,128)(2,1)S(1)}, bf16[2048,128]{1,0:T(8,128)(2,1)S(1)}, s16[1040,128]{1,0:T(8,128)(2,1)S(1)}, s16[1040,128]{1,0:T(8,128)(2,1)S(1)}) custom-call(bf16[2048,1024]{1,0:T(8,128)(2,1)} %dos.3, f32[1024,128]{1,0:T(8,128)} %z.3, f32[320,1024]{1,0:T(8,128)} %bitcast.5, s32[2,1024]{1,0:T(2,128)} %bitcast.11), custom_call_target="tpu_custom_call" | custom-call | tf_op jit(solution)/shard_map/pack/pallas_call | solution.py:181
  2.4 0.6 %collective-permute-start.2 = (bf16[2048,128]{1,0:T(8,128)(2,1)S(1)}, bf16[2048,128]{1,0:T(8,128)(2,1)S(1)}, u32[]{:S(2)}, u32[]{:S(2)}) collective-permute-start(bf16[2048,128]{1,0:T(8,128)(2,1)S(1)} %get-tuple-element.21.sent_e), channel_id=1, source_target_pairs={{0,1},{1,0},{2,3},{3,2},{4,5},{5,4},{6,7},{7,6},{8,9},{9,8},{10,11... | collective-permute-start | bytes 1572872 | tf_op jit(solution)/shard_map/ppermute | solution.py:197
  2.9 0.7 %collective-permute-start.3 = (bf16[2048,128]{1,0:T(8,128)(2,1)S(1)}, bf16[2048,128]{1,0:T(8,128)(2,1)S(1)}, u32[]{:S(2)}, u32[]{:S(2)}) collective-permute-start(bf16[2048,128]{1,0:T(8,128)(2,1)S(1)} %get-tuple-element.22.sent_o), channel_id=1, source_target_pairs={{1,2},{2,1},{5,6},{6,5},{9,10},{10,9},{13,14},{14,13},{17,18},{18,... | collective-permute-start | bytes 1572872 | tf_op jit(solution)/shard_map/ppermute | solution.py:201
  3.6 2.6 %collective-permute-start = (s16[1040,128]{1,0:T(8,128)(2,1)S(1)}, s16[1040,128]{1,0:T(8,128)(2,1)S(1)}, u32[]{:S(2)}, u32[]{:S(2)}) collective-permute-start(s16[1040,128]{1,0:T(8,128)(2,1)S(1)} %get-tuple-element.18), channel_id=1, source_target_pairs={{0,4},{4,0},{8,12},{12,8},{1,5},{5,1},{9,13},{13,9},{2,6},{6,2},{1... | collective-permute-start | bytes 798728 | tf_op jit(solution)/shard_map/ppermute | solution.py:201
  6.3 0.7 %collective-permute-start.1 = (s16[1040,128]{1,0:T(8,128)(2,1)S(1)}, s16[1040,128]{1,0:T(8,128)(2,1)S(1)}, u32[]{:S(2)}, u32[]{:S(2)}) collective-permute-start(s16[1040,128]{1,0:T(8,128)(2,1)S(1)} %get-tuple-element.19), channel_id=1, source_target_pairs={{4,8},{8,4},{5,9},{9,5},{6,10},{10,6},{7,11},{11,7},{20,24},{24,20... | collective-permute-start | bytes 798728 | tf_op jit(solution)/shard_map/ppermute | solution.py:201
  6.9 0.0 copy-done.2
  6.9 0.0 copy-done.3
  7.0 5.8 %gram.1 = (f32[176,256]{1,0:T(8,128)S(1)}, s16[176,256]{1,0:T(8,128)(2,1)S(1)}, s16[176,256]{1,0:T(8,128)(2,1)S(1)}, s16[176,256]{1,0:T(8,128)(2,1)S(1)}) custom-call(bf16[2048,1024]{1,0:T(8,128)(2,1)} %dos.3, f32[32,128]{1,0:T(8,128)S(1)} %bitcast.7, f32[32,128]{1,0:T(8,128)S(1)} %bitcast.9), custom_call_target="tpu_custom_call" | custom-call | flops 1610612736 | bytes 8388608 | tf_op jit(solution)/shard_map/gram/pallas_call | solution.py:310
  12.7 0.0 copy-start
  12.7 0.0 copy-start.1
  12.7 0.0 copy-start.4
  12.8 0.0 copy-start.6
  12.8 0.0 collective-permute-done.2.got_e
  12.8 0.0 collective-permute-done.3.got_o
  12.8 1.1 %cross.1 = (f32[176,256]{1,0:T(8,128)S(1)}, s16[176,256]{1,0:T(8,128)(2,1)S(1)}, s16[176,256]{1,0:T(8,128)(2,1)S(1)}, s16[176,256]{1,0:T(8,128)(2,1)S(1)}) custom-call(bf16[2048,128]{1,0:T(8,128)(2,1)S(1)} %get-tuple-element.21.sent_e, bf16[2048,128]{1,0:T(8,128)(2,1)S(1)} %get-tuple-element.22.sent_o, bf16[2048,128]{1,0:T(8,128)(2,1)S(1)} %collective-permute-done.2.got_e, ...), custom_call_target="tpu_custom_call" | custom-call | tf_op jit(solution)/shard_map/cross/pallas_call | solution.py:373
  13.9 4.4 %collective-permute-start.4 = (s16[176,256]{1,0:T(8,128)(2,1)S(1)}, s16[176,256]{1,0:T(8,128)(2,1)S(1)}, u32[]{:S(2)}, u32[]{:S(2)}) collective-permute-start(s16[176,256]{1,0:T(8,128)(2,1)S(1)} %get-tuple-element.28), channel_id=1, source_target_pairs={{0,4},{4,0},{8,12},{12,8},{1,5},{5,1},{9,13},{13,9},{2,6},{6,2},{1... | collective-permute-start | bytes 270344 | tf_op jit(solution)/shard_map/ppermute | solution.py:795
  18.4 0.9 %collective-permute-start.5 = (s16[176,256]{1,0:T(8,128)(2,1)S(1)}, s16[176,256]{1,0:T(8,128)(2,1)S(1)}, u32[]{:S(2)}, u32[]{:S(2)}) collective-permute-start(s16[176,256]{1,0:T(8,128)(2,1)S(1)} %get-tuple-element.29), channel_id=1, source_target_pairs={{0,12},{4,8},{8,4},{12,0},{1,13},{5,9},{9,5},{13,1},{2,14},{6,10},... | collective-permute-start | bytes 270344 | tf_op jit(solution)/shard_map/ppermute | solution.py:795
  19.3 0.0 copy-start.5
  19.3 0.6 %collective-permute-start.6 = (s16[176,256]{1,0:T(8,128)(2,1)S(1)}, s16[176,256]{1,0:T(8,128)(2,1)S(1)}, u32[]{:S(2)}, u32[]{:S(2)}) collective-permute-start(s16[176,256]{1,0:T(8,128)(2,1)S(1)} %get-tuple-element.30), channel_id=1, source_target_pairs={{0,8},{4,12},{8,0},{12,4},{1,9},{5,13},{9,1},{13,5},{2,10},{6,14},... | collective-permute-start | bytes 270344 | tf_op jit(solution)/shard_map/ppermute | solution.py:795
  19.9 0.0 collective-permute-done.got_e
  19.9 0.0 collective-permute-done.1.got_o
  19.9 0.0 copy-done
  19.9 0.0 copy-done.1
  19.9 0.0 copy-done.4
  19.9 0.0 copy-done.6
  19.9 4.2 %krylov.1 = (f32[3,1024,128]{2,1,0:T(8,128)S(1)}, f32[8,128]{1,0:T(8,128)S(1)}) custom-call(s32[64]{0:T(128)S(1)} %copy-done.6, f32[320,1024]{1,0:T(8,128)S(1)} %bitcast.6, f32[1024,128]{1,0:T(8,128)S(1)} %copy-done.1, s32[2,1024]{1,0:T(2,128)S(1)} %bitcast.12, s16[1040,128]{1,0:T(8,128)(2,1)S(1)} %collective-permute-done.got_e, ...), custom_call_target="tpu_custom_call" | custom-call | flops 1321205760 | bytes 1310720 | tf_op jit(solution)/shard_map/krylov/pallas_call | solution.py:683
  24.2 0.0 collective-permute-done.4.rest_0_
  24.2 0.6 %collective-permute-done.5.rest_1_ = s16[176,256]{1,0:T(8,128)(2,1)S(1)} collective-permute-done((s16[176,256]{1,0:T(8,128)(2,1)S(1)}, s16[176,256]{1,0:T(8,128)(2,1)S(1)}, u32[]{:S(2)}, u32[]{:S(2)}) %collective-permute-start.5) | collective-permute-done | bytes 90144 | tf_op jit(solution)/shard_map/ppermute | solution.py:795
  24.8 4.6 %collective-permute-done.6.rest_2_ = s16[176,256]{1,0:T(8,128)(2,1)S(1)} collective-permute-done((s16[176,256]{1,0:T(8,128)(2,1)S(1)}, s16[176,256]{1,0:T(8,128)(2,1)S(1)}, u32[]{:S(2)}, u32[]{:S(2)}) %collective-permute-start.6) | collective-permute-done | bytes 90144 | tf_op jit(solution)/shard_map/ppermute | solution.py:795
  29.4 0.3 total.1.rest_0_
  29.7 0.1 collective-permute-start.9
  29.8 1.8 %collective-permute-start.8 = (s16[192,256]{1,0:T(8,128)(2,1)S(1)}, s16[192,256]{1,0:T(8,128)(2,1)S(1)}, u32[]{:S(2)}, u32[]{:S(2)}) collective-permute-start(s16[192,256]{1,0:T(8,128)(2,1)S(1)} %total.1.rest_0_), channel_id=1, source_target_pairs={{0,12},{4,8},{8,4},{12,0},{1,13},{5,9},{9,5},{13,1},{2,14},{6,10},... | collective-permute-start | bytes 294920 | tf_op jit(solution)/shard_map/ppermute | solution.py:795
  31.6 1.7 %collective-permute-start.7 = (s16[192,256]{1,0:T(8,128)(2,1)S(1)}, s16[192,256]{1,0:T(8,128)(2,1)S(1)}, u32[]{:S(2)}, u32[]{:S(2)}) collective-permute-start(s16[192,256]{1,0:T(8,128)(2,1)S(1)} %total.1.rest_0_), channel_id=1, source_target_pairs={{0,8},{4,12},{8,0},{12,4},{1,9},{5,13},{9,1},{13,5},{2,10},{6,14},... | collective-permute-start | bytes 294920 | tf_op jit(solution)/shard_map/ppermute | solution.py:795
  33.3 1.6 %collective-permute-done.9.rest_3_ = s16[192,256]{1,0:T(8,128)(2,1)S(1)} collective-permute-done((s16[192,256]{1,0:T(8,128)(2,1)S(1)}, s16[192,256]{1,0:T(8,128)(2,1)S(1)}, u32[]{:S(2)}, u32[]{:S(2)}) %collective-permute-start.9) | collective-permute-done | bytes 98336 | tf_op jit(solution)/shard_map/ppermute | solution.py:795
  34.8 2.6 %collective-permute-done.8.rest_2_ = s16[192,256]{1,0:T(8,128)(2,1)S(1)} collective-permute-done((s16[192,256]{1,0:T(8,128)(2,1)S(1)}, s16[192,256]{1,0:T(8,128)(2,1)S(1)}, u32[]{:S(2)}, u32[]{:S(2)}) %collective-permute-start.8) | collective-permute-done | bytes 98336 | tf_op jit(solution)/shard_map/ppermute | solution.py:795
  37.5 4.7 %collective-permute-done.7.rest_1_ = s16[192,256]{1,0:T(8,128)(2,1)S(1)} collective-permute-done((s16[192,256]{1,0:T(8,128)(2,1)S(1)}, s16[192,256]{1,0:T(8,128)(2,1)S(1)}, u32[]{:S(2)}, u32[]{:S(2)}) %collective-permute-start.7) | collective-permute-done | bytes 98336 | tf_op jit(solution)/shard_map/ppermute | solution.py:795
  42.1 0.0 copy-done.5
  42.1 2.7 %final.1 = (f32[320,1024]{1,0:T(8,128)}, f32[1024,128]{1,0:T(8,128)}) custom-call(s32[64]{0:T(128)S(1)} %copy-done.5, f32[3,1024,128]{2,1,0:T(8,128)S(1)} %get-tuple-element.20.w, s16[192,256]{1,0:T(8,128)(2,1)S(1)} %total.1.rest_0_, s16[192,256]{1,0:T(8,128)(2,1)S(1)} %collective-permute-done.7.rest_1_, s16[192,256]{1,0:T(8,128)(2,1)S(1)} %collective-permute-done.8.rest_2_, ...), custom_call_target="tpu_custom_call" | custom-call | tf_op jit(solution)/shard_map/final/pallas_call | solution.py:499
Async XLA Ops:
  0.6 6.3 %copy-start.2 = (f32[4096]{0:T(1024)S(1)}, f32[4096]{0:T(1024)}, u32[]{:S(2)}) copy-start(f32[4096]{0:T(1024)} %param.9) | copy-start | bytes 49156
  0.6 6.3 %copy-start.3 = (f32[4096]{0:T(1024)S(1)}, f32[4096]{0:T(1024)}, u32[]{:S(2)}) copy-start(f32[4096]{0:T(1024)} %param.10) | copy-start | bytes 49156
  2.4 10.4 %collective-permute-start.2 = (bf16[2048,128]{1,0:T(8,128)(2,1)S(1)}, bf16[2048,128]{1,0:T(8,128)(2,1)S(1)}, u32[]{:S(2)}, u32[]{:S(2)}) collective-permute-start(bf16[2048,128]{1,0:T(8,128)(2,1)S(1)} %get-tuple-element.21.sent_e), channel_id=1, source_target_pairs={{0,1},{1,0},{2,3},{3,2},{4,5},{5,4},{6,7},{7,6},{8,9},{9,8},{10,11... | collective-permute-start | bytes 1572872 | tf_op jit(solution)/shard_map/ppermute | solution.py:197
  2.9 9.9 %collective-permute-start.3 = (bf16[2048,128]{1,0:T(8,128)(2,1)S(1)}, bf16[2048,128]{1,0:T(8,128)(2,1)S(1)}, u32[]{:S(2)}, u32[]{:S(2)}) collective-permute-start(bf16[2048,128]{1,0:T(8,128)(2,1)S(1)} %get-tuple-element.22.sent_o), channel_id=1, source_target_pairs={{1,2},{2,1},{5,6},{6,5},{9,10},{10,9},{13,14},{14,13},{17,18},{18,... | collective-permute-start | bytes 1572872 | tf_op jit(solution)/shard_map/ppermute | solution.py:201
  3.6 16.3 %collective-permute-start = (s16[1040,128]{1,0:T(8,128)(2,1)S(1)}, s16[1040,128]{1,0:T(8,128)(2,1)S(1)}, u32[]{:S(2)}, u32[]{:S(2)}) collective-permute-start(s16[1040,128]{1,0:T(8,128)(2,1)S(1)} %get-tuple-element.18), channel_id=1, source_target_pairs={{0,4},{4,0},{8,12},{12,8},{1,5},{5,1},{9,13},{13,9},{2,6},{6,2},{1... | collective-permute-start | bytes 798728 | tf_op jit(solution)/shard_map/ppermute | solution.py:201
  6.3 13.6 %collective-permute-start.1 = (s16[1040,128]{1,0:T(8,128)(2,1)S(1)}, s16[1040,128]{1,0:T(8,128)(2,1)S(1)}, u32[]{:S(2)}, u32[]{:S(2)}) collective-permute-start(s16[1040,128]{1,0:T(8,128)(2,1)S(1)} %get-tuple-element.19), channel_id=1, source_target_pairs={{4,8},{8,4},{5,9},{9,5},{6,10},{10,6},{7,11},{11,7},{20,24},{24,20... | collective-permute-start | bytes 798728 | tf_op jit(solution)/shard_map/ppermute | solution.py:201
  12.7 7.2 %copy-start = (f32[1024,320]{0,1:T(8,128)S(1)}, f32[1024,320]{0,1:T(8,128)}, u32[]{:S(2)}) copy-start(f32[1024,320]{0,1:T(8,128)} %param.12) | copy-start | bytes 3932164
  12.7 7.2 %copy-start.1 = (f32[1024,128]{1,0:T(8,128)S(1)}, f32[1024,128]{1,0:T(8,128)}, u32[]{:S(2)}) copy-start(f32[1024,128]{1,0:T(8,128)} %z.3) | copy-start | bytes 1572868
  12.7 7.2 %copy-start.4 = (s32[1024,2]{0,1:T(2,128)S(1)}, s32[1024,2]{0,1:T(2,128)}, u32[]{:S(2)}) copy-start(s32[1024,2]{0,1:T(2,128)} %param.15) | copy-start | bytes 24580
  12.8 7.2 %copy-start.6 = (s32[64]{0:T(128)S(1)}, s32[64]{0:T(128)}, u32[]{:S(2)}) copy-start(s32[64]{0:T(128)} %band.2) | copy-start | bytes 772
  13.9 10.2 %collective-permute-start.4 = (s16[176,256]{1,0:T(8,128)(2,1)S(1)}, s16[176,256]{1,0:T(8,128)(2,1)S(1)}, u32[]{:S(2)}, u32[]{:S(2)}) collective-permute-start(s16[176,256]{1,0:T(8,128)(2,1)S(1)} %get-tuple-element.28), channel_id=1, source_target_pairs={{0,4},{4,0},{8,12},{12,8},{1,5},{5,1},{9,13},{13,9},{2,6},{6,2},{1... | collective-permute-start | bytes 270344 | tf_op jit(solution)/shard_map/ppermute | solution.py:795
  18.4 6.4 %collective-permute-start.5 = (s16[176,256]{1,0:T(8,128)(2,1)S(1)}, s16[176,256]{1,0:T(8,128)(2,1)S(1)}, u32[]{:S(2)}, u32[]{:S(2)}) collective-permute-start(s16[176,256]{1,0:T(8,128)(2,1)S(1)} %get-tuple-element.29), channel_id=1, source_target_pairs={{0,12},{4,8},{8,4},{12,0},{1,13},{5,9},{9,5},{13,1},{2,14},{6,10},... | collective-permute-start | bytes 270344 | tf_op jit(solution)/shard_map/ppermute | solution.py:795
  19.3 22.9 %copy-start.5 = (s32[64]{0:T(128)S(1)}, s32[64]{0:T(128)}, u32[]{:S(2)}) copy-start(s32[64]{0:T(128)} %band.3) | copy-start | bytes 772
  19.3 10.1 %collective-permute-start.6 = (s16[176,256]{1,0:T(8,128)(2,1)S(1)}, s16[176,256]{1,0:T(8,128)(2,1)S(1)}, u32[]{:S(2)}, u32[]{:S(2)}) collective-permute-start(s16[176,256]{1,0:T(8,128)(2,1)S(1)} %get-tuple-element.30), channel_id=1, source_target_pairs={{0,8},{4,12},{8,0},{12,4},{1,9},{5,13},{9,1},{13,5},{2,10},{6,14},... | collective-permute-start | bytes 270344 | tf_op jit(solution)/shard_map/ppermute | solution.py:795
  29.7 5.1 %collective-permute-start.9 = (s16[192,256]{1,0:T(8,128)(2,1)S(1)}, s16[192,256]{1,0:T(8,128)(2,1)S(1)}, u32[]{:S(2)}, u32[]{:S(2)}) collective-permute-start(s16[192,256]{1,0:T(8,128)(2,1)S(1)} %total.1.rest_0_), channel_id=1, source_target_pairs={{0,4},{4,0},{8,12},{12,8},{1,5},{5,1},{9,13},{13,9},{2,6},{6,2},{1... | collective-permute-start | bytes 294920 | tf_op jit(solution)/shard_map/ppermute | solution.py:795
  29.8 7.6 %collective-permute-start.8 = (s16[192,256]{1,0:T(8,128)(2,1)S(1)}, s16[192,256]{1,0:T(8,128)(2,1)S(1)}, u32[]{:S(2)}, u32[]{:S(2)}) collective-permute-start(s16[192,256]{1,0:T(8,128)(2,1)S(1)} %total.1.rest_0_), channel_id=1, source_target_pairs={{0,12},{4,8},{8,4},{12,0},{1,13},{5,9},{9,5},{13,1},{2,14},{6,10},... | collective-permute-start | bytes 294920 | tf_op jit(solution)/shard_map/ppermute | solution.py:795
  31.6 10.5 %collective-permute-start.7 = (s16[192,256]{1,0:T(8,128)(2,1)S(1)}, s16[192,256]{1,0:T(8,128)(2,1)S(1)}, u32[]{:S(2)}, u32[]{:S(2)}) collective-permute-start(s16[192,256]{1,0:T(8,128)(2,1)S(1)} %total.1.rest_0_), channel_id=1, source_target_pairs={{0,8},{4,12},{8,0},{12,4},{1,9},{5,13},{9,1},{13,5},{2,10},{6,14},... | collective-permute-start | bytes 294920 | tf_op jit(solution)/shard_map/ppermute | solution.py:795

commit v6 on v5

--- a/solution.py
+++ b/solution.py
@@ -325,7 +325,7 @@
     )(in_hbm(dosage), mean, scale)
 
 
-def cross_kernel(parts, rot, inv, cols, sent_e, sent_o, got_e, got_o, mean, scale, *rest):
+def cross_kernel(parts, rot, inv, cols, sent_e, sent_o, got_o, got_e, mean, scale, *rest):
     ins, outs, (zero, one) = rest[:parts], rest[parts : 2 * parts], rest[-2:]
     blocks = QW // LANE
     tail = tail_rows(parts)
@@ -378,7 +378,7 @@
         scratch_shapes=[pltpu.VMEM((TILE, LANE), jnp.float32)] * 2,
         compiler_params=params(12),
         name="cross",
-    )(sent_e, sent_o, got_e, got_o, mean, scale, *blocks)
+    )(sent_e, sent_o, got_o, got_e, mean, scale, *blocks)
 
 
 def total_kernel(count, own, *rest):
@@ -532,7 +532,7 @@
 
 
 def krylov_kernel(
-    tile_total, sb, paired, band, ldt, z, obs, got_e, got_o, w_out, mom_out,
+    tile_total, sb, paired, band, ldt, z, obs, got_o, got_e, w_out, mom_out,
     dh, dl, ucat, seen, u_prev, y
 ):
     rows = ldt.shape[1]
@@ -701,7 +701,7 @@
             flops=ITERS * 6 * ext * SPAN * TILE * traits, bytes_accessed=ldt.size * 4, transcendentals=0
         ),
         name="krylov",
-    )(band_prev, ldt, z, obs, got_e, got_o)
+    )(band_prev, ldt, z, obs, got_o, got_e)
 
 
 def solve(w, mom, out):
@@ -774,11 +774,11 @@
     paired = rows >= HZ
 
     sent = pack(dosage, zscores, ldt, obs, paired)
+    dos_o = exchange(sent[1], line, 1)
     dos_e = exchange(sent[0], line, 0)
-    dos_o = exchange(sent[1], line, 1)
     if paired:
+        got_o = exchange(sent[3], ("smp",), 1)
         got_e = exchange(sent[2], ("smp",), 0)
-        got_o = exchange(sent[3], ("smp",), 1)
     else:
         got_o, got_e = halos(zscores, ldt, obs, "smp")
 

time: 45 us -> 44.8 us (level)
  waiting for transfers between devices: 14.1 us -> 13.5 us
    ppermute x3, starting transfers between devices: 4 us -> 6.82 us  [exchange(): return lax.ppermute(value, axes, pairs)]
    ppermute x6, starting transfers between devices: 9.53 us -> 7.1 us  [swap(): return lax.ppermute(value, 'smp', [(i, i ^ by) for i in range(n_smp)])]
    ppermute x6, waiting for transfers between devices: 14.1 us -> 13.5 us  [swap(): return lax.ppermute(value, 'smp', [(i, i ^ by) for i in range(n_smp)])]
  transfers between devices with their start and end apart: 10 -> 10, of which waited for: 5 -> 4; matrix products, arithmetic and copies ran while one was open for 0% -> 0% of each run, Pallas kernels for 25% -> 25%
where the time goes in v6:
time: 44.8 us; the launch traced here: 44.6 us
  Pallas kernels  15.8 us (35%)
  starting transfers between devices  14.5 us (32%)
  waiting for transfers between devices  13.5 us (30%)
  between operations  0.8 us (2%)
    ppermute x6, waiting for transfers between devices, swap(): return lax.ppermute(value, 'smp', [(i, i ^ by) for i in range(n_smp)])  13.5 us
    ppermute x6, starting transfers between devices, swap(): return lax.ppermute(value, 'smp', [(i, i ^ by) for i in range(n_smp)])  7.1 us
    ppermute x3, starting transfers between devices, exchange(): return lax.ppermute(value, axes, pairs)  6.82 us
    pallas_call x1, Pallas kernels, gram_parts(): pl.pallas_call(functools.partial(gram_kernel, parts, rot, inv), in_specs=...  5.76 us
    pallas_call x1, Pallas kernels, krylov(): pl.pallas_call(functools.partial(krylov_kernel, band_prev.shape[0], sb, p...  4.21 us
    pallas_call x1, Pallas kernels, final(): pl.pallas_call(functools.partial(final_kernel, parts, rot, len(moms), ban...  2.69 us
    pallas_call x1, Pallas kernels, pack(): pl.pallas_call(pack_kernel, in_specs=[far] * 4, out_specs=[VMEM] * len(sh...  1.7 us
    pallas_call x1, Pallas kernels, cross_parts(): pl.pallas_call(functools.partial(cross_kernel, parts, rot, inv, cols), in...  1.11 us
  transfers between devices with their start and end apart: 10, of which 4 were waited for; matrix products, arithmetic and copies ran while one was open for 0% of the time, Pallas kernels for 25%

profile of v6, /device:TPU:0, one launch (start us, length us, event | category | flops | bytes accessed | tf_op | source)
XLA Modules:
  0.0 44.6 jit_solution(15136609311917298432)
XLA Ops:
  0.6 0.0 copy-start.2
  0.6 0.0 copy-start.3
  0.6 1.7 %pack.1 = (bf16[2048,128]{1,0:T(8,128)(2,1)S(1)}, bf16[2048,128]{1,0:T(8,128)(2,1)S(1)}, s16[1040,128]{1,0:T(8,128)(2,1)S(1)}, s16[1040,128]{1,0:T(8,128)(2,1)S(1)}) custom-call(bf16[2048,1024]{1,0:T(8,128)(2,1)} %dos.3, f32[1024,128]{1,0:T(8,128)} %z.3, f32[320,1024]{1,0:T(8,128)} %bitcast.5, s32[2,1024]{1,0:T(2,128)} %bitcast.11), custom_call_target="tpu_custom_call" | custom-call | tf_op jit(solution)/shard_map/pack/pallas_call | solution.py:181
  2.4 0.6 %collective-permute-start.3 = (bf16[2048,128]{1,0:T(8,128)(2,1)S(1)}, bf16[2048,128]{1,0:T(8,128)(2,1)S(1)}, u32[]{:S(2)}, u32[]{:S(2)}) collective-permute-start(bf16[2048,128]{1,0:T(8,128)(2,1)S(1)} %get-tuple-element.21.sent_e), channel_id=1, source_target_pairs={{0,1},{1,0},{2,3},{3,2},{4,5},{5,4},{6,7},{7,6},{8,9},{9,8},{10,11... | collective-permute-start | bytes 1572872 | tf_op jit(solution)/shard_map/ppermute | solution.py:197
  2.9 0.7 %collective-permute-start.2 = (bf16[2048,128]{1,0:T(8,128)(2,1)S(1)}, bf16[2048,128]{1,0:T(8,128)(2,1)S(1)}, u32[]{:S(2)}, u32[]{:S(2)}) collective-permute-start(bf16[2048,128]{1,0:T(8,128)(2,1)S(1)} %get-tuple-element.22.sent_o), channel_id=1, source_target_pairs={{1,2},{2,1},{5,6},{6,5},{9,10},{10,9},{13,14},{14,13},{17,18},{18,... | collective-permute-start | bytes 1572872 | tf_op jit(solution)/shard_map/ppermute | solution.py:201
  3.6 0.7 %collective-permute-start = (s16[1040,128]{1,0:T(8,128)(2,1)S(1)}, s16[1040,128]{1,0:T(8,128)(2,1)S(1)}, u32[]{:S(2)}, u32[]{:S(2)}) collective-permute-start(s16[1040,128]{1,0:T(8,128)(2,1)S(1)} %get-tuple-element.18), channel_id=1, source_target_pairs={{4,8},{8,4},{5,9},{9,5},{6,10},{10,6},{7,11},{11,7},{20,24},{24,20... | collective-permute-start | bytes 798728 | tf_op jit(solution)/shard_map/ppermute | solution.py:201
  4.3 5.5 %collective-permute-start.1 = (s16[1040,128]{1,0:T(8,128)(2,1)S(1)}, s16[1040,128]{1,0:T(8,128)(2,1)S(1)}, u32[]{:S(2)}, u32[]{:S(2)}) collective-permute-start(s16[1040,128]{1,0:T(8,128)(2,1)S(1)} %get-tuple-element.19), channel_id=1, source_target_pairs={{0,4},{4,0},{8,12},{12,8},{1,5},{5,1},{9,13},{13,9},{2,6},{6,2},{1... | collective-permute-start | bytes 798728 | tf_op jit(solution)/shard_map/ppermute | solution.py:201
  9.8 0.0 copy-done.2
  9.8 0.0 copy-done.3
  9.8 5.8 %gram.1 = (f32[176,256]{1,0:T(8,128)S(1)}, s16[176,256]{1,0:T(8,128)(2,1)S(1)}, s16[176,256]{1,0:T(8,128)(2,1)S(1)}, s16[176,256]{1,0:T(8,128)(2,1)S(1)}) custom-call(bf16[2048,1024]{1,0:T(8,128)(2,1)} %dos.3, f32[32,128]{1,0:T(8,128)S(1)} %bitcast.7, f32[32,128]{1,0:T(8,128)S(1)} %bitcast.9), custom_call_target="tpu_custom_call" | custom-call | flops 1610612736 | bytes 8388608 | tf_op jit(solution)/shard_map/gram/pallas_call | solution.py:310
  15.5 0.0 copy-start
  15.5 0.0 copy-start.1
  15.6 0.0 copy-start.4
  15.6 0.0 copy-start.6
  15.6 0.0 collective-permute-done.3.got_e
  15.6 0.0 collective-permute-done.2.got_o
  15.6 1.1 %cross.1 = (f32[176,256]{1,0:T(8,128)S(1)}, s16[176,256]{1,0:T(8,128)(2,1)S(1)}, s16[176,256]{1,0:T(8,128)(2,1)S(1)}, s16[176,256]{1,0:T(8,128)(2,1)S(1)}) custom-call(bf16[2048,128]{1,0:T(8,128)(2,1)S(1)} %get-tuple-element.21.sent_e, bf16[2048,128]{1,0:T(8,128)(2,1)S(1)} %get-tuple-element.22.sent_o, bf16[2048,128]{1,0:T(8,128)(2,1)S(1)} %collective-permute-done.2.got_o, ...), custom_call_target="tpu_custom_call" | custom-call | tf_op jit(solution)/shard_map/cross/pallas_call | solution.py:373
  16.7 0.1 collective-permute-start.4
  16.8 1.4 %collective-permute-start.5 = (s16[176,256]{1,0:T(8,128)(2,1)S(1)}, s16[176,256]{1,0:T(8,128)(2,1)S(1)}, u32[]{:S(2)}, u32[]{:S(2)}) collective-permute-start(s16[176,256]{1,0:T(8,128)(2,1)S(1)} %get-tuple-element.29), channel_id=1, source_target_pairs={{0,12},{4,8},{8,4},{12,0},{1,13},{5,9},{9,5},{13,1},{2,14},{6,10},... | collective-permute-start | bytes 270344 | tf_op jit(solution)/shard_map/ppermute | solution.py:795
  18.2 0.0 copy-start.5
  18.2 2.1 %collective-permute-start.6 = (s16[176,256]{1,0:T(8,128)(2,1)S(1)}, s16[176,256]{1,0:T(8,128)(2,1)S(1)}, u32[]{:S(2)}, u32[]{:S(2)}) collective-permute-start(s16[176,256]{1,0:T(8,128)(2,1)S(1)} %get-tuple-element.30), channel_id=1, source_target_pairs={{0,8},{4,12},{8,0},{12,4},{1,9},{5,13},{9,1},{13,5},{2,10},{6,14},... | collective-permute-start | bytes 270344 | tf_op jit(solution)/shard_map/ppermute | solution.py:795
  20.3 0.0 collective-permute-done.got_o
  20.3 0.0 collective-permute-done.1.got_e
  20.3 0.0 copy-done
  20.3 0.0 copy-done.1
  20.3 0.0 copy-done.4
  20.3 0.0 copy-done.6
  20.3 4.2 %krylov.1 = (f32[3,1024,128]{2,1,0:T(8,128)S(1)}, f32[8,128]{1,0:T(8,128)S(1)}) custom-call(s32[64]{0:T(128)S(1)} %copy-done.6, f32[320,1024]{1,0:T(8,128)S(1)} %bitcast.6, f32[1024,128]{1,0:T(8,128)S(1)} %copy-done.1, s32[2,1024]{1,0:T(2,128)S(1)} %bitcast.12, s16[1040,128]{1,0:T(8,128)(2,1)S(1)} %collective-permute-done.got_o, ...), custom_call_target="tpu_custom_call" | custom-call | flops 1321205760 | bytes 1310720 | tf_op jit(solution)/shard_map/krylov/pallas_call | solution.py:683
  24.5 0.0 collective-permute-done.4.rest_0_
  24.5 0.0 collective-permute-done.5.rest_1_
  24.6 4.5 %collective-permute-done.6.rest_2_ = s16[176,256]{1,0:T(8,128)(2,1)S(1)} collective-permute-done((s16[176,256]{1,0:T(8,128)(2,1)S(1)}, s16[176,256]{1,0:T(8,128)(2,1)S(1)}, u32[]{:S(2)}, u32[]{:S(2)}) %collective-permute-start.6) | collective-permute-done | bytes 90144 | tf_op jit(solution)/shard_map/ppermute | solution.py:795
  29.0 0.3 total.1.rest_0_
  29.3 0.1 collective-permute-start.9
  29.4 1.3 %collective-permute-start.8 = (s16[192,256]{1,0:T(8,128)(2,1)S(1)}, s16[192,256]{1,0:T(8,128)(2,1)S(1)}, u32[]{:S(2)}, u32[]{:S(2)}) collective-permute-start(s16[192,256]{1,0:T(8,128)(2,1)S(1)} %total.1.rest_0_), channel_id=1, source_target_pairs={{0,12},{4,8},{8,4},{12,0},{1,13},{5,9},{9,5},{13,1},{2,14},{6,10},... | collective-permute-start | bytes 294920 | tf_op jit(solution)/shard_map/ppermute | solution.py:795
  30.7 2.2 %collective-permute-start.7 = (s16[192,256]{1,0:T(8,128)(2,1)S(1)}, s16[192,256]{1,0:T(8,128)(2,1)S(1)}, u32[]{:S(2)}, u32[]{:S(2)}) collective-permute-start(s16[192,256]{1,0:T(8,128)(2,1)S(1)} %total.1.rest_0_), channel_id=1, source_target_pairs={{0,8},{4,12},{8,0},{12,4},{1,9},{5,13},{9,1},{13,5},{2,10},{6,14},... | collective-permute-start | bytes 294920 | tf_op jit(solution)/shard_map/ppermute | solution.py:795
  32.9 3.2 %collective-permute-done.9.rest_3_ = s16[192,256]{1,0:T(8,128)(2,1)S(1)} collective-permute-done((s16[192,256]{1,0:T(8,128)(2,1)S(1)}, s16[192,256]{1,0:T(8,128)(2,1)S(1)}, u32[]{:S(2)}, u32[]{:S(2)}) %collective-permute-start.9) | collective-permute-done | bytes 98336 | tf_op jit(solution)/shard_map/ppermute | solution.py:795
  36.0 1.0 %collective-permute-done.8.rest_2_ = s16[192,256]{1,0:T(8,128)(2,1)S(1)} collective-permute-done((s16[192,256]{1,0:T(8,128)(2,1)S(1)}, s16[192,256]{1,0:T(8,128)(2,1)S(1)}, u32[]{:S(2)}, u32[]{:S(2)}) %collective-permute-start.8) | collective-permute-done | bytes 98336 | tf_op jit(solution)/shard_map/ppermute | solution.py:795
  37.0 4.9 %collective-permute-done.7.rest_1_ = s16[192,256]{1,0:T(8,128)(2,1)S(1)} collective-permute-done((s16[192,256]{1,0:T(8,128)(2,1)S(1)}, s16[192,256]{1,0:T(8,128)(2,1)S(1)}, u32[]{:S(2)}, u32[]{:S(2)}) %collective-permute-start.7) | collective-permute-done | bytes 98336 | tf_op jit(solution)/shard_map/ppermute | solution.py:795
  41.9 0.0 copy-done.5
  42.0 2.7 %final.1 = (f32[320,1024]{1,0:T(8,128)}, f32[1024,128]{1,0:T(8,128)}) custom-call(s32[64]{0:T(128)S(1)} %copy-done.5, f32[3,1024,128]{2,1,0:T(8,128)S(1)} %get-tuple-element.20.w, s16[192,256]{1,0:T(8,128)(2,1)S(1)} %total.1.rest_0_, s16[192,256]{1,0:T(8,128)(2,1)S(1)} %collective-permute-done.7.rest_1_, s16[192,256]{1,0:T(8,128)(2,1)S(1)} %collective-permute-done.8.rest_2_, ...), custom_call_target="tpu_custom_call" | custom-call | tf_op jit(solution)/shard_map/final/pallas_call | solution.py:499
Async XLA Ops:
  0.6 9.1 %copy-start.2 = (f32[4096]{0:T(1024)S(1)}, f32[4096]{0:T(1024)}, u32[]{:S(2)}) copy-start(f32[4096]{0:T(1024)} %param.9) | copy-start | bytes 49156
  0.6 9.1 %copy-start.3 = (f32[4096]{0:T(1024)S(1)}, f32[4096]{0:T(1024)}, u32[]{:S(2)}) copy-start(f32[4096]{0:T(1024)} %param.10) | copy-start | bytes 49156
  2.4 13.2 %collective-permute-start.3 = (bf16[2048,128]{1,0:T(8,128)(2,1)S(1)}, bf16[2048,128]{1,0:T(8,128)(2,1)S(1)}, u32[]{:S(2)}, u32[]{:S(2)}) collective-permute-start(bf16[2048,128]{1,0:T(8,128)(2,1)S(1)} %get-tuple-element.21.sent_e), channel_id=1, source_target_pairs={{0,1},{1,0},{2,3},{3,2},{4,5},{5,4},{6,7},{7,6},{8,9},{9,8},{10,11... | collective-permute-start | bytes 1572872 | tf_op jit(solution)/shard_map/ppermute | solution.py:197
  2.9 12.7 %collective-permute-start.2 = (bf16[2048,128]{1,0:T(8,128)(2,1)S(1)}, bf16[2048,128]{1,0:T(8,128)(2,1)S(1)}, u32[]{:S(2)}, u32[]{:S(2)}) collective-permute-start(bf16[2048,128]{1,0:T(8,128)(2,1)S(1)} %get-tuple-element.22.sent_o), channel_id=1, source_target_pairs={{1,2},{2,1},{5,6},{6,5},{9,10},{10,9},{13,14},{14,13},{17,18},{18,... | collective-permute-start | bytes 1572872 | tf_op jit(solution)/shard_map/ppermute | solution.py:201
  3.6 16.7 %collective-permute-start = (s16[1040,128]{1,0:T(8,128)(2,1)S(1)}, s16[1040,128]{1,0:T(8,128)(2,1)S(1)}, u32[]{:S(2)}, u32[]{:S(2)}) collective-permute-start(s16[1040,128]{1,0:T(8,128)(2,1)S(1)} %get-tuple-element.18), channel_id=1, source_target_pairs={{4,8},{8,4},{5,9},{9,5},{6,10},{10,6},{7,11},{11,7},{20,24},{24,20... | collective-permute-start | bytes 798728 | tf_op jit(solution)/shard_map/ppermute | solution.py:201
  4.3 16.0 %collective-permute-start.1 = (s16[1040,128]{1,0:T(8,128)(2,1)S(1)}, s16[1040,128]{1,0:T(8,128)(2,1)S(1)}, u32[]{:S(2)}, u32[]{:S(2)}) collective-permute-start(s16[1040,128]{1,0:T(8,128)(2,1)S(1)} %get-tuple-element.19), channel_id=1, source_target_pairs={{0,4},{4,0},{8,12},{12,8},{1,5},{5,1},{9,13},{13,9},{2,6},{6,2},{1... | collective-permute-start | bytes 798728 | tf_op jit(solution)/shard_map/ppermute | solution.py:201
  15.5 4.8 %copy-start = (f32[1024,320]{0,1:T(8,128)S(1)}, f32[1024,320]{0,1:T(8,128)}, u32[]{:S(2)}) copy-start(f32[1024,320]{0,1:T(8,128)} %param.12) | copy-start | bytes 3932164
  15.5 4.7 %copy-start.1 = (f32[1024,128]{1,0:T(8,128)S(1)}, f32[1024,128]{1,0:T(8,128)}, u32[]{:S(2)}) copy-start(f32[1024,128]{1,0:T(8,128)} %z.3) | copy-start | bytes 1572868
  15.6 4.7 %copy-start.4 = (s32[1024,2]{0,1:T(2,128)S(1)}, s32[1024,2]{0,1:T(2,128)}, u32[]{:S(2)}) copy-start(s32[1024,2]{0,1:T(2,128)} %param.15) | copy-start | bytes 24580
  15.6 4.7 %copy-start.6 = (s32[64]{0:T(128)S(1)}, s32[64]{0:T(128)}, u32[]{:S(2)}) copy-start(s32[64]{0:T(128)} %band.2) | copy-start | bytes 772
  16.7 7.8 %collective-permute-start.4 = (s16[176,256]{1,0:T(8,128)(2,1)S(1)}, s16[176,256]{1,0:T(8,128)(2,1)S(1)}, u32[]{:S(2)}, u32[]{:S(2)}) collective-permute-start(s16[176,256]{1,0:T(8,128)(2,1)S(1)} %get-tuple-element.28), channel_id=1, source_target_pairs={{0,4},{4,0},{8,12},{12,8},{1,5},{5,1},{9,13},{13,9},{2,6},{6,2},{1... | collective-permute-start | bytes 270344 | tf_op jit(solution)/shard_map/ppermute | solution.py:795
  16.8 7.7 %collective-permute-start.5 = (s16[176,256]{1,0:T(8,128)(2,1)S(1)}, s16[176,256]{1,0:T(8,128)(2,1)S(1)}, u32[]{:S(2)}, u32[]{:S(2)}) collective-permute-start(s16[176,256]{1,0:T(8,128)(2,1)S(1)} %get-tuple-element.29), channel_id=1, source_target_pairs={{0,12},{4,8},{8,4},{12,0},{1,13},{5,9},{9,5},{13,1},{2,14},{6,10},... | collective-permute-start | bytes 270344 | tf_op jit(solution)/shard_map/ppermute | solution.py:795
  18.2 23.8 %copy-start.5 = (s32[64]{0:T(128)S(1)}, s32[64]{0:T(128)}, u32[]{:S(2)}) copy-start(s32[64]{0:T(128)} %band.3) | copy-start | bytes 772
  18.2 10.8 %collective-permute-start.6 = (s16[176,256]{1,0:T(8,128)(2,1)S(1)}, s16[176,256]{1,0:T(8,128)(2,1)S(1)}, u32[]{:S(2)}, u32[]{:S(2)}) collective-permute-start(s16[176,256]{1,0:T(8,128)(2,1)S(1)} %get-tuple-element.30), channel_id=1, source_target_pairs={{0,8},{4,12},{8,0},{12,4},{1,9},{5,13},{9,1},{13,5},{2,10},{6,14},... | collective-permute-start | bytes 270344 | tf_op jit(solution)/shard_map/ppermute | solution.py:795
  29.3 6.7 %collective-permute-start.9 = (s16[192,256]{1,0:T(8,128)(2,1)S(1)}, s16[192,256]{1,0:T(8,128)(2,1)S(1)}, u32[]{:S(2)}, u32[]{:S(2)}) collective-permute-start(s16[192,256]{1,0:T(8,128)(2,1)S(1)} %total.1.rest_0_), channel_id=1, source_target_pairs={{0,4},{4,0},{8,12},{12,8},{1,5},{5,1},{9,13},{13,9},{2,6},{6,2},{1... | collective-permute-start | bytes 294920 | tf_op jit(solution)/shard_map/ppermute | solution.py:795
  29.4 7.6 %collective-permute-start.8 = (s16[192,256]{1,0:T(8,128)(2,1)S(1)}, s16[192,256]{1,0:T(8,128)(2,1)S(1)}, u32[]{:S(2)}, u32[]{:S(2)}) collective-permute-start(s16[192,256]{1,0:T(8,128)(2,1)S(1)} %total.1.rest_0_), channel_id=1, source_target_pairs={{0,12},{4,8},{8,4},{12,0},{1,13},{5,9},{9,5},{13,1},{2,14},{6,10},... | collective-permute-start | bytes 294920 | tf_op jit(solution)/shard_map/ppermute | solution.py:795
  30.7 11.2 %collective-permute-start.7 = (s16[192,256]{1,0:T(8,128)(2,1)S(1)}, s16[192,256]{1,0:T(8,128)(2,1)S(1)}, u32[]{:S(2)}, u32[]{:S(2)}) collective-permute-start(s16[192,256]{1,0:T(8,128)(2,1)S(1)} %total.1.rest_0_), channel_id=1, source_target_pairs={{0,8},{4,12},{8,0},{12,4},{1,9},{5,13},{9,1},{13,5},{2,10},{6,14},... | collective-permute-start | bytes 294920 | tf_op jit(solution)/shard_map/ppermute | solution.py:795

commit v7 on v6

--- a/solution.py
+++ b/solution.py
@@ -207,7 +207,9 @@
 
 
 def quarter_at(step, first, parts):
-    return jnp.bitwise_xor(step, first)
+    if isinstance(first, int):
+        return (step + first) % parts
+    return lax.rem(step + first, parts)
 
 
 def tail_rows(parts):
@@ -222,58 +224,43 @@
 
 
 def gram_kernel(parts, rot, inv, dos, mean, scale, *rest):
-    outs = rest[:parts]
-    raw, normed, sem = rest[parts:]
+    outs, (head, last), normed = rest[:parts], rest[parts : parts + 2], rest[parts + 2]
     blocks = QW // LANE
     samples, cols = dos.shape
     base = line_index(("snp", "pair")) * (cols // LANE)
     first = lax.axis_index("smp") if rot else 0
-
-    def quarter_of(g):
-        return lax.rem(g + first, parts)
-
-    def fetch(g):
-        at = pl.multiple_of(quarter_of(g) * QW, QW)
-        return pltpu.make_async_copy(dos.at[:, pl.ds(at, QW)], raw.at[g], sem.at[g])
-
-    for g in range(parts):
-        fetch(g).start()
-
-    def settle(g):
-        fetch(g).wait()
-        block = quarter_of(g) * blocks
-        for b in range(blocks):
-            at = pl.multiple_of((block + b) * LANE, LANE)
-            normed[:, pl.ds(at, LANE)] = standard(
-                raw[g, :, b * LANE : (b + 1) * LANE], mean, scale, base + block + b
-            )
-
-    normed[:, cols:] = jnp.zeros((samples, LANE), jnp.bfloat16)
-    settle(0)
-    rows = (BMAX + 1) * TILE
     tail = tail_rows(parts)
-    low = low_lanes((rows, LANE))
     sub = lax.broadcasted_iota(jnp.int32, (TILE, LANE), 0)
     lane = lax.broadcasted_iota(jnp.int32, (TILE, LANE), 1)
     spot = lax.broadcasted_iota(jnp.int32, (tail, LANE), 0)
-
-    def step(g, _):
-        @pl.when(g < parts - 1)
-        def _():
-            settle(jnp.minimum(g + 1, parts - 1))
-
-        at = pl.multiple_of(quarter_of(g) * QW, QW)
-        full = tdot(normed[:, pl.ds(at, QW + LANE)], normed[:, pl.ds(at, QW)])
+    low = low_lanes(((BMAX + 1) * TILE, LANE))
+
+    def settle(g):
+        block = quarter_at(g, first, parts) * blocks
+        for b in range(blocks):
+            at = block + b
+            if rot:
+                at = pl.multiple_of(at * LANE, LANE)
+                values = dos[:, pl.ds(at, LANE)]
+            else:
+                values = dos[:, at * LANE : (at + 1) * LANE]
+            normed[g, :, b * LANE : (b + 1) * LANE] = standard(
+                values, mean, scale, base + block + b
+            )
+
+    settle(0)
+    for g in range(parts):
+        if g + 1 < parts:
+            settle(g + 1)
+        own = normed[g]
+        top = tdot(own, own)
+        bottom = tdot(normed[(g + 1) % parts, :, :LANE], own)
         pieces = []
         for b in range(blocks):
             cut = slice(b * LANE, (b + 1) * LANE)
+            full = jnp.concatenate([top[b * LANE :, cut], bottom[:, cut]], axis=0)
             pieces.append(
-                inv
-                * jnp.where(
-                    low,
-                    full[b * LANE : b * LANE + rows, cut],
-                    full[b * LANE + TILE : b * LANE + TILE + rows, cut],
-                )
+                inv * jnp.where(low, full[: low.shape[0]], full[TILE : TILE + low.shape[0]])
             )
         folded = [
             jnp.where(sub <= lane, p[:TILE], pltpu.roll(p[:TILE], TILE, axis=1)) for p in pieces
@@ -284,22 +271,15 @@
             for p in pieces
         ]
         ends = jnp.where(spot == 0, diagonals[0], jnp.where(spot == 1, diagonals[1], 0.0))
-        slot = quarter_at(quarter_of(g), first, parts)
-        for i in range(parts):
-
-            @pl.when(slot == i)
-            def _(i=i):
-                send = encode if rot and i > 0 else (lambda v: v)
-                for b in range(blocks):
-                    cut = slice(b * LANE, (b + 1) * LANE)
-                    outs[i][:DIAG, cut] = send(folded[b * DIAG : (b + 1) * DIAG])
-                    outs[i][DIAG:NEAR, cut] = send(pieces[b][TILE:])
-                outs[i][NEAR:, :LANE] = jnp.zeros((tail, LANE), outs[i].dtype)
-                outs[i][NEAR:, LANE:] = send(ends)
-
-        return 0
-
-    lax.fori_loop(0, parts, step, 0)
+        send = encode if rot and g > 0 else (lambda v: v)
+        for b in range(blocks):
+            cut = slice(b * LANE, (b + 1) * LANE)
+            outs[g][:DIAG, cut] = send(folded[b * DIAG : (b + 1) * DIAG])
+            outs[g][DIAG:NEAR, cut] = send(pieces[b][TILE:])
+        outs[g][NEAR:, :LANE] = jnp.zeros((tail, LANE), outs[g].dtype)
+        outs[g][NEAR:, LANE:] = send(ends)
+    head[...] = normed[lax.rem(parts - first, parts), :, :LANE]
+    last[...] = normed[parts - 1 - first, :, (blocks - 1) * LANE :]
 
 
 def gram_parts(dosage, mean, scale, rot, inv):
@@ -307,25 +287,23 @@
     parts = cols // QW
     rows = NEAR + tail_rows(parts)
     kinds = [jnp.float32] + [jnp.int16 if rot else jnp.float32] * (parts - 1)
+    shapes = [jax.ShapeDtypeStruct((rows, QW), kind) for kind in kinds]
+    shapes += [jax.ShapeDtypeStruct((samples, LANE), jnp.bfloat16)] * 2
     return pl.pallas_call(
         functools.partial(gram_kernel, parts, rot, inv),
-        in_specs=[pl.BlockSpec(memory_space=pltpu.HBM)] + [VMEM] * 2,
-        out_specs=[VMEM] * parts,
-        out_shape=[jax.ShapeDtypeStruct((rows, QW), kind) for kind in kinds],
-        scratch_shapes=[
-            pltpu.VMEM((parts, samples, QW), jnp.bfloat16),
-            pltpu.VMEM((samples, cols + LANE), jnp.bfloat16),
-            pltpu.SemaphoreType.DMA((parts,)),
-        ],
+        in_specs=[VMEM] * 3,
+        out_specs=[VMEM] * len(shapes),
+        out_shape=shapes,
+        scratch_shapes=[pltpu.VMEM((parts, samples, QW), jnp.bfloat16)],
         compiler_params=params(24),
         cost_estimate=pl.CostEstimate(
             flops=2 * samples * cols * (QW + LANE), bytes_accessed=dosage.size * 4, transcendentals=0
         ),
         name="gram",
-    )(in_hbm(dosage), mean, scale)
-
-
-def cross_kernel(parts, rot, inv, cols, sent_e, sent_o, got_o, got_e, mean, scale, *rest):
+    )(dosage, mean, scale)
+
+
+def cross_kernel(parts, rot, inv, cols, head, last, got_o, got_e, mean, scale, *rest):
     ins, outs, (zero, one) = rest[:parts], rest[parts : 2 * parts], rest[-2:]
     blocks = QW // LANE
     tail = tail_rows(parts)
@@ -336,10 +314,8 @@
     pick = lambda one, two: jnp.where(even, one[...], two[...])
     right = standard(pick(got_e, got_o), mean, scale, end)
     left = standard(pick(got_o, got_e), mean, scale, base - 1)
-    last = standard(pick(sent_e, sent_o), mean, scale, end - 1)
-    head = standard(pick(sent_o, sent_e), mean, scale, base)
-    ahead = inv * tdot(right, last)
-    behind = inv * tdot(left, head)
+    ahead = inv * tdot(right, last[...])
+    behind = inv * tdot(left, head[...])
     low = low_lanes((TILE, LANE))
     turned = pltpu.roll(behind[TILE:], TILE, axis=1)
     zero[...] = jnp.where(low, behind[:TILE], turned)
@@ -352,22 +328,27 @@
         kind = outs[i].dtype
         outs[i][:NEAR, :] = ins[i][:NEAR, :]
         quarter = quarter_at(i, first, parts)
-        share = pl.ds(pl.multiple_of(quarter * tail, 8), tail)
+        share = pl.ds(pl.multiple_of(quarter * tail, 8) if rot else quarter * tail, tail)
         outs[i][NEAR:, :LANE] = send(zero[share, :])
         outs[i][NEAR:, LANE:] = jnp.where(
             low_lanes((tail, LANE)), wide(send(one[share, :])), wide(ins[i][NEAR:, LANE:])
         ).astype(kind)
 
-        @pl.when(quarter == parts - 1)
-        def _(i=i, send=send, wide=wide, kind=kind):
+        def join(i=i, send=send, wide=wide, kind=kind):
             next_one = slice(DIAG, DIAG + TILE)
             outs[i][next_one, far] = jnp.where(
                 low, wide(ins[i][next_one, far]), wide(send(ahead[:TILE]))
             ).astype(kind)
             outs[i][DIAG + TILE : NEAR, far] = send(jnp.where(low, ahead[:TILE], ahead[TILE:]))
 
-
-def cross_parts(sent_e, sent_o, got_e, got_o, mean, scale, blocks, cols, rot, inv):
+        if rot:
+            pl.when(quarter == parts - 1)(join)
+        elif i == parts - 1:
+            join()
+
+
+def cross_parts(got_e, got_o, mean, scale, made, cols, rot, inv):
+    *blocks, head, last = made
     parts = len(blocks)
     height = NEAR + tail_rows(parts)
     return pl.pallas_call(
@@ -378,7 +359,7 @@
         scratch_shapes=[pltpu.VMEM((TILE, LANE), jnp.float32)] * 2,
         compiler_params=params(12),
         name="cross",
-    )(sent_e, sent_o, got_o, got_e, mean, scale, *blocks)
+    )(head, last, got_o, got_e, mean, scale, *blocks)
 
 
 def total_kernel(count, own, *rest):
@@ -433,7 +414,7 @@
         k = lax.axis_index("smp")
         total = None
         for piece, by in zip(ring, RING):
-            held[quarter_at(by, k, parts)] = decode(piece[0:height, :])
+            held[jnp.bitwise_xor(k, by)] = decode(piece[0:height, :])
             code = from_code(piece[height : height + 16, :])
             lanes = code.shape[1] // 2
             mom = decode_exact(code[:8, :lanes], code[8:, :lanes], code[:8, lanes:])
@@ -624,21 +605,33 @@
     def product(both, rest):
         return both[:, :traits] + both[:, traits:] + rest
 
-    def apply():
+    ext = total_blocks * LANE
+
+    def apply(step):
+        lo, hi = (step + 1) * REACH, ext - (step + 1) * REACH
+        done = 0
         for s in range(supers):
-            vec = ucat[REACH + s * sb : REACH + (s + 1) * sb, :]
-            part = product(dot(dh[s], vec), dot(dl[s], vec[:, :traits]))
             at = s * sb
-            if s == 0:
-                y[at : at + window, :] = part
-            else:
-                y[at : at + 2 * REACH, :] += part[: 2 * REACH]
-                y[at + 2 * REACH : at + window, :] = part[2 * REACH :]
+            begin = max(REACH + at, lo - REACH)
+            end = min(REACH + at + sb, hi + REACH)
+            top, bottom = max(at, lo), min(at + window, hi)
+            if begin >= end or top >= bottom:
+                continue
+            r = slice(top - at, bottom - at)
+            c = slice(begin - at - REACH, end - at - REACH)
+            vec = ucat[begin:end, :]
+            part = product(dot(dh[s, r, c], vec), dot(dl[s, r, c], vec[:, :traits]))
+            both = min(max(done - top, 0), bottom - top)
+            if both:
+                y[top : top + both, :] += part[:both]
+            if both < bottom - top:
+                y[top + both : bottom, :] = part[both:]
+            done = max(done, bottom)
 
     own = slice(HZ, HZ + rows)
     sums = []
     for step in range(ITERS):
-        apply()
+        apply(step)
         if step == 0:
             for edge_rows, edge_cols, s, target, source in (
                 (slice(0, LANE), slice(0, LANE), 0, 1, 0),
@@ -787,14 +780,17 @@
     inv = 1.0 / (samples if rot else samples * n_smp)
     mean = allele_mean.reshape(-1, LANE)
     scale = snp_scale.reshape(-1, LANE)
-    blocks = gram_parts(dosage, mean, scale, rot, inv)
-    blocks = cross_parts(sent[0], sent[1], dos_e, dos_o, mean, scale, blocks, cols, rot, inv)
+    made = gram_parts(dosage, mean, scale, rot, inv)
+    blocks = cross_parts(dos_e, dos_o, mean, scale, made, cols, rot, inv)
     if rot:
+
+        def shift(value, by):
+            return lax.ppermute(value, "smp", [(i, (i + by) % n_smp) for i in range(n_smp)])
 
         def swap(value, by):
             return lax.ppermute(value, "smp", [(i, i ^ by) for i in range(n_smp)])
 
-        got = [swap(blocks[by], by) for by in (1, 3, 2)]
+        got = [shift(blocks[by], by) for by in (1, 2, 3)]
     w, mom = krylov(ldt, zscores, obs, got_e, got_o, band_prev, paired)
     if rot:
         mine = total_of(blocks[0], got, mom)

time: 44.8 us -> 42.7 us (0.953)
  starting transfers between devices: 14.5 us -> 17.7 us
  Pallas kernels: 15.8 us -> 13.1 us
  waiting for transfers between devices: 13.5 us -> 10.9 us
    ppermute x6 -> x3, waiting for transfers between devices: 13.5 us -> 8.84 us  [swap(): return lax.ppermute(value, 'smp', [(i, i ^ by) for i in range(n_smp)])]
    ppermute x0 -> x3, starting transfers between devices: none -> 3.88 us  [shift(): lax.ppermute(value, 'smp', [(i, (i + by) % n_smp) for i in range(n_smp)])]
    ppermute x1, starting transfers between devices: 0.56 us -> 4.36 us  [exchange(): return lax.ppermute(value, axes[-1], [(0, 1), (1, 0)])]
    ppermute x6 -> x3, starting transfers between devices: 7.1 us -> 3.55 us  [swap(): return lax.ppermute(value, 'smp', [(i, i ^ by) for i in range(n_smp)])]
    pallas_call x1, Pallas kernels: 5.76 us -> 3.61 us  [gram_parts(): pl.pallas_call(functools.partial(gram_kernel, parts, rot, inv), in_specs=...]
    ppermute x0 -> x3, waiting for transfers between devices: none -> 2.03 us  [shift(): lax.ppermute(value, 'smp', [(i, (i + by) % n_smp) for i in range(n_smp)])]
    ppermute x3, starting transfers between devices: 6.82 us -> 5.94 us  [exchange(): return lax.ppermute(value, axes, pairs)]
  transfers between devices with their start and end apart: 10 -> 10, of which waited for: 4 -> 4; matrix products, arithmetic and copies ran while one was open for 0% -> 0% of each run, Pallas kernels for 25% -> 19%
where the time goes in v7:
time: 42.7 us; the launch traced here: 42.5 us
  starting transfers between devices  17.7 us (41%)
  Pallas kernels  13.1 us (31%)
  waiting for transfers between devices  10.9 us (26%)
  between operations  0.79 us (2%)
    ppermute x3, waiting for transfers between devices, swap(): return lax.ppermute(value, 'smp', [(i, i ^ by) for i in range(n_smp)])  8.84 us
    ppermute x3, starting transfers between devices, exchange(): return lax.ppermute(value, axes, pairs)  5.94 us
    ppermute x1, starting transfers between devices, exchange(): return lax.ppermute(value, axes[-1], [(0, 1), (1, 0)])  4.36 us
    ppermute x3, starting transfers between devices, shift(): lax.ppermute(value, 'smp', [(i, (i + by) % n_smp) for i in range(n_smp)])  3.88 us
    pallas_call x1, Pallas kernels, krylov(): pl.pallas_call(functools.partial(krylov_kernel, band_prev.shape[0], sb, p...  3.84 us
    pallas_call x1, Pallas kernels, gram_parts(): pl.pallas_call(functools.partial(gram_kernel, parts, rot, inv), in_specs=...  3.61 us
    ppermute x3, starting transfers between devices, swap(): return lax.ppermute(value, 'smp', [(i, i ^ by) for i in range(n_smp)])  3.55 us
    pallas_call x1, Pallas kernels, final(): pl.pallas_call(functools.partial(final_kernel, parts, rot, len(moms), ban...  2.69 us
  transfers between devices with their start and end apart: 10, of which 4 were waited for; matrix products, arithmetic and copies ran while one was open for 0% of the time, Pallas kernels for 19%

profile of v7, /device:TPU:0, one launch (start us, length us, event | category | flops | bytes accessed | tf_op | source)
XLA Modules:
  0.0 42.5 jit_solution(10124028559119665121)
XLA Ops:
  0.6 0.0 copy-start
  0.6 0.0 copy-start.3
  0.6 0.0 copy-start.4
  0.7 1.8 %pack.1 = (bf16[2048,128]{1,0:T(8,128)(2,1)S(1)}, bf16[2048,128]{1,0:T(8,128)(2,1)S(1)}, s16[1040,128]{1,0:T(8,128)(2,1)S(1)}, s16[1040,128]{1,0:T(8,128)(2,1)S(1)}) custom-call(bf16[2048,1024]{1,0:T(8,128)(2,1)} %dos.3, f32[1024,128]{1,0:T(8,128)} %z.3, f32[320,1024]{1,0:T(8,128)} %bitcast.5, s32[2,1024]{1,0:T(2,128)} %bitcast.11), custom_call_target="tpu_custom_call" | custom-call | tf_op jit(solution)/shard_map/pack/pallas_call | solution.py:181
  2.5 0.8 %collective-permute-start.2 = (bf16[2048,128]{1,0:T(8,128)(2,1)S(1)}, bf16[2048,128]{1,0:T(8,128)(2,1)S(1)}, u32[]{:S(2)}, u32[]{:S(2)}) collective-permute-start(bf16[2048,128]{1,0:T(8,128)(2,1)S(1)} %get-tuple-element.25), channel_id=1, source_target_pairs={{1,2},{2,1},{5,6},{6,5},{9,10},{10,9},{13,14},{14,13},{17,18},{18,... | collective-permute-start | bytes 1572872 | tf_op jit(solution)/shard_map/ppermute | solution.py:201
  3.3 4.4 %collective-permute-start.3 = (bf16[2048,128]{1,0:T(8,128)(2,1)S(1)}, bf16[2048,128]{1,0:T(8,128)(2,1)S(1)}, u32[]{:S(2)}, u32[]{:S(2)}) collective-permute-start(bf16[2048,128]{1,0:T(8,128)(2,1)S(1)} %get-tuple-element.26), channel_id=1, source_target_pairs={{0,1},{1,0},{2,3},{3,2},{4,5},{5,4},{6,7},{7,6},{8,9},{9,8},{10,11... | collective-permute-start | bytes 1572872 | tf_op jit(solution)/shard_map/ppermute | solution.py:197
  7.7 0.7 %collective-permute-start = (s16[1040,128]{1,0:T(8,128)(2,1)S(1)}, s16[1040,128]{1,0:T(8,128)(2,1)S(1)}, u32[]{:S(2)}, u32[]{:S(2)}) collective-permute-start(s16[1040,128]{1,0:T(8,128)(2,1)S(1)} %get-tuple-element.20), channel_id=1, source_target_pairs={{4,8},{8,4},{5,9},{9,5},{6,10},{10,6},{7,11},{11,7},{20,24},{24,20... | collective-permute-start | bytes 798728 | tf_op jit(solution)/shard_map/ppermute | solution.py:201
  8.4 4.4 %collective-permute-start.1 = (s16[1040,128]{1,0:T(8,128)(2,1)S(1)}, s16[1040,128]{1,0:T(8,128)(2,1)S(1)}, u32[]{:S(2)}, u32[]{:S(2)}) collective-permute-start(s16[1040,128]{1,0:T(8,128)(2,1)S(1)} %get-tuple-element.21), channel_id=1, source_target_pairs={{0,4},{4,0},{8,12},{12,8},{1,5},{5,1},{9,13},{13,9},{2,6},{6,2},{1... | collective-permute-start | bytes 798728 | tf_op jit(solution)/shard_map/ppermute | solution.py:201
  12.8 0.0 copy-done
  12.8 0.0 copy-done.3
  12.8 0.0 copy-done.4
  12.8 3.6 %gram.1 = (f32[176,256]{1,0:T(8,128)S(1)}, s16[176,256]{1,0:T(8,128)(2,1)S(1)}, s16[176,256]{1,0:T(8,128)(2,1)S(1)}, s16[176,256]{1,0:T(8,128)(2,1)S(1)}, bf16[2...) custom-call(bf16[2048,1024]{1,0:T(8,128)(2,1)S(1)} %copy-done, f32[32,128]{1,0:T(8,128)S(1)} %bitcast.7, ...), custom_call_target="tpu_custom_call" | custom-call | flops 1610612736 | bytes 8388608 | tf_op jit(solution)/shard_map/gram/pallas_call | solution.py:292
  16.4 0.0 copy-start.1
  16.5 0.0 copy-start.2
  16.5 0.0 copy-start.5
  16.5 0.0 copy-start.7
  16.5 0.0 collective-permute-done.2.got_o
  16.5 0.0 collective-permute-done.3.got_e
  16.5 0.8 %cross.1 = (f32[176,256]{1,0:T(8,128)S(1)}, s16[176,256]{1,0:T(8,128)(2,1)S(1)}, s16[176,256]{1,0:T(8,128)(2,1)S(1)}, s16[176,256]{1,0:T(8,128)(2,1)S(1)}) custom-call(bf16[2048,128]{1,0:T(8,128)(2,1)S(1)} %get-tuple-element.23.head, bf16[2048,128]{1,0:T(8,128)(2,1)S(1)} %get-tuple-element.24.last, bf16[2048,128]{1,0:T(8,128)(2,1)S(1)} %collective-permute-done.2.got_o, ...), custom_call_target="tpu_custom_call" | custom-call | tf_op jit(solution)/shard_map/cross/pallas_call | solution.py:354
  17.3 0.1 collective-permute-start.4
  17.4 1.8 %collective-permute-start.5 = (s16[176,256]{1,0:T(8,128)(2,1)S(1)}, s16[176,256]{1,0:T(8,128)(2,1)S(1)}, u32[]{:S(2)}, u32[]{:S(2)}) collective-permute-start(s16[176,256]{1,0:T(8,128)(2,1)S(1)} %get-tuple-element.33), channel_id=1, source_target_pairs={{0,8},{4,12},{8,0},{12,4},{1,9},{5,13},{9,1},{13,5},{2,10},{6,14},... | collective-permute-start | bytes 270344 | tf_op jit(solution)/shard_map/ppermute | solution.py:788
  19.2 0.0 copy-start.6
  19.2 2.0 %collective-permute-start.6 = (s16[176,256]{1,0:T(8,128)(2,1)S(1)}, s16[176,256]{1,0:T(8,128)(2,1)S(1)}, u32[]{:S(2)}, u32[]{:S(2)}) collective-permute-start(s16[176,256]{1,0:T(8,128)(2,1)S(1)} %get-tuple-element.34), channel_id=1, source_target_pairs={{0,12},{4,0},{8,4},{12,8},{1,13},{5,1},{9,5},{13,9},{2,14},{6,2},{... | collective-permute-start | bytes 270344 | tf_op jit(solution)/shard_map/ppermute | solution.py:788
  21.2 0.0 collective-permute-done.got_o
  21.2 0.0 collective-permute-done.1.got_e
  21.2 0.0 copy-done.1
  21.2 0.0 copy-done.2
  21.2 0.0 copy-done.5
  21.2 0.0 copy-done.7
  21.2 3.8 %krylov.1 = (f32[3,1024,128]{2,1,0:T(8,128)S(1)}, f32[8,128]{1,0:T(8,128)S(1)}) custom-call(s32[64]{0:T(128)S(1)} %copy-done.7, f32[320,1024]{1,0:T(8,128)S(1)} %bitcast.6, f32[1024,128]{1,0:T(8,128)S(1)} %copy-done.2, s32[2,1024]{1,0:T(2,128)S(1)} %bitcast.12, s16[1040,128]{1,0:T(8,128)(2,1)S(1)} %collective-permute-done.got_o, ...), custom_call_target="tpu_custom_call" | custom-call | flops 1321205760 | bytes 1310720 | tf_op jit(solution)/shard_map/krylov/pallas_call | solution.py:676
  25.1 0.0 collective-permute-done.4.rest_0_
  25.1 2.0 %collective-permute-done.5.rest_1_ = s16[176,256]{1,0:T(8,128)(2,1)S(1)} collective-permute-done((s16[176,256]{1,0:T(8,128)(2,1)S(1)}, s16[176,256]{1,0:T(8,128)(2,1)S(1)}, u32[]{:S(2)}, u32[]{:S(2)}) %collective-permute-start.5) | collective-permute-done | bytes 90144 | tf_op jit(solution)/shard_map/ppermute | solution.py:788
  27.1 0.0 collective-permute-done.6.rest_2_
  27.1 0.3 total.1.rest_0_
  27.4 1.6 %collective-permute-start.9 = (s16[192,256]{1,0:T(8,128)(2,1)S(1)}, s16[192,256]{1,0:T(8,128)(2,1)S(1)}, u32[]{:S(2)}, u32[]{:S(2)}) collective-permute-start(s16[192,256]{1,0:T(8,128)(2,1)S(1)} %total.1.rest_0_), channel_id=1, source_target_pairs={{0,4},{4,0},{8,12},{12,8},{1,5},{5,1},{9,13},{13,9},{2,6},{6,2},{1... | collective-permute-start | bytes 294920 | tf_op jit(solution)/shard_map/ppermute | solution.py:791
  29.1 1.0 %collective-permute-start.8 = (s16[192,256]{1,0:T(8,128)(2,1)S(1)}, s16[192,256]{1,0:T(8,128)(2,1)S(1)}, u32[]{:S(2)}, u32[]{:S(2)}) collective-permute-start(s16[192,256]{1,0:T(8,128)(2,1)S(1)} %total.1.rest_0_), channel_id=1, source_target_pairs={{0,12},{4,8},{8,4},{12,0},{1,13},{5,9},{9,5},{13,1},{2,14},{6,10},... | collective-permute-start | bytes 294920 | tf_op jit(solution)/shard_map/ppermute | solution.py:791
  30.1 0.9 %collective-permute-start.7 = (s16[192,256]{1,0:T(8,128)(2,1)S(1)}, s16[192,256]{1,0:T(8,128)(2,1)S(1)}, u32[]{:S(2)}, u32[]{:S(2)}) collective-permute-start(s16[192,256]{1,0:T(8,128)(2,1)S(1)} %total.1.rest_0_), channel_id=1, source_target_pairs={{0,8},{4,12},{8,0},{12,4},{1,9},{5,13},{9,1},{13,5},{2,10},{6,14},... | collective-permute-start | bytes 294920 | tf_op jit(solution)/shard_map/ppermute | solution.py:791
  31.0 1.3 %collective-permute-done.9.rest_3_ = s16[192,256]{1,0:T(8,128)(2,1)S(1)} collective-permute-done((s16[192,256]{1,0:T(8,128)(2,1)S(1)}, s16[192,256]{1,0:T(8,128)(2,1)S(1)}, u32[]{:S(2)}, u32[]{:S(2)}) %collective-permute-start.9) | collective-permute-done | bytes 98336 | tf_op jit(solution)/shard_map/ppermute | solution.py:791
  32.3 3.6 %collective-permute-done.8.rest_2_ = s16[192,256]{1,0:T(8,128)(2,1)S(1)} collective-permute-done((s16[192,256]{1,0:T(8,128)(2,1)S(1)}, s16[192,256]{1,0:T(8,128)(2,1)S(1)}, u32[]{:S(2)}, u32[]{:S(2)}) %collective-permute-start.8) | collective-permute-done | bytes 98336 | tf_op jit(solution)/shard_map/ppermute | solution.py:791
  35.9 3.9 %collective-permute-done.7.rest_1_ = s16[192,256]{1,0:T(8,128)(2,1)S(1)} collective-permute-done((s16[192,256]{1,0:T(8,128)(2,1)S(1)}, s16[192,256]{1,0:T(8,128)(2,1)S(1)}, u32[]{:S(2)}, u32[]{:S(2)}) %collective-permute-start.7) | collective-permute-done | bytes 98336 | tf_op jit(solution)/shard_map/ppermute | solution.py:791
  39.8 0.0 copy-done.6
  39.9 2.7 %final.1 = (f32[320,1024]{1,0:T(8,128)}, f32[1024,128]{1,0:T(8,128)}) custom-call(s32[64]{0:T(128)S(1)} %copy-done.6, f32[3,1024,128]{2,1,0:T(8,128)S(1)} %get-tuple-element.22.w, s16[192,256]{1,0:T(8,128)(2,1)S(1)} %total.1.rest_0_, s16[192,256]{1,0:T(8,128)(2,1)S(1)} %collective-permute-done.7.rest_1_, s16[192,256]{1,0:T(8,128)(2,1)S(1)} %collective-permute-done.8.rest_2_, ...), custom_call_target="tpu_custom_call" | custom-call | tf_op jit(solution)/shard_map/final/pallas_call | solution.py:480
Async XLA Ops:
  0.6 12.2 %copy-start = (bf16[2048,1024]{1,0:T(8,128)(2,1)S(1)}, bf16[2048,1024]{1,0:T(8,128)(2,1)}, u32[]{:S(2)}) copy-start(bf16[2048,1024]{1,0:T(8,128)(2,1)} %dos.3) | copy-start | bytes 12582916
  0.6 12.2 %copy-start.3 = (f32[4096]{0:T(1024)S(1)}, f32[4096]{0:T(1024)}, u32[]{:S(2)}) copy-start(f32[4096]{0:T(1024)} %param.9) | copy-start | bytes 49156
  0.6 12.2 %copy-start.4 = (f32[4096]{0:T(1024)S(1)}, f32[4096]{0:T(1024)}, u32[]{:S(2)}) copy-start(f32[4096]{0:T(1024)} %param.10) | copy-start | bytes 49156
  2.5 14.0 %collective-permute-start.2 = (bf16[2048,128]{1,0:T(8,128)(2,1)S(1)}, bf16[2048,128]{1,0:T(8,128)(2,1)S(1)}, u32[]{:S(2)}, u32[]{:S(2)}) collective-permute-start(bf16[2048,128]{1,0:T(8,128)(2,1)S(1)} %get-tuple-element.25), channel_id=1, source_target_pairs={{1,2},{2,1},{5,6},{6,5},{9,10},{10,9},{13,14},{14,13},{17,18},{18,... | collective-permute-start | bytes 1572872 | tf_op jit(solution)/shard_map/ppermute | solution.py:201
  3.3 13.2 %collective-permute-start.3 = (bf16[2048,128]{1,0:T(8,128)(2,1)S(1)}, bf16[2048,128]{1,0:T(8,128)(2,1)S(1)}, u32[]{:S(2)}, u32[]{:S(2)}) collective-permute-start(bf16[2048,128]{1,0:T(8,128)(2,1)S(1)} %get-tuple-element.26), channel_id=1, source_target_pairs={{0,1},{1,0},{2,3},{3,2},{4,5},{5,4},{6,7},{7,6},{8,9},{9,8},{10,11... | collective-permute-start | bytes 1572872 | tf_op jit(solution)/shard_map/ppermute | solution.py:197
  7.7 13.5 %collective-permute-start = (s16[1040,128]{1,0:T(8,128)(2,1)S(1)}, s16[1040,128]{1,0:T(8,128)(2,1)S(1)}, u32[]{:S(2)}, u32[]{:S(2)}) collective-permute-start(s16[1040,128]{1,0:T(8,128)(2,1)S(1)} %get-tuple-element.20), channel_id=1, source_target_pairs={{4,8},{8,4},{5,9},{9,5},{6,10},{10,6},{7,11},{11,7},{20,24},{24,20... | collective-permute-start | bytes 798728 | tf_op jit(solution)/shard_map/ppermute | solution.py:201
  8.4 12.8 %collective-permute-start.1 = (s16[1040,128]{1,0:T(8,128)(2,1)S(1)}, s16[1040,128]{1,0:T(8,128)(2,1)S(1)}, u32[]{:S(2)}, u32[]{:S(2)}) collective-permute-start(s16[1040,128]{1,0:T(8,128)(2,1)S(1)} %get-tuple-element.21), channel_id=1, source_target_pairs={{0,4},{4,0},{8,12},{12,8},{1,5},{5,1},{9,13},{13,9},{2,6},{6,2},{1... | collective-permute-start | bytes 798728 | tf_op jit(solution)/shard_map/ppermute | solution.py:201
  16.4 4.8 %copy-start.1 = (f32[1024,320]{0,1:T(8,128)S(1)}, f32[1024,320]{0,1:T(8,128)}, u32[]{:S(2)}) copy-start(f32[1024,320]{0,1:T(8,128)} %param.12) | copy-start | bytes 3932164
  16.5 4.8 %copy-start.2 = (f32[1024,128]{1,0:T(8,128)S(1)}, f32[1024,128]{1,0:T(8,128)}, u32[]{:S(2)}) copy-start(f32[1024,128]{1,0:T(8,128)} %z.3) | copy-start | bytes 1572868
  16.5 4.8 %copy-start.5 = (s32[1024,2]{0,1:T(2,128)S(1)}, s32[1024,2]{0,1:T(2,128)}, u32[]{:S(2)}) copy-start(s32[1024,2]{0,1:T(2,128)} %param.15) | copy-start | bytes 24580
  16.5 4.8 %copy-start.7 = (s32[64]{0:T(128)S(1)}, s32[64]{0:T(128)}, u32[]{:S(2)}) copy-start(s32[64]{0:T(128)} %band.2) | copy-start | bytes 772
  17.3 7.8 %collective-permute-start.4 = (s16[176,256]{1,0:T(8,128)(2,1)S(1)}, s16[176,256]{1,0:T(8,128)(2,1)S(1)}, u32[]{:S(2)}, u32[]{:S(2)}) collective-permute-start(s16[176,256]{1,0:T(8,128)(2,1)S(1)} %get-tuple-element.32), channel_id=1, source_target_pairs={{0,4},{4,8},{8,12},{12,0},{1,5},{5,9},{9,13},{13,1},{2,6},{6,10},{... | collective-permute-start | bytes 270344 | tf_op jit(solution)/shard_map/ppermute | solution.py:788
  17.4 9.7 %collective-permute-start.5 = (s16[176,256]{1,0:T(8,128)(2,1)S(1)}, s16[176,256]{1,0:T(8,128)(2,1)S(1)}, u32[]{:S(2)}, u32[]{:S(2)}) collective-permute-start(s16[176,256]{1,0:T(8,128)(2,1)S(1)} %get-tuple-element.33), channel_id=1, source_target_pairs={{0,8},{4,12},{8,0},{12,4},{1,9},{5,13},{9,1},{13,5},{2,10},{6,14},... | collective-permute-start | bytes 270344 | tf_op jit(solution)/shard_map/ppermute | solution.py:788
  19.2 20.6 %copy-start.6 = (s32[64]{0:T(128)S(1)}, s32[64]{0:T(128)}, u32[]{:S(2)}) copy-start(s32[64]{0:T(128)} %band.3) | copy-start | bytes 772
  19.2 7.9 %collective-permute-start.6 = (s16[176,256]{1,0:T(8,128)(2,1)S(1)}, s16[176,256]{1,0:T(8,128)(2,1)S(1)}, u32[]{:S(2)}, u32[]{:S(2)}) collective-permute-start(s16[176,256]{1,0:T(8,128)(2,1)S(1)} %get-tuple-element.34), channel_id=1, source_target_pairs={{0,12},{4,0},{8,4},{12,8},{1,13},{5,1},{9,5},{13,9},{2,14},{6,2},{... | collective-permute-start | bytes 270344 | tf_op jit(solution)/shard_map/ppermute | solution.py:788
  27.4 4.8 %collective-permute-start.9 = (s16[192,256]{1,0:T(8,128)(2,1)S(1)}, s16[192,256]{1,0:T(8,128)(2,1)S(1)}, u32[]{:S(2)}, u32[]{:S(2)}) collective-permute-start(s16[192,256]{1,0:T(8,128)(2,1)S(1)} %total.1.rest_0_), channel_id=1, source_target_pairs={{0,4},{4,0},{8,12},{12,8},{1,5},{5,1},{9,13},{13,9},{2,6},{6,2},{1... | collective-permute-start | bytes 294920 | tf_op jit(solution)/shard_map/ppermute | solution.py:791
  29.1 6.8 %collective-permute-start.8 = (s16[192,256]{1,0:T(8,128)(2,1)S(1)}, s16[192,256]{1,0:T(8,128)(2,1)S(1)}, u32[]{:S(2)}, u32[]{:S(2)}) collective-permute-start(s16[192,256]{1,0:T(8,128)(2,1)S(1)} %total.1.rest_0_), channel_id=1, source_target_pairs={{0,12},{4,8},{8,4},{12,0},{1,13},{5,9},{9,5},{13,1},{2,14},{6,10},... | collective-permute-start | bytes 294920 | tf_op jit(solution)/shard_map/ppermute | solution.py:791
  30.1 9.7 %collective-permute-start.7 = (s16[192,256]{1,0:T(8,128)(2,1)S(1)}, s16[192,256]{1,0:T(8,128)(2,1)S(1)}, u32[]{:S(2)}, u32[]{:S(2)}) collective-permute-start(s16[192,256]{1,0:T(8,128)(2,1)S(1)} %total.1.rest_0_), channel_id=1, source_target_pairs={{0,8},{4,12},{8,0},{12,4},{1,9},{5,13},{9,1},{13,5},{2,10},{6,14},... | collective-permute-start | bytes 294920 | tf_op jit(solution)/shard_map/ppermute | solution.py:791

commit v8 on v7

--- a/solution.py
+++ b/solution.py
@@ -19,28 +19,35 @@
 HB = (ITERS - 1) * REACH
 TINY = 1e-6
 VMEM = pl.BlockSpec(memory_space=pltpu.VMEM)
-SMEM = pl.BlockSpec(memory_space=pltpu.SMEM)
 
 
 def params(mib):
     return pltpu.CompilerParams(vmem_limit_bytes=mib * 1024 * 1024)
 
 
-def mask_rows(band_ref, first_tile, total):
-    def width(t):
-        inside = (t >= 0) & (t < total)
-        return jnp.where(inside, band_ref[jnp.clip(t, 0, total - 1)], 0)
-
-    widths = [width(first_tile + d) for d in range(-BMAX, BMAX + 2)]
-    low = lax.broadcasted_iota(jnp.int32, (1, LANE), 1) < TILE
+def mask_table(band_ref, first_tile, tiles):
+    total = band_ref.shape[1]
+    lanes = (tiles + 2 * BMAX) * TILE
+    shape = (total, lanes)
+    tile = lax.broadcasted_iota(jnp.int32, shape, 1) // TILE + (first_tile - BMAX)
+    chosen = tile == lax.broadcasted_iota(jnp.int32, shape, 0)
+    given = jnp.broadcast_to(band_ref[...].astype(jnp.float32), (8, total)).astype(jnp.bfloat16)
+    widths = dot(given, chosen.astype(jnp.float32).astype(jnp.bfloat16))[:1]
+    here = widths[:, BMAX * TILE : (BMAX + tiles) * TILE]
     rows = []
     for q in range(-BMAX, BMAX + 1):
-        flags = [
-            (abs(q) <= jnp.minimum(widths[BMAX + t], widths[BMAX + t + q])).astype(jnp.float32)
-            for t in range(2)
-        ]
-        rows.append(jnp.where(low, flags[0], flags[1]))
+        if q % 2:
+            beside = pltpu.roll(widths, (-q * TILE) % lanes, axis=1)[
+                :, BMAX * TILE : (BMAX + tiles) * TILE
+            ]
+        else:
+            beside = widths[:, (BMAX + q) * TILE : (BMAX + q + tiles) * TILE]
+        rows.append((abs(q) <= jnp.minimum(here, beside)).astype(jnp.float32))
     return rows
+
+
+def masks_at(table, block):
+    return [row[:, block * LANE : (block + 1) * LANE] for row in table]
 
 
 def low_lanes(shape):
@@ -303,7 +310,7 @@
     )(dosage, mean, scale)
 
 
-def cross_kernel(parts, rot, inv, cols, head, last, got_o, got_e, mean, scale, *rest):
+def cross_kernel(parts, rot, inv, cols, head, last, got_e, got_o, mean, scale, *rest):
     ins, outs, (zero, one) = rest[:parts], rest[parts : 2 * parts], rest[-2:]
     blocks = QW // LANE
     tail = tail_rows(parts)
@@ -359,7 +366,7 @@
         scratch_shapes=[pltpu.VMEM((TILE, LANE), jnp.float32)] * 2,
         compiler_params=params(12),
         name="cross",
-    )(head, last, got_o, got_e, mean, scale, *blocks)
+    )(head, last, got_e, got_o, mean, scale, *blocks)
 
 
 def total_kernel(count, own, *rest):
@@ -388,7 +395,7 @@
     )(own, *others, mom)
 
 
-def final_kernel(parts, rot, moments, tile_total, band, w, *rest):
+def final_kernel(parts, rot, moments, band, w, *rest):
     ring = rest[:parts]
     moms = rest[parts : parts + moments]
     out_far, imputed_far, held, out, imputed, sem = rest[parts + moments :]
@@ -400,6 +407,7 @@
     lane = lax.broadcasted_iota(jnp.int32, (TILE, LANE), 1)
     cols = out.shape[1]
     first_tile = line_index(("snp", "pair")) * (cols // TILE)
+    table = mask_table(band, first_tile, cols // TILE)
     copies = []
 
     def ship(source, target):
@@ -434,7 +442,7 @@
             a = quarter * blocks + b
             cut = slice(b * LANE, (b + 1) * LANE)
             cols_here = slice(a * LANE, (a + 1) * LANE)
-            masks = mask_rows(band, first_tile + 2 * a, tile_total)
+            masks = masks_at(table, a)
             here, there = (fold, mirror) if b == 0 else (swap(fold), swap(mirror))
             second = jnp.where(
                 sub == lane - TILE,
@@ -478,8 +486,8 @@
         jax.ShapeDtypeStruct(w.shape[1:], jnp.float32),
     ]
     return pl.pallas_call(
-        functools.partial(final_kernel, parts, rot, len(moms), band_next.shape[0]),
-        in_specs=[SMEM] + [VMEM] * (1 + parts + len(moms)),
+        functools.partial(final_kernel, parts, rot, len(moms)),
+        in_specs=[VMEM] * (2 + parts + len(moms)),
         out_specs=[pl.BlockSpec(memory_space=pltpu.HBM)] * 2,
         out_shape=shapes,
         scratch_shapes=[
@@ -490,7 +498,7 @@
         ],
         compiler_params=params(16),
         name="final",
-    )(band_next, w, *ring, *moms)
+    )(band_next.reshape(1, -1), w, *ring, *moms)
 
 
 class Side:
@@ -513,7 +521,7 @@
 
 
 def krylov_kernel(
-    tile_total, sb, paired, band, ldt, z, obs, got_o, got_e, w_out, mom_out,
+    sb, paired, band, ldt, z, obs, got_o, got_e, w_out, mom_out,
     dh, dl, ucat, seen, u_prev, y
 ):
     rows = ldt.shape[1]
@@ -563,6 +571,7 @@
     sub = lax.broadcasted_iota(jnp.int32, (TILE, LANE), 0)
     lane = lax.broadcasted_iota(jnp.int32, (TILE, LANE), 1)
     chunks = SPAN + 1
+    table = mask_table(band, first_tile - HB // TILE, (rows + 2 * HB) // TILE)
     for c in range(own_blocks + 2 * bb):
         if c < bb:
             full = halo_l.band((slice(HZ + c * ld_rows, HZ + (c + 1) * ld_rows), slice(None)))
@@ -573,7 +582,7 @@
             o = c - bb - own_blocks
             full = halo_r.band((slice(HZ + o * ld_rows, HZ + (o + 1) * ld_rows), slice(None)))
             get = lambda q, full=full: full[q * TILE : (q + 1) * TILE]
-        masks = mask_rows(band, first_tile + 2 * (c - bb), tile_total)
+        masks = masks_at(table, c)
         s, h = c // per, c % per
         cols = slice(h * LANE, (h + 1) * LANE)
         parts = [get(q) * masks[q] for q in range(SPAN)]
@@ -674,8 +683,8 @@
     ext = rows + 2 * HZ
     supers = wide // sb
     return pl.pallas_call(
-        functools.partial(krylov_kernel, band_prev.shape[0], sb, paired),
-        in_specs=[SMEM] + [VMEM] * 5,
+        functools.partial(krylov_kernel, sb, paired),
+        in_specs=[VMEM] * 6,
         out_specs=[VMEM, VMEM],
         out_shape=[
             jax.ShapeDtypeStruct((ITERS, rows, traits), jnp.float32),
@@ -694,7 +703,7 @@
             flops=ITERS * 6 * ext * SPAN * TILE * traits, bytes_accessed=ldt.size * 4, transcendentals=0
         ),
         name="krylov",
-    )(band_prev, ldt, z, obs, got_o, got_e)
+    )(band_prev.reshape(1, -1), ldt, z, obs, got_o, got_e)
 
 
 def solve(w, mom, out):
@@ -767,8 +776,8 @@
     paired = rows >= HZ
 
     sent = pack(dosage, zscores, ldt, obs, paired)
+    dos_e = exchange(sent[0], line, 0)
     dos_o = exchange(sent[1], line, 1)
-    dos_e = exchange(sent[0], line, 0)
     if paired:
         got_o = exchange(sent[3], ("smp",), 1)
         got_e = exchange(sent[2], ("smp",), 0)

time: 42.7 us -> 40.8 us (0.956)
  starting transfers between devices: 17.7 us -> 16.7 us
  Pallas kernels: 13.1 us -> 12.2 us
    ppermute x1, starting transfers between devices: 4.36 us -> 0.56 us  [exchange(): return lax.ppermute(value, axes[-1], [(0, 1), (1, 0)])]
    ppermute x3, starting transfers between devices: 3.55 us -> 5.33 us  [swap(): return lax.ppermute(value, 'smp', [(i, i ^ by) for i in range(n_smp)])]
    ppermute x3, starting transfers between devices: 5.94 us -> 6.95 us  [exchange(): return lax.ppermute(value, axes, pairs)]
    pallas_call x2, Pallas kernels: 6.53 us -> 5.6 us  [the longest x1 3.47 us: krylov(): pl.pallas_call(functools.partial(krylov_kernel, sb, paired), in_specs=[VM...]
    ppermute x3, waiting for transfers between devices: 8.84 us -> 9.38 us  [swap(): return lax.ppermute(value, 'smp', [(i, i ^ by) for i in range(n_smp)])]
    ppermute x3, waiting for transfers between devices: 2.03 us -> 1.55 us  [shift(): lax.ppermute(value, 'smp', [(i, (i + by) % n_smp) for i in range(n_smp)])]
  transfers between devices with their start and end apart: 10 -> 10, of which waited for: 4 -> 5; matrix products, arithmetic and copies ran while one was open for 0% -> 0% of each run, Pallas kernels for 19% -> 19%
where the time goes in v8:
time: 40.8 us; the launch traced here: 40.7 us
  starting transfers between devices  16.7 us (41%)
  Pallas kernels  12.2 us (30%)
  waiting for transfers between devices  10.9 us (27%)
  between operations  0.8 us (2%)
    ppermute x3, waiting for transfers between devices, swap(): return lax.ppermute(value, 'smp', [(i, i ^ by) for i in range(n_smp)])  9.38 us
    ppermute x3, starting transfers between devices, exchange(): return lax.ppermute(value, axes, pairs)  6.95 us
    ppermute x3, starting transfers between devices, swap(): return lax.ppermute(value, 'smp', [(i, i ^ by) for i in range(n_smp)])  5.33 us
    ppermute x3, starting transfers between devices, shift(): lax.ppermute(value, 'smp', [(i, (i + by) % n_smp) for i in range(n_smp)])  3.88 us
    pallas_call x1, Pallas kernels, gram_parts(): pl.pallas_call(functools.partial(gram_kernel, parts, rot, inv), in_specs=...  3.61 us
    pallas_call x1, Pallas kernels, krylov(): pl.pallas_call(functools.partial(krylov_kernel, sb, paired), in_specs=[VM...  3.47 us
    pallas_call x1, Pallas kernels, final(): pl.pallas_call(functools.partial(final_kernel, parts, rot, len(moms)), in...  2.13 us
    pallas_call x1, Pallas kernels, pack(): pl.pallas_call(pack_kernel, in_specs=[far] * 4, out_specs=[VMEM] * len(sh...  1.83 us
  transfers between devices with their start and end apart: 10, of which 5 were waited for; matrix products, arithmetic and copies ran while one was open for 0% of the time, Pallas kernels for 19%

profile of v8, /device:TPU:0, one launch (start us, length us, event | category | flops | bytes accessed | tf_op | source)
XLA Modules:
  0.0 40.7 jit_solution(11826034876364152901)
XLA Ops:
  0.6 0.0 copy-start
  0.6 0.0 copy-start.3
  0.6 0.0 copy-start.4
  0.7 1.8 %pack.1 = (bf16[2048,128]{1,0:T(8,128)(2,1)S(1)}, bf16[2048,128]{1,0:T(8,128)(2,1)S(1)}, s16[1040,128]{1,0:T(8,128)(2,1)S(1)}, s16[1040,128]{1,0:T(8,128)(2,1)S(1)}) custom-call(bf16[2048,1024]{1,0:T(8,128)(2,1)} %dos.3, f32[1024,128]{1,0:T(8,128)} %z.3, f32[320,1024]{1,0:T(8,128)} %bitcast.7, s32[2,1024]{1,0:T(2,128)} %bitcast.13), custom_call_target="tpu_custom_call" | custom-call | tf_op jit(solution)/shard_map/pack/pallas_call | solution.py:188
  2.5 0.6 %collective-permute-start.2 = (bf16[2048,128]{1,0:T(8,128)(2,1)S(1)}, bf16[2048,128]{1,0:T(8,128)(2,1)S(1)}, u32[]{:S(2)}, u32[]{:S(2)}) collective-permute-start(bf16[2048,128]{1,0:T(8,128)(2,1)S(1)} %get-tuple-element.25), channel_id=1, source_target_pairs={{0,1},{1,0},{2,3},{3,2},{4,5},{5,4},{6,7},{7,6},{8,9},{9,8},{10,11... | collective-permute-start | bytes 1572872 | tf_op jit(solution)/shard_map/ppermute | solution.py:204
  3.1 0.7 %collective-permute-start.3 = (bf16[2048,128]{1,0:T(8,128)(2,1)S(1)}, bf16[2048,128]{1,0:T(8,128)(2,1)S(1)}, u32[]{:S(2)}, u32[]{:S(2)}) collective-permute-start(bf16[2048,128]{1,0:T(8,128)(2,1)S(1)} %get-tuple-element.26), channel_id=1, source_target_pairs={{1,2},{2,1},{5,6},{6,5},{9,10},{10,9},{13,14},{14,13},{17,18},{18,... | collective-permute-start | bytes 1572872 | tf_op jit(solution)/shard_map/ppermute | solution.py:208
  3.7 0.7 %collective-permute-start = (s16[1040,128]{1,0:T(8,128)(2,1)S(1)}, s16[1040,128]{1,0:T(8,128)(2,1)S(1)}, u32[]{:S(2)}, u32[]{:S(2)}) collective-permute-start(s16[1040,128]{1,0:T(8,128)(2,1)S(1)} %get-tuple-element.20), channel_id=1, source_target_pairs={{4,8},{8,4},{5,9},{9,5},{6,10},{10,6},{7,11},{11,7},{20,24},{24,20... | collective-permute-start | bytes 798728 | tf_op jit(solution)/shard_map/ppermute | solution.py:208
  4.4 5.6 %collective-permute-start.1 = (s16[1040,128]{1,0:T(8,128)(2,1)S(1)}, s16[1040,128]{1,0:T(8,128)(2,1)S(1)}, u32[]{:S(2)}, u32[]{:S(2)}) collective-permute-start(s16[1040,128]{1,0:T(8,128)(2,1)S(1)} %get-tuple-element.21), channel_id=1, source_target_pairs={{0,4},{4,0},{8,12},{12,8},{1,5},{5,1},{9,13},{13,9},{2,6},{6,2},{1... | collective-permute-start | bytes 798728 | tf_op jit(solution)/shard_map/ppermute | solution.py:208
  10.0 0.0 copy-done
  10.0 0.0 copy-done.3
  10.0 0.0 copy-done.4
  10.0 3.6 %gram.1 = (f32[176,256]{1,0:T(8,128)S(1)}, s16[176,256]{1,0:T(8,128)(2,1)S(1)}, s16[176,256]{1,0:T(8,128)(2,1)S(1)}, s16[176,256]{1,0:T(8,128)(2,1)S(1)}, bf16[2...) custom-call(bf16[2048,1024]{1,0:T(8,128)(2,1)S(1)} %copy-done, f32[32,128]{1,0:T(8,128)S(1)} %bitcast.9, ...), custom_call_target="tpu_custom_call" | custom-call | flops 1610612736 | bytes 8388608 | tf_op jit(solution)/shard_map/gram/pallas_call | solution.py:299
  13.6 0.0 copy-start.1
  13.7 0.0 copy-start.2
  13.7 0.0 copy-start.5
  13.7 0.0 copy-start.7
  13.7 0.0 collective-permute-done.2.got_e
  13.7 0.0 collective-permute-done.3.got_o
  13.7 0.8 %cross.1 = (f32[176,256]{1,0:T(8,128)S(1)}, s16[176,256]{1,0:T(8,128)(2,1)S(1)}, s16[176,256]{1,0:T(8,128)(2,1)S(1)}, s16[176,256]{1,0:T(8,128)(2,1)S(1)}) custom-call(bf16[2048,128]{1,0:T(8,128)(2,1)S(1)} %get-tuple-element.23.head, bf16[2048,128]{1,0:T(8,128)(2,1)S(1)} %get-tuple-element.24.last, bf16[2048,128]{1,0:T(8,128)(2,1)S(1)} %collective-permute-done.2.got_e, ...), custom_call_target="tpu_custom_call" | custom-call | tf_op jit(solution)/shard_map/cross/pallas_call | solution.py:361
  14.5 0.1 collective-permute-start.4
  14.6 1.8 %collective-permute-start.5 = (s16[176,256]{1,0:T(8,128)(2,1)S(1)}, s16[176,256]{1,0:T(8,128)(2,1)S(1)}, u32[]{:S(2)}, u32[]{:S(2)}) collective-permute-start(s16[176,256]{1,0:T(8,128)(2,1)S(1)} %get-tuple-element.33), channel_id=1, source_target_pairs={{0,8},{4,12},{8,0},{12,4},{1,9},{5,13},{9,1},{13,5},{2,10},{6,14},... | collective-permute-start | bytes 270344 | tf_op jit(solution)/shard_map/ppermute | solution.py:797
  16.4 2.0 %collective-permute-start.6 = (s16[176,256]{1,0:T(8,128)(2,1)S(1)}, s16[176,256]{1,0:T(8,128)(2,1)S(1)}, u32[]{:S(2)}, u32[]{:S(2)}) collective-permute-start(s16[176,256]{1,0:T(8,128)(2,1)S(1)} %get-tuple-element.34), channel_id=1, source_target_pairs={{0,12},{4,0},{8,4},{12,8},{1,13},{5,1},{9,5},{13,9},{2,14},{6,2},{... | collective-permute-start | bytes 270344 | tf_op jit(solution)/shard_map/ppermute | solution.py:797
  18.4 0.0 collective-permute-done.got_o
  18.4 0.0 collective-permute-done.1.got_e
  18.4 0.0 copy-done.1
  18.4 0.0 copy-done.2
  18.4 0.0 copy-done.5
  18.4 0.0 copy-done.7
  18.4 0.0 copy-start.6
  18.5 3.5 %krylov.1 = (f32[3,1024,128]{2,1,0:T(8,128)S(1)}, f32[8,128]{1,0:T(8,128)S(1)}) custom-call(s32[1,64]{1,0:T(1,128)S(1)} %bitcast.16, f32[320,1024]{1,0:T(8,128)S(1)} %bitcast.8, f32[1024,128]{1,0:T(8,128)S(1)} %copy-done.2, s32[2,1024]{1,0:T(2,128)S(1)} %bitcast.14, s16[1040,128]{1,0:T(8,128)(2,1)S(1)} %collective-permute-done.got_o, ...), custom_call_target="tpu_custom_call" | custom-call | flops 1321205760 | bytes 1310720 | tf_op jit(solution)/shard_map/krylov/pallas_call | solution.py:685
  21.9 0.0 collective-permute-done.4.rest_0_
  21.9 0.9 %collective-permute-done.5.rest_1_ = s16[176,256]{1,0:T(8,128)(2,1)S(1)} collective-permute-done((s16[176,256]{1,0:T(8,128)(2,1)S(1)}, s16[176,256]{1,0:T(8,128)(2,1)S(1)}, u32[]{:S(2)}, u32[]{:S(2)}) %collective-permute-start.5) | collective-permute-done | bytes 90144 | tf_op jit(solution)/shard_map/ppermute | solution.py:797
  22.9 0.6 %collective-permute-done.6.rest_2_ = s16[176,256]{1,0:T(8,128)(2,1)S(1)} collective-permute-done((s16[176,256]{1,0:T(8,128)(2,1)S(1)}, s16[176,256]{1,0:T(8,128)(2,1)S(1)}, u32[]{:S(2)}, u32[]{:S(2)}) %collective-permute-start.6) | collective-permute-done | bytes 90144 | tf_op jit(solution)/shard_map/ppermute | solution.py:797
  23.5 0.3 total.1.rest_0_
  23.8 3.1 %collective-permute-start.9 = (s16[192,256]{1,0:T(8,128)(2,1)S(1)}, s16[192,256]{1,0:T(8,128)(2,1)S(1)}, u32[]{:S(2)}, u32[]{:S(2)}) collective-permute-start(s16[192,256]{1,0:T(8,128)(2,1)S(1)} %total.1.rest_0_), channel_id=1, source_target_pairs={{0,4},{4,0},{8,12},{12,8},{1,5},{5,1},{9,13},{13,9},{2,6},{6,2},{1... | collective-permute-start | bytes 294920 | tf_op jit(solution)/shard_map/ppermute | solution.py:800
  26.9 1.8 %collective-permute-start.8 = (s16[192,256]{1,0:T(8,128)(2,1)S(1)}, s16[192,256]{1,0:T(8,128)(2,1)S(1)}, u32[]{:S(2)}, u32[]{:S(2)}) collective-permute-start(s16[192,256]{1,0:T(8,128)(2,1)S(1)} %total.1.rest_0_), channel_id=1, source_target_pairs={{0,12},{4,8},{8,4},{12,0},{1,13},{5,9},{9,5},{13,1},{2,14},{6,10},... | collective-permute-start | bytes 294920 | tf_op jit(solution)/shard_map/ppermute | solution.py:800
  28.7 0.5 %collective-permute-start.7 = (s16[192,256]{1,0:T(8,128)(2,1)S(1)}, s16[192,256]{1,0:T(8,128)(2,1)S(1)}, u32[]{:S(2)}, u32[]{:S(2)}) collective-permute-start(s16[192,256]{1,0:T(8,128)(2,1)S(1)} %total.1.rest_0_), channel_id=1, source_target_pairs={{0,8},{4,12},{8,0},{12,4},{1,9},{5,13},{9,1},{13,5},{2,10},{6,14},... | collective-permute-start | bytes 294920 | tf_op jit(solution)/shard_map/ppermute | solution.py:800
  29.1 1.2 %collective-permute-done.9.rest_3_ = s16[192,256]{1,0:T(8,128)(2,1)S(1)} collective-permute-done((s16[192,256]{1,0:T(8,128)(2,1)S(1)}, s16[192,256]{1,0:T(8,128)(2,1)S(1)}, u32[]{:S(2)}, u32[]{:S(2)}) %collective-permute-start.9) | collective-permute-done | bytes 98336 | tf_op jit(solution)/shard_map/ppermute | solution.py:800
  30.3 4.1 %collective-permute-done.8.rest_2_ = s16[192,256]{1,0:T(8,128)(2,1)S(1)} collective-permute-done((s16[192,256]{1,0:T(8,128)(2,1)S(1)}, s16[192,256]{1,0:T(8,128)(2,1)S(1)}, u32[]{:S(2)}, u32[]{:S(2)}) %collective-permute-start.8) | collective-permute-done | bytes 98336 | tf_op jit(solution)/shard_map/ppermute | solution.py:800
  34.4 4.1 %collective-permute-done.7.rest_1_ = s16[192,256]{1,0:T(8,128)(2,1)S(1)} collective-permute-done((s16[192,256]{1,0:T(8,128)(2,1)S(1)}, s16[192,256]{1,0:T(8,128)(2,1)S(1)}, u32[]{:S(2)}, u32[]{:S(2)}) %collective-permute-start.7) | collective-permute-done | bytes 98336 | tf_op jit(solution)/shard_map/ppermute | solution.py:800
  38.5 0.0 copy-done.6
  38.5 2.1 %final.1 = (f32[320,1024]{1,0:T(8,128)}, f32[1024,128]{1,0:T(8,128)}) custom-call(s32[1,64]{1,0:T(1,128)S(1)} %bitcast.15, f32[3,1024,128]{2,1,0:T(8,128)S(1)} %get-tuple-element.22.w, s16[192,256]{1,0:T(8,128)(2,1)S(1)} %total.1.rest_0_, s16[192,256]{1,0:T(8,128)(2,1)S(1)} %collective-permute-done.7.rest_1_, ...), custom_call_target="tpu_custom_call" | custom-call | tf_op jit(solution)/shard_map/final/pallas_call | solution.py:488
Async XLA Ops:
  0.6 9.4 %copy-start = (bf16[2048,1024]{1,0:T(8,128)(2,1)S(1)}, bf16[2048,1024]{1,0:T(8,128)(2,1)}, u32[]{:S(2)}) copy-start(bf16[2048,1024]{1,0:T(8,128)(2,1)} %dos.3) | copy-start | bytes 12582916
  0.6 9.4 %copy-start.3 = (f32[4096]{0:T(1024)S(1)}, f32[4096]{0:T(1024)}, u32[]{:S(2)}) copy-start(f32[4096]{0:T(1024)} %param.9) | copy-start | bytes 49156
  0.6 9.4 %copy-start.4 = (f32[4096]{0:T(1024)S(1)}, f32[4096]{0:T(1024)}, u32[]{:S(2)}) copy-start(f32[4096]{0:T(1024)} %param.10) | copy-start | bytes 49156
  2.5 11.2 %collective-permute-start.2 = (bf16[2048,128]{1,0:T(8,128)(2,1)S(1)}, bf16[2048,128]{1,0:T(8,128)(2,1)S(1)}, u32[]{:S(2)}, u32[]{:S(2)}) collective-permute-start(bf16[2048,128]{1,0:T(8,128)(2,1)S(1)} %get-tuple-element.25), channel_id=1, source_target_pairs={{0,1},{1,0},{2,3},{3,2},{4,5},{5,4},{6,7},{7,6},{8,9},{9,8},{10,11... | collective-permute-start | bytes 1572872 | tf_op jit(solution)/shard_map/ppermute | solution.py:204
  3.1 10.7 %collective-permute-start.3 = (bf16[2048,128]{1,0:T(8,128)(2,1)S(1)}, bf16[2048,128]{1,0:T(8,128)(2,1)S(1)}, u32[]{:S(2)}, u32[]{:S(2)}) collective-permute-start(bf16[2048,128]{1,0:T(8,128)(2,1)S(1)} %get-tuple-element.26), channel_id=1, source_target_pairs={{1,2},{2,1},{5,6},{6,5},{9,10},{10,9},{13,14},{14,13},{17,18},{18,... | collective-permute-start | bytes 1572872 | tf_op jit(solution)/shard_map/ppermute | solution.py:208
  3.7 14.7 %collective-permute-start = (s16[1040,128]{1,0:T(8,128)(2,1)S(1)}, s16[1040,128]{1,0:T(8,128)(2,1)S(1)}, u32[]{:S(2)}, u32[]{:S(2)}) collective-permute-start(s16[1040,128]{1,0:T(8,128)(2,1)S(1)} %get-tuple-element.20), channel_id=1, source_target_pairs={{4,8},{8,4},{5,9},{9,5},{6,10},{10,6},{7,11},{11,7},{20,24},{24,20... | collective-permute-start | bytes 798728 | tf_op jit(solution)/shard_map/ppermute | solution.py:208
  4.4 14.0 %collective-permute-start.1 = (s16[1040,128]{1,0:T(8,128)(2,1)S(1)}, s16[1040,128]{1,0:T(8,128)(2,1)S(1)}, u32[]{:S(2)}, u32[]{:S(2)}) collective-permute-start(s16[1040,128]{1,0:T(8,128)(2,1)S(1)} %get-tuple-element.21), channel_id=1, source_target_pairs={{0,4},{4,0},{8,12},{12,8},{1,5},{5,1},{9,13},{13,9},{2,6},{6,2},{1... | collective-permute-start | bytes 798728 | tf_op jit(solution)/shard_map/ppermute | solution.py:208
  13.6 4.8 %copy-start.1 = (f32[1024,320]{0,1:T(8,128)S(1)}, f32[1024,320]{0,1:T(8,128)}, u32[]{:S(2)}) copy-start(f32[1024,320]{0,1:T(8,128)} %param.12) | copy-start | bytes 3932164
  13.7 4.8 %copy-start.2 = (f32[1024,128]{1,0:T(8,128)S(1)}, f32[1024,128]{1,0:T(8,128)}, u32[]{:S(2)}) copy-start(f32[1024,128]{1,0:T(8,128)} %z.3) | copy-start | bytes 1572868
  13.7 4.8 %copy-start.5 = (s32[1024,2]{0,1:T(2,128)S(1)}, s32[1024,2]{0,1:T(2,128)}, u32[]{:S(2)}) copy-start(s32[1024,2]{0,1:T(2,128)} %param.15) | copy-start | bytes 24580
  13.7 4.8 %copy-start.7 = (s32[64]{0:T(128)S(1)}, s32[64]{0:T(128)}, u32[]{:S(2)}) copy-start(s32[64]{0:T(128)} %param.13) | copy-start | bytes 772
  14.5 7.4 %collective-permute-start.4 = (s16[176,256]{1,0:T(8,128)(2,1)S(1)}, s16[176,256]{1,0:T(8,128)(2,1)S(1)}, u32[]{:S(2)}, u32[]{:S(2)}) collective-permute-start(s16[176,256]{1,0:T(8,128)(2,1)S(1)} %get-tuple-element.32), channel_id=1, source_target_pairs={{0,4},{4,8},{8,12},{12,0},{1,5},{5,9},{9,13},{13,1},{2,6},{6,10},{... | collective-permute-start | bytes 270344 | tf_op jit(solution)/shard_map/ppermute | solution.py:797
  14.6 8.3 %collective-permute-start.5 = (s16[176,256]{1,0:T(8,128)(2,1)S(1)}, s16[176,256]{1,0:T(8,128)(2,1)S(1)}, u32[]{:S(2)}, u32[]{:S(2)}) collective-permute-start(s16[176,256]{1,0:T(8,128)(2,1)S(1)} %get-tuple-element.33), channel_id=1, source_target_pairs={{0,8},{4,12},{8,0},{12,4},{1,9},{5,13},{9,1},{13,5},{2,10},{6,14},... | collective-permute-start | bytes 270344 | tf_op jit(solution)/shard_map/ppermute | solution.py:797
  16.4 7.1 %collective-permute-start.6 = (s16[176,256]{1,0:T(8,128)(2,1)S(1)}, s16[176,256]{1,0:T(8,128)(2,1)S(1)}, u32[]{:S(2)}, u32[]{:S(2)}) collective-permute-start(s16[176,256]{1,0:T(8,128)(2,1)S(1)} %get-tuple-element.34), channel_id=1, source_target_pairs={{0,12},{4,0},{8,4},{12,8},{1,13},{5,1},{9,5},{13,9},{2,14},{6,2},{... | collective-permute-start | bytes 270344 | tf_op jit(solution)/shard_map/ppermute | solution.py:797
  18.4 20.1 %copy-start.6 = (s32[64]{0:T(128)S(1)}, s32[64]{0:T(128)}, u32[]{:S(2)}) copy-start(s32[64]{0:T(128)} %param.11) | copy-start | bytes 772
  23.8 6.5 %collective-permute-start.9 = (s16[192,256]{1,0:T(8,128)(2,1)S(1)}, s16[192,256]{1,0:T(8,128)(2,1)S(1)}, u32[]{:S(2)}, u32[]{:S(2)}) collective-permute-start(s16[192,256]{1,0:T(8,128)(2,1)S(1)} %total.1.rest_0_), channel_id=1, source_target_pairs={{0,4},{4,0},{8,12},{12,8},{1,5},{5,1},{9,13},{13,9},{2,6},{6,2},{1... | collective-permute-start | bytes 294920 | tf_op jit(solution)/shard_map/ppermute | solution.py:800
  26.9 7.6 %collective-permute-start.8 = (s16[192,256]{1,0:T(8,128)(2,1)S(1)}, s16[192,256]{1,0:T(8,128)(2,1)S(1)}, u32[]{:S(2)}, u32[]{:S(2)}) collective-permute-start(s16[192,256]{1,0:T(8,128)(2,1)S(1)} %total.1.rest_0_), channel_id=1, source_target_pairs={{0,12},{4,8},{8,4},{12,0},{1,13},{5,9},{9,5},{13,1},{2,14},{6,10},... | collective-permute-start | bytes 294920 | tf_op jit(solution)/shard_map/ppermute | solution.py:800
  28.7 9.9 %collective-permute-start.7 = (s16[192,256]{1,0:T(8,128)(2,1)S(1)}, s16[192,256]{1,0:T(8,128)(2,1)S(1)}, u32[]{:S(2)}, u32[]{:S(2)}) collective-permute-start(s16[192,256]{1,0:T(8,128)(2,1)S(1)} %total.1.rest_0_), channel_id=1, source_target_pairs={{0,8},{4,12},{8,0},{12,4},{1,9},{5,13},{9,1},{13,5},{2,10},{6,14},... | collective-permute-start | bytes 294920 | tf_op jit(solution)/shard_map/ppermute | solution.py:800

commit v9 on v8

--- a/solution.py
+++ b/solution.py
@@ -81,7 +81,10 @@
 
 
 def decode(code, largest=LARGEST, roots=3):
-    value = from_code(code)
+    return decoded(from_code(code), largest, roots)
+
+
+def decoded(value, largest, roots):
     size = value * (1.0 / LEVELS)
     for _ in range(roots):
         size = size * size
@@ -508,16 +511,16 @@
     def pick(self, at, convert):
         if self.flag is None:
             return self.one[at]
-        return jnp.where(self.flag, convert(self.one[at]), convert(self.two[at]))
+        return convert(jnp.where(self.flag, from_code(self.one[at]), from_code(self.two[at])))
 
     def vector(self, at):
-        return self.pick(at, lambda code: decode(code, Z_LARGEST, Z_ROOTS))
+        return self.pick(at, lambda value: decoded(value, Z_LARGEST, Z_ROOTS))
 
     def band(self, at):
-        return self.pick(at, lambda code: from_code(code) * (1.0 / LEVELS))
+        return self.pick(at, lambda value: value * (1.0 / LEVELS))
 
     def flags(self, at):
-        return self.pick(at, from_code)
+        return self.pick(at, lambda value: value)
 
 
 def krylov_kernel(
@@ -799,7 +802,7 @@
         def swap(value, by):
             return lax.ppermute(value, "smp", [(i, i ^ by) for i in range(n_smp)])
 
-        got = [shift(blocks[by], by) for by in (1, 2, 3)]
+        got = [shift(blocks[by], by) for by in (1, 3, 2)]
     w, mom = krylov(ldt, zscores, obs, got_e, got_o, band_prev, paired)
     if rot:
         mine = total_of(blocks[0], got, mom)

time: 40.8 us -> 41.6 us (1.020)
  waiting for transfers between devices: 10.9 us -> 13.6 us
  starting transfers between devices: 16.7 us -> 14.9 us
    ppermute x3, waiting for transfers between devices: 1.55 us -> 4.64 us  [shift(): lax.ppermute(value, 'smp', [(i, (i + by) % n_smp) for i in range(n_smp)])]
    ppermute x3, starting transfers between devices: 5.33 us -> 3.55 us  [swap(): return lax.ppermute(value, 'smp', [(i, i ^ by) for i in range(n_smp)])]
    ppermute x3, waiting for transfers between devices: 9.38 us -> 8.91 us  [swap(): return lax.ppermute(value, 'smp', [(i, i ^ by) for i in range(n_smp)])]
  transfers between devices with their start and end apart: 10 -> 10, of which waited for: 5 -> 4; matrix products, arithmetic and copies ran while one was open for 0% -> 0% of each run, Pallas kernels for 19% -> 19%
where the time goes in v9:
time: 41.6 us; the launch traced here: 41.4 us
  starting transfers between devices  14.9 us (36%)
  waiting for transfers between devices  13.6 us (33%)
  Pallas kernels  12 us (29%)
  between operations  0.82 us (2%)
    ppermute x3, waiting for transfers between devices, swap(): return lax.ppermute(value, 'smp', [(i, i ^ by) for i in range(n_smp)])  8.91 us
    ppermute x3, starting transfers between devices, exchange(): return lax.ppermute(value, axes, pairs)  6.95 us
    ppermute x3, waiting for transfers between devices, shift(): lax.ppermute(value, 'smp', [(i, (i + by) % n_smp) for i in range(n_smp)])  4.64 us
    ppermute x3, starting transfers between devices, shift(): lax.ppermute(value, 'smp', [(i, (i + by) % n_smp) for i in range(n_smp)])  3.88 us
    pallas_call x1, Pallas kernels, gram_parts(): pl.pallas_call(functools.partial(gram_kernel, parts, rot, inv), in_specs=...  3.61 us
    ppermute x3, starting transfers between devices, swap(): return lax.ppermute(value, 'smp', [(i, i ^ by) for i in range(n_smp)])  3.55 us
    pallas_call x1, Pallas kernels, krylov(): pl.pallas_call(functools.partial(krylov_kernel, sb, paired), in_specs=[VM...  3.35 us
    pallas_call x1, Pallas kernels, final(): pl.pallas_call(functools.partial(final_kernel, parts, rot, len(moms)), in...  2.13 us
  transfers between devices with their start and end apart: 10, of which 4 were waited for; matrix products, arithmetic and copies ran while one was open for 0% of the time, Pallas kernels for 19%

profile of v9, /device:TPU:0, one launch (start us, length us, event | category | flops | bytes accessed | tf_op | source)
XLA Modules:
  0.0 41.4 jit_solution(3294978870642327019)
XLA Ops:
  0.6 0.0 copy-start
  0.6 0.0 copy-start.3
  0.6 0.0 copy-start.4
  0.7 1.8 %pack.1 = (bf16[2048,128]{1,0:T(8,128)(2,1)S(1)}, bf16[2048,128]{1,0:T(8,128)(2,1)S(1)}, s16[1040,128]{1,0:T(8,128)(2,1)S(1)}, s16[1040,128]{1,0:T(8,128)(2,1)S(1)}) custom-call(bf16[2048,1024]{1,0:T(8,128)(2,1)} %dos.3, f32[1024,128]{1,0:T(8,128)} %z.3, f32[320,1024]{1,0:T(8,128)} %bitcast.7, s32[2,1024]{1,0:T(2,128)} %bitcast.13), custom_call_target="tpu_custom_call" | custom-call | tf_op jit(solution)/shard_map/pack/pallas_call | solution.py:191
  2.5 0.6 %collective-permute-start.2 = (bf16[2048,128]{1,0:T(8,128)(2,1)S(1)}, bf16[2048,128]{1,0:T(8,128)(2,1)S(1)}, u32[]{:S(2)}, u32[]{:S(2)}) collective-permute-start(bf16[2048,128]{1,0:T(8,128)(2,1)S(1)} %get-tuple-element.25), channel_id=1, source_target_pairs={{0,1},{1,0},{2,3},{3,2},{4,5},{5,4},{6,7},{7,6},{8,9},{9,8},{10,11... | collective-permute-start | bytes 1572872 | tf_op jit(solution)/shard_map/ppermute | solution.py:207
  3.1 0.7 %collective-permute-start.3 = (bf16[2048,128]{1,0:T(8,128)(2,1)S(1)}, bf16[2048,128]{1,0:T(8,128)(2,1)S(1)}, u32[]{:S(2)}, u32[]{:S(2)}) collective-permute-start(bf16[2048,128]{1,0:T(8,128)(2,1)S(1)} %get-tuple-element.26), channel_id=1, source_target_pairs={{1,2},{2,1},{5,6},{6,5},{9,10},{10,9},{13,14},{14,13},{17,18},{18,... | collective-permute-start | bytes 1572872 | tf_op jit(solution)/shard_map/ppermute | solution.py:211
  3.7 0.7 %collective-permute-start = (s16[1040,128]{1,0:T(8,128)(2,1)S(1)}, s16[1040,128]{1,0:T(8,128)(2,1)S(1)}, u32[]{:S(2)}, u32[]{:S(2)}) collective-permute-start(s16[1040,128]{1,0:T(8,128)(2,1)S(1)} %get-tuple-element.20), channel_id=1, source_target_pairs={{4,8},{8,4},{5,9},{9,5},{6,10},{10,6},{7,11},{11,7},{20,24},{24,20... | collective-permute-start | bytes 798728 | tf_op jit(solution)/shard_map/ppermute | solution.py:211
  4.4 5.6 %collective-permute-start.1 = (s16[1040,128]{1,0:T(8,128)(2,1)S(1)}, s16[1040,128]{1,0:T(8,128)(2,1)S(1)}, u32[]{:S(2)}, u32[]{:S(2)}) collective-permute-start(s16[1040,128]{1,0:T(8,128)(2,1)S(1)} %get-tuple-element.21), channel_id=1, source_target_pairs={{0,4},{4,0},{8,12},{12,8},{1,5},{5,1},{9,13},{13,9},{2,6},{6,2},{1... | collective-permute-start | bytes 798728 | tf_op jit(solution)/shard_map/ppermute | solution.py:211
  10.0 0.0 copy-done
  10.0 0.0 copy-done.3
  10.0 0.0 copy-done.4
  10.0 3.6 %gram.1 = (f32[176,256]{1,0:T(8,128)S(1)}, s16[176,256]{1,0:T(8,128)(2,1)S(1)}, s16[176,256]{1,0:T(8,128)(2,1)S(1)}, s16[176,256]{1,0:T(8,128)(2,1)S(1)}, bf16[2...) custom-call(bf16[2048,1024]{1,0:T(8,128)(2,1)S(1)} %copy-done, f32[32,128]{1,0:T(8,128)S(1)} %bitcast.9, ...), custom_call_target="tpu_custom_call" | custom-call | flops 1610612736 | bytes 8388608 | tf_op jit(solution)/shard_map/gram/pallas_call | solution.py:302
  13.6 0.0 copy-start.1
  13.7 0.0 copy-start.2
  13.7 0.0 copy-start.5
  13.7 0.0 copy-start.7
  13.7 0.0 collective-permute-done.2.got_e
  13.7 0.0 collective-permute-done.3.got_o
  13.7 0.8 %cross.1 = (f32[176,256]{1,0:T(8,128)S(1)}, s16[176,256]{1,0:T(8,128)(2,1)S(1)}, s16[176,256]{1,0:T(8,128)(2,1)S(1)}, s16[176,256]{1,0:T(8,128)(2,1)S(1)}) custom-call(bf16[2048,128]{1,0:T(8,128)(2,1)S(1)} %get-tuple-element.23.head, bf16[2048,128]{1,0:T(8,128)(2,1)S(1)} %get-tuple-element.24.last, bf16[2048,128]{1,0:T(8,128)(2,1)S(1)} %collective-permute-done.2.got_e, ...), custom_call_target="tpu_custom_call" | custom-call | tf_op jit(solution)/shard_map/cross/pallas_call | solution.py:364
  14.5 0.1 collective-permute-start.4
  14.6 3.8 %collective-permute-start.5 = (s16[176,256]{1,0:T(8,128)(2,1)S(1)}, s16[176,256]{1,0:T(8,128)(2,1)S(1)}, u32[]{:S(2)}, u32[]{:S(2)}) collective-permute-start(s16[176,256]{1,0:T(8,128)(2,1)S(1)} %get-tuple-element.33), channel_id=1, source_target_pairs={{0,12},{4,0},{8,4},{12,8},{1,13},{5,1},{9,5},{13,9},{2,14},{6,2},{... | collective-permute-start | bytes 270344 | tf_op jit(solution)/shard_map/ppermute | solution.py:800
  18.4 0.0 collective-permute-start.6
  18.4 0.0 collective-permute-done.got_o
  18.4 0.0 collective-permute-done.1.got_e
  18.4 0.0 copy-done.1
  18.4 0.0 copy-done.2
  18.4 0.0 copy-done.5
  18.4 0.0 copy-done.7
  18.5 0.0 copy-start.6
  18.5 3.4 %krylov.1 = (f32[3,1024,128]{2,1,0:T(8,128)S(1)}, f32[8,128]{1,0:T(8,128)S(1)}) custom-call(s32[1,64]{1,0:T(1,128)S(1)} %bitcast.16, f32[320,1024]{1,0:T(8,128)S(1)} %bitcast.8, f32[1024,128]{1,0:T(8,128)S(1)} %copy-done.2, s32[2,1024]{1,0:T(2,128)S(1)} %bitcast.14, s16[1040,128]{1,0:T(8,128)(2,1)S(1)} %collective-permute-done.got_o, ...), custom_call_target="tpu_custom_call" | custom-call | flops 1321205760 | bytes 1310720 | tf_op jit(solution)/shard_map/krylov/pallas_call | solution.py:688
  21.8 0.0 collective-permute-done.4.rest_0_
  21.8 0.0 collective-permute-done.5.rest_1_
  21.8 4.6 %collective-permute-done.6.rest_2_ = s16[176,256]{1,0:T(8,128)(2,1)S(1)} collective-permute-done((s16[176,256]{1,0:T(8,128)(2,1)S(1)}, s16[176,256]{1,0:T(8,128)(2,1)S(1)}, u32[]{:S(2)}, u32[]{:S(2)}) %collective-permute-start.6) | collective-permute-done | bytes 90144 | tf_op jit(solution)/shard_map/ppermute | solution.py:800
  26.5 0.3 total.1.rest_0_
  26.8 0.1 collective-permute-start.9
  26.9 1.6 %collective-permute-start.8 = (s16[192,256]{1,0:T(8,128)(2,1)S(1)}, s16[192,256]{1,0:T(8,128)(2,1)S(1)}, u32[]{:S(2)}, u32[]{:S(2)}) collective-permute-start(s16[192,256]{1,0:T(8,128)(2,1)S(1)} %total.1.rest_0_), channel_id=1, source_target_pairs={{0,12},{4,8},{8,4},{12,0},{1,13},{5,9},{9,5},{13,1},{2,14},{6,10},... | collective-permute-start | bytes 294920 | tf_op jit(solution)/shard_map/ppermute | solution.py:803
  28.4 1.9 %collective-permute-start.7 = (s16[192,256]{1,0:T(8,128)(2,1)S(1)}, s16[192,256]{1,0:T(8,128)(2,1)S(1)}, u32[]{:S(2)}, u32[]{:S(2)}) collective-permute-start(s16[192,256]{1,0:T(8,128)(2,1)S(1)} %total.1.rest_0_), channel_id=1, source_target_pairs={{0,8},{4,12},{8,0},{12,4},{1,9},{5,13},{9,1},{13,5},{2,10},{6,14},... | collective-permute-start | bytes 294920 | tf_op jit(solution)/shard_map/ppermute | solution.py:803
  30.4 1.3 %collective-permute-done.9.rest_3_ = s16[192,256]{1,0:T(8,128)(2,1)S(1)} collective-permute-done((s16[192,256]{1,0:T(8,128)(2,1)S(1)}, s16[192,256]{1,0:T(8,128)(2,1)S(1)}, u32[]{:S(2)}, u32[]{:S(2)}) %collective-permute-start.9) | collective-permute-done | bytes 98336 | tf_op jit(solution)/shard_map/ppermute | solution.py:803
  31.7 2.8 %collective-permute-done.8.rest_2_ = s16[192,256]{1,0:T(8,128)(2,1)S(1)} collective-permute-done((s16[192,256]{1,0:T(8,128)(2,1)S(1)}, s16[192,256]{1,0:T(8,128)(2,1)S(1)}, u32[]{:S(2)}, u32[]{:S(2)}) %collective-permute-start.8) | collective-permute-done | bytes 98336 | tf_op jit(solution)/shard_map/ppermute | solution.py:803
  34.5 4.8 %collective-permute-done.7.rest_1_ = s16[192,256]{1,0:T(8,128)(2,1)S(1)} collective-permute-done((s16[192,256]{1,0:T(8,128)(2,1)S(1)}, s16[192,256]{1,0:T(8,128)(2,1)S(1)}, u32[]{:S(2)}, u32[]{:S(2)}) %collective-permute-start.7) | collective-permute-done | bytes 98336 | tf_op jit(solution)/shard_map/ppermute | solution.py:803
  39.3 0.0 copy-done.6
  39.3 2.1 %final.1 = (f32[320,1024]{1,0:T(8,128)}, f32[1024,128]{1,0:T(8,128)}) custom-call(s32[1,64]{1,0:T(1,128)S(1)} %bitcast.15, f32[3,1024,128]{2,1,0:T(8,128)S(1)} %get-tuple-element.22.w, s16[192,256]{1,0:T(8,128)(2,1)S(1)} %total.1.rest_0_, s16[192,256]{1,0:T(8,128)(2,1)S(1)} %collective-permute-done.7.rest_1_, ...), custom_call_target="tpu_custom_call" | custom-call | tf_op jit(solution)/shard_map/final/pallas_call | solution.py:491
Async XLA Ops:
  0.6 9.4 %copy-start = (bf16[2048,1024]{1,0:T(8,128)(2,1)S(1)}, bf16[2048,1024]{1,0:T(8,128)(2,1)}, u32[]{:S(2)}) copy-start(bf16[2048,1024]{1,0:T(8,128)(2,1)} %dos.3) | copy-start | bytes 12582916
  0.6 9.4 %copy-start.3 = (f32[4096]{0:T(1024)S(1)}, f32[4096]{0:T(1024)}, u32[]{:S(2)}) copy-start(f32[4096]{0:T(1024)} %param.9) | copy-start | bytes 49156
  0.6 9.4 %copy-start.4 = (f32[4096]{0:T(1024)S(1)}, f32[4096]{0:T(1024)}, u32[]{:S(2)}) copy-start(f32[4096]{0:T(1024)} %param.10) | copy-start | bytes 49156
  2.5 11.2 %collective-permute-start.2 = (bf16[2048,128]{1,0:T(8,128)(2,1)S(1)}, bf16[2048,128]{1,0:T(8,128)(2,1)S(1)}, u32[]{:S(2)}, u32[]{:S(2)}) collective-permute-start(bf16[2048,128]{1,0:T(8,128)(2,1)S(1)} %get-tuple-element.25), channel_id=1, source_target_pairs={{0,1},{1,0},{2,3},{3,2},{4,5},{5,4},{6,7},{7,6},{8,9},{9,8},{10,11... | collective-permute-start | bytes 1572872 | tf_op jit(solution)/shard_map/ppermute | solution.py:207
  3.1 10.7 %collective-permute-start.3 = (bf16[2048,128]{1,0:T(8,128)(2,1)S(1)}, bf16[2048,128]{1,0:T(8,128)(2,1)S(1)}, u32[]{:S(2)}, u32[]{:S(2)}) collective-permute-start(bf16[2048,128]{1,0:T(8,128)(2,1)S(1)} %get-tuple-element.26), channel_id=1, source_target_pairs={{1,2},{2,1},{5,6},{6,5},{9,10},{10,9},{13,14},{14,13},{17,18},{18,... | collective-permute-start | bytes 1572872 | tf_op jit(solution)/shard_map/ppermute | solution.py:211
  3.7 14.7 %collective-permute-start = (s16[1040,128]{1,0:T(8,128)(2,1)S(1)}, s16[1040,128]{1,0:T(8,128)(2,1)S(1)}, u32[]{:S(2)}, u32[]{:S(2)}) collective-permute-start(s16[1040,128]{1,0:T(8,128)(2,1)S(1)} %get-tuple-element.20), channel_id=1, source_target_pairs={{4,8},{8,4},{5,9},{9,5},{6,10},{10,6},{7,11},{11,7},{20,24},{24,20... | collective-permute-start | bytes 798728 | tf_op jit(solution)/shard_map/ppermute | solution.py:211
  4.4 14.0 %collective-permute-start.1 = (s16[1040,128]{1,0:T(8,128)(2,1)S(1)}, s16[1040,128]{1,0:T(8,128)(2,1)S(1)}, u32[]{:S(2)}, u32[]{:S(2)}) collective-permute-start(s16[1040,128]{1,0:T(8,128)(2,1)S(1)} %get-tuple-element.21), channel_id=1, source_target_pairs={{0,4},{4,0},{8,12},{12,8},{1,5},{5,1},{9,13},{13,9},{2,6},{6,2},{1... | collective-permute-start | bytes 798728 | tf_op jit(solution)/shard_map/ppermute | solution.py:211
  13.6 4.8 %copy-start.1 = (f32[1024,320]{0,1:T(8,128)S(1)}, f32[1024,320]{0,1:T(8,128)}, u32[]{:S(2)}) copy-start(f32[1024,320]{0,1:T(8,128)} %param.12) | copy-start | bytes 3932164
  13.7 4.8 %copy-start.2 = (f32[1024,128]{1,0:T(8,128)S(1)}, f32[1024,128]{1,0:T(8,128)}, u32[]{:S(2)}) copy-start(f32[1024,128]{1,0:T(8,128)} %z.3) | copy-start | bytes 1572868
  13.7 4.8 %copy-start.5 = (s32[1024,2]{0,1:T(2,128)S(1)}, s32[1024,2]{0,1:T(2,128)}, u32[]{:S(2)}) copy-start(s32[1024,2]{0,1:T(2,128)} %param.15) | copy-start | bytes 24580
  13.7 4.8 %copy-start.7 = (s32[64]{0:T(128)S(1)}, s32[64]{0:T(128)}, u32[]{:S(2)}) copy-start(s32[64]{0:T(128)} %param.13) | copy-start | bytes 772
  14.5 7.3 %collective-permute-start.4 = (s16[176,256]{1,0:T(8,128)(2,1)S(1)}, s16[176,256]{1,0:T(8,128)(2,1)S(1)}, u32[]{:S(2)}, u32[]{:S(2)}) collective-permute-start(s16[176,256]{1,0:T(8,128)(2,1)S(1)} %get-tuple-element.32), channel_id=1, source_target_pairs={{0,4},{4,8},{8,12},{12,0},{1,5},{5,9},{9,13},{13,1},{2,6},{6,10},{... | collective-permute-start | bytes 270344 | tf_op jit(solution)/shard_map/ppermute | solution.py:800
  14.6 7.2 %collective-permute-start.5 = (s16[176,256]{1,0:T(8,128)(2,1)S(1)}, s16[176,256]{1,0:T(8,128)(2,1)S(1)}, u32[]{:S(2)}, u32[]{:S(2)}) collective-permute-start(s16[176,256]{1,0:T(8,128)(2,1)S(1)} %get-tuple-element.33), channel_id=1, source_target_pairs={{0,12},{4,0},{8,4},{12,8},{1,13},{5,1},{9,5},{13,9},{2,14},{6,2},{... | collective-permute-start | bytes 270344 | tf_op jit(solution)/shard_map/ppermute | solution.py:800
  18.4 8.1 %collective-permute-start.6 = (s16[176,256]{1,0:T(8,128)(2,1)S(1)}, s16[176,256]{1,0:T(8,128)(2,1)S(1)}, u32[]{:S(2)}, u32[]{:S(2)}) collective-permute-start(s16[176,256]{1,0:T(8,128)(2,1)S(1)} %get-tuple-element.34), channel_id=1, source_target_pairs={{0,8},{4,12},{8,0},{12,4},{1,9},{5,13},{9,1},{13,5},{2,10},{6,14},... | collective-permute-start | bytes 270344 | tf_op jit(solution)/shard_map/ppermute | solution.py:800
  18.5 20.8 %copy-start.6 = (s32[64]{0:T(128)S(1)}, s32[64]{0:T(128)}, u32[]{:S(2)}) copy-start(s32[64]{0:T(128)} %param.11) | copy-start | bytes 772
  26.8 4.9 %collective-permute-start.9 = (s16[192,256]{1,0:T(8,128)(2,1)S(1)}, s16[192,256]{1,0:T(8,128)(2,1)S(1)}, u32[]{:S(2)}, u32[]{:S(2)}) collective-permute-start(s16[192,256]{1,0:T(8,128)(2,1)S(1)} %total.1.rest_0_), channel_id=1, source_target_pairs={{0,4},{4,0},{8,12},{12,8},{1,5},{5,1},{9,13},{13,9},{2,6},{6,2},{1... | collective-permute-start | bytes 294920 | tf_op jit(solution)/shard_map/ppermute | solution.py:803
  26.9 7.6 %collective-permute-start.8 = (s16[192,256]{1,0:T(8,128)(2,1)S(1)}, s16[192,256]{1,0:T(8,128)(2,1)S(1)}, u32[]{:S(2)}, u32[]{:S(2)}) collective-permute-start(s16[192,256]{1,0:T(8,128)(2,1)S(1)} %total.1.rest_0_), channel_id=1, source_target_pairs={{0,12},{4,8},{8,4},{12,0},{1,13},{5,9},{9,5},{13,1},{2,14},{6,10},... | collective-permute-start | bytes 294920 | tf_op jit(solution)/shard_map/ppermute | solution.py:803
  28.4 10.8 %collective-permute-start.7 = (s16[192,256]{1,0:T(8,128)(2,1)S(1)}, s16[192,256]{1,0:T(8,128)(2,1)S(1)}, u32[]{:S(2)}, u32[]{:S(2)}) collective-permute-start(s16[192,256]{1,0:T(8,128)(2,1)S(1)} %total.1.rest_0_), channel_id=1, source_target_pairs={{0,8},{4,12},{8,0},{12,4},{1,9},{5,13},{9,1},{13,5},{2,10},{6,14},... | collective-permute-start | bytes 294920 | tf_op jit(solution)/shard_map/ppermute | solution.py:803

commit v10 on v9

--- a/solution.py
+++ b/solution.py
@@ -802,7 +802,7 @@
         def swap(value, by):
             return lax.ppermute(value, "smp", [(i, i ^ by) for i in range(n_smp)])
 
-        got = [shift(blocks[by], by) for by in (1, 3, 2)]
+        got = [shift(blocks[by], by) for by in (3, 2, 1)]
     w, mom = krylov(ldt, zscores, obs, got_e, got_o, band_prev, paired)
     if rot:
         mine = total_of(blocks[0], got, mom)

time: 41.6 us -> 41.3 us (level)
  starting transfers between devices: 14.9 us -> 13.1 us
  waiting for transfers between devices: 13.6 us -> 15.1 us
    ppermute x3, starting transfers between devices: 3.88 us -> 2.08 us  [shift(): lax.ppermute(value, 'smp', [(i, (i + by) % n_smp) for i in range(n_smp)])]
    ppermute x3, waiting for transfers between devices: 4.64 us -> 5.8 us  [shift(): lax.ppermute(value, 'smp', [(i, (i + by) % n_smp) for i in range(n_smp)])]
where the time goes in v10:
time: 41.3 us; the launch traced here: 41.1 us
  waiting for transfers between devices  15.1 us (37%)
  starting transfers between devices  13.1 us (32%)
  Pallas kernels  12 us (29%)
  between operations  0.81 us (2%)
    ppermute x3, waiting for transfers between devices, swap(): return lax.ppermute(value, 'smp', [(i, i ^ by) for i in range(n_smp)])  9.25 us
    ppermute x3, starting transfers between devices, exchange(): return lax.ppermute(value, axes, pairs)  6.95 us
    ppermute x3, waiting for transfers between devices, shift(): lax.ppermute(value, 'smp', [(i, (i + by) % n_smp) for i in range(n_smp)])  5.8 us
    pallas_call x1, Pallas kernels, gram_parts(): pl.pallas_call(functools.partial(gram_kernel, parts, rot, inv), in_specs=...  3.61 us
    ppermute x3, starting transfers between devices, swap(): return lax.ppermute(value, 'smp', [(i, i ^ by) for i in range(n_smp)])  3.55 us
    pallas_call x1, Pallas kernels, krylov(): pl.pallas_call(functools.partial(krylov_kernel, sb, paired), in_specs=[VM...  3.35 us
    pallas_call x1, Pallas kernels, final(): pl.pallas_call(functools.partial(final_kernel, parts, rot, len(moms)), in...  2.13 us
    ppermute x3, starting transfers between devices, shift(): lax.ppermute(value, 'smp', [(i, (i + by) % n_smp) for i in range(n_smp)])  2.08 us
  transfers between devices with their start and end apart: 10, of which 4 were waited for; matrix products, arithmetic and copies ran while one was open for 0% of the time, Pallas kernels for 19%

profile of v10, /device:TPU:0, one launch (start us, length us, event | category | flops | bytes accessed | tf_op | source)
XLA Modules:
  0.0 41.1 jit_solution(4546430494554211081)
XLA Ops:
  0.6 0.0 copy-start
  0.6 0.0 copy-start.3
  0.6 0.0 copy-start.4
  0.7 1.8 %pack.1 = (bf16[2048,128]{1,0:T(8,128)(2,1)S(1)}, bf16[2048,128]{1,0:T(8,128)(2,1)S(1)}, s16[1040,128]{1,0:T(8,128)(2,1)S(1)}, s16[1040,128]{1,0:T(8,128)(2,1)S(1)}) custom-call(bf16[2048,1024]{1,0:T(8,128)(2,1)} %dos.3, f32[1024,128]{1,0:T(8,128)} %z.3, f32[320,1024]{1,0:T(8,128)} %bitcast.7, s32[2,1024]{1,0:T(2,128)} %bitcast.13), custom_call_target="tpu_custom_call" | custom-call | tf_op jit(solution)/shard_map/pack/pallas_call | solution.py:191
  2.5 0.6 %collective-permute-start.2 = (bf16[2048,128]{1,0:T(8,128)(2,1)S(1)}, bf16[2048,128]{1,0:T(8,128)(2,1)S(1)}, u32[]{:S(2)}, u32[]{:S(2)}) collective-permute-start(bf16[2048,128]{1,0:T(8,128)(2,1)S(1)} %get-tuple-element.25), channel_id=1, source_target_pairs={{0,1},{1,0},{2,3},{3,2},{4,5},{5,4},{6,7},{7,6},{8,9},{9,8},{10,11... | collective-permute-start | bytes 1572872 | tf_op jit(solution)/shard_map/ppermute | solution.py:207
  3.1 0.7 %collective-permute-start.3 = (bf16[2048,128]{1,0:T(8,128)(2,1)S(1)}, bf16[2048,128]{1,0:T(8,128)(2,1)S(1)}, u32[]{:S(2)}, u32[]{:S(2)}) collective-permute-start(bf16[2048,128]{1,0:T(8,128)(2,1)S(1)} %get-tuple-element.26), channel_id=1, source_target_pairs={{1,2},{2,1},{5,6},{6,5},{9,10},{10,9},{13,14},{14,13},{17,18},{18,... | collective-permute-start | bytes 1572872 | tf_op jit(solution)/shard_map/ppermute | solution.py:211
  3.7 0.7 %collective-permute-start = (s16[1040,128]{1,0:T(8,128)(2,1)S(1)}, s16[1040,128]{1,0:T(8,128)(2,1)S(1)}, u32[]{:S(2)}, u32[]{:S(2)}) collective-permute-start(s16[1040,128]{1,0:T(8,128)(2,1)S(1)} %get-tuple-element.20), channel_id=1, source_target_pairs={{4,8},{8,4},{5,9},{9,5},{6,10},{10,6},{7,11},{11,7},{20,24},{24,20... | collective-permute-start | bytes 798728 | tf_op jit(solution)/shard_map/ppermute | solution.py:211
  4.4 5.6 %collective-permute-start.1 = (s16[1040,128]{1,0:T(8,128)(2,1)S(1)}, s16[1040,128]{1,0:T(8,128)(2,1)S(1)}, u32[]{:S(2)}, u32[]{:S(2)}) collective-permute-start(s16[1040,128]{1,0:T(8,128)(2,1)S(1)} %get-tuple-element.21), channel_id=1, source_target_pairs={{0,4},{4,0},{8,12},{12,8},{1,5},{5,1},{9,13},{13,9},{2,6},{6,2},{1... | collective-permute-start | bytes 798728 | tf_op jit(solution)/shard_map/ppermute | solution.py:211
  10.0 0.0 copy-done
  10.0 0.0 copy-done.3
  10.0 0.0 copy-done.4
  10.0 3.6 %gram.1 = (f32[176,256]{1,0:T(8,128)S(1)}, s16[176,256]{1,0:T(8,128)(2,1)S(1)}, s16[176,256]{1,0:T(8,128)(2,1)S(1)}, s16[176,256]{1,0:T(8,128)(2,1)S(1)}, bf16[2...) custom-call(bf16[2048,1024]{1,0:T(8,128)(2,1)S(1)} %copy-done, f32[32,128]{1,0:T(8,128)S(1)} %bitcast.9, ...), custom_call_target="tpu_custom_call" | custom-call | flops 1610612736 | bytes 8388608 | tf_op jit(solution)/shard_map/gram/pallas_call | solution.py:302
  13.6 0.0 copy-start.1
  13.7 0.0 copy-start.2
  13.7 0.0 copy-start.5
  13.7 0.0 copy-start.7
  13.7 0.0 collective-permute-done.2.got_e
  13.7 0.0 collective-permute-done.3.got_o
  13.7 0.8 %cross.1 = (f32[176,256]{1,0:T(8,128)S(1)}, s16[176,256]{1,0:T(8,128)(2,1)S(1)}, s16[176,256]{1,0:T(8,128)(2,1)S(1)}, s16[176,256]{1,0:T(8,128)(2,1)S(1)}) custom-call(bf16[2048,128]{1,0:T(8,128)(2,1)S(1)} %get-tuple-element.23.head, bf16[2048,128]{1,0:T(8,128)(2,1)S(1)} %get-tuple-element.24.last, bf16[2048,128]{1,0:T(8,128)(2,1)S(1)} %collective-permute-done.2.got_e, ...), custom_call_target="tpu_custom_call" | custom-call | tf_op jit(solution)/shard_map/cross/pallas_call | solution.py:364
  14.5 1.3 %collective-permute-start.4 = (s16[176,256]{1,0:T(8,128)(2,1)S(1)}, s16[176,256]{1,0:T(8,128)(2,1)S(1)}, u32[]{:S(2)}, u32[]{:S(2)}) collective-permute-start(s16[176,256]{1,0:T(8,128)(2,1)S(1)} %get-tuple-element.32), channel_id=1, source_target_pairs={{0,12},{4,0},{8,4},{12,8},{1,13},{5,1},{9,5},{13,9},{2,14},{6,2},{... | collective-permute-start | bytes 270344 | tf_op jit(solution)/shard_map/ppermute | solution.py:800
  15.9 0.2 collective-permute-start.5
  16.1 0.5 %collective-permute-start.6 = (s16[176,256]{1,0:T(8,128)(2,1)S(1)}, s16[176,256]{1,0:T(8,128)(2,1)S(1)}, u32[]{:S(2)}, u32[]{:S(2)}) collective-permute-start(s16[176,256]{1,0:T(8,128)(2,1)S(1)} %get-tuple-element.34), channel_id=1, source_target_pairs={{0,4},{4,8},{8,12},{12,0},{1,5},{5,9},{9,13},{13,1},{2,6},{6,10},{... | collective-permute-start | bytes 270344 | tf_op jit(solution)/shard_map/ppermute | solution.py:800
  16.6 0.0 collective-permute-done.got_o
  16.6 0.0 collective-permute-done.1.got_e
  16.6 0.0 copy-done.1
  16.6 0.0 copy-done.2
  16.6 0.0 copy-done.5
  16.6 0.0 copy-done.7
  16.6 0.0 copy-start.6
  16.7 3.4 %krylov.1 = (f32[3,1024,128]{2,1,0:T(8,128)S(1)}, f32[8,128]{1,0:T(8,128)S(1)}) custom-call(s32[1,64]{1,0:T(1,128)S(1)} %bitcast.16, f32[320,1024]{1,0:T(8,128)S(1)} %bitcast.8, f32[1024,128]{1,0:T(8,128)S(1)} %copy-done.2, s32[2,1024]{1,0:T(2,128)S(1)} %bitcast.14, s16[1040,128]{1,0:T(8,128)(2,1)S(1)} %collective-permute-done.got_o, ...), custom_call_target="tpu_custom_call" | custom-call | flops 1321205760 | bytes 1310720 | tf_op jit(solution)/shard_map/krylov/pallas_call | solution.py:688
  20.0 0.0 collective-permute-done.4.rest_0_
  20.0 5.8 %collective-permute-done.5.rest_1_ = s16[176,256]{1,0:T(8,128)(2,1)S(1)} collective-permute-done((s16[176,256]{1,0:T(8,128)(2,1)S(1)}, s16[176,256]{1,0:T(8,128)(2,1)S(1)}, u32[]{:S(2)}, u32[]{:S(2)}) %collective-permute-start.5) | collective-permute-done | bytes 90144 | tf_op jit(solution)/shard_map/ppermute | solution.py:800
  25.8 0.0 collective-permute-done.6.rest_2_
  25.8 0.3 total.1.rest_0_
  26.2 0.1 collective-permute-start.9
  26.2 2.1 %collective-permute-start.8 = (s16[192,256]{1,0:T(8,128)(2,1)S(1)}, s16[192,256]{1,0:T(8,128)(2,1)S(1)}, u32[]{:S(2)}, u32[]{:S(2)}) collective-permute-start(s16[192,256]{1,0:T(8,128)(2,1)S(1)} %total.1.rest_0_), channel_id=1, source_target_pairs={{0,12},{4,8},{8,4},{12,0},{1,13},{5,9},{9,5},{13,1},{2,14},{6,10},... | collective-permute-start | bytes 294920 | tf_op jit(solution)/shard_map/ppermute | solution.py:803
  28.4 1.3 %collective-permute-start.7 = (s16[192,256]{1,0:T(8,128)(2,1)S(1)}, s16[192,256]{1,0:T(8,128)(2,1)S(1)}, u32[]{:S(2)}, u32[]{:S(2)}) collective-permute-start(s16[192,256]{1,0:T(8,128)(2,1)S(1)} %total.1.rest_0_), channel_id=1, source_target_pairs={{0,8},{4,12},{8,0},{12,4},{1,9},{5,13},{9,1},{13,5},{2,10},{6,14},... | collective-permute-start | bytes 294920 | tf_op jit(solution)/shard_map/ppermute | solution.py:803
  29.7 1.8 %collective-permute-done.9.rest_3_ = s16[192,256]{1,0:T(8,128)(2,1)S(1)} collective-permute-done((s16[192,256]{1,0:T(8,128)(2,1)S(1)}, s16[192,256]{1,0:T(8,128)(2,1)S(1)}, u32[]{:S(2)}, u32[]{:S(2)}) %collective-permute-start.9) | collective-permute-done | bytes 98336 | tf_op jit(solution)/shard_map/ppermute | solution.py:803
  31.6 2.7 %collective-permute-done.8.rest_2_ = s16[192,256]{1,0:T(8,128)(2,1)S(1)} collective-permute-done((s16[192,256]{1,0:T(8,128)(2,1)S(1)}, s16[192,256]{1,0:T(8,128)(2,1)S(1)}, u32[]{:S(2)}, u32[]{:S(2)}) %collective-permute-start.8) | collective-permute-done | bytes 98336 | tf_op jit(solution)/shard_map/ppermute | solution.py:803
  34.2 4.8 %collective-permute-done.7.rest_1_ = s16[192,256]{1,0:T(8,128)(2,1)S(1)} collective-permute-done((s16[192,256]{1,0:T(8,128)(2,1)S(1)}, s16[192,256]{1,0:T(8,128)(2,1)S(1)}, u32[]{:S(2)}, u32[]{:S(2)}) %collective-permute-start.7) | collective-permute-done | bytes 98336 | tf_op jit(solution)/shard_map/ppermute | solution.py:803
  39.0 0.0 copy-done.6
  39.0 2.1 %final.1 = (f32[320,1024]{1,0:T(8,128)}, f32[1024,128]{1,0:T(8,128)}) custom-call(s32[1,64]{1,0:T(1,128)S(1)} %bitcast.15, f32[3,1024,128]{2,1,0:T(8,128)S(1)} %get-tuple-element.22.w, s16[192,256]{1,0:T(8,128)(2,1)S(1)} %total.1.rest_0_, s16[192,256]{1,0:T(8,128)(2,1)S(1)} %collective-permute-done.7.rest_1_, ...), custom_call_target="tpu_custom_call" | custom-call | tf_op jit(solution)/shard_map/final/pallas_call | solution.py:491
Async XLA Ops:
  0.6 9.4 %copy-start = (bf16[2048,1024]{1,0:T(8,128)(2,1)S(1)}, bf16[2048,1024]{1,0:T(8,128)(2,1)}, u32[]{:S(2)}) copy-start(bf16[2048,1024]{1,0:T(8,128)(2,1)} %dos.3) | copy-start | bytes 12582916
  0.6 9.4 %copy-start.3 = (f32[4096]{0:T(1024)S(1)}, f32[4096]{0:T(1024)}, u32[]{:S(2)}) copy-start(f32[4096]{0:T(1024)} %param.9) | copy-start | bytes 49156
  0.6 9.4 %copy-start.4 = (f32[4096]{0:T(1024)S(1)}, f32[4096]{0:T(1024)}, u32[]{:S(2)}) copy-start(f32[4096]{0:T(1024)} %param.10) | copy-start | bytes 49156
  2.5 11.2 %collective-permute-start.2 = (bf16[2048,128]{1,0:T(8,128)(2,1)S(1)}, bf16[2048,128]{1,0:T(8,128)(2,1)S(1)}, u32[]{:S(2)}, u32[]{:S(2)}) collective-permute-start(bf16[2048,128]{1,0:T(8,128)(2,1)S(1)} %get-tuple-element.25), channel_id=1, source_target_pairs={{0,1},{1,0},{2,3},{3,2},{4,5},{5,4},{6,7},{7,6},{8,9},{9,8},{10,11... | collective-permute-start | bytes 1572872 | tf_op jit(solution)/shard_map/ppermute | solution.py:207
  3.1 10.7 %collective-permute-start.3 = (bf16[2048,128]{1,0:T(8,128)(2,1)S(1)}, bf16[2048,128]{1,0:T(8,128)(2,1)S(1)}, u32[]{:S(2)}, u32[]{:S(2)}) collective-permute-start(bf16[2048,128]{1,0:T(8,128)(2,1)S(1)} %get-tuple-element.26), channel_id=1, source_target_pairs={{1,2},{2,1},{5,6},{6,5},{9,10},{10,9},{13,14},{14,13},{17,18},{18,... | collective-permute-start | bytes 1572872 | tf_op jit(solution)/shard_map/ppermute | solution.py:211
  3.7 12.9 %collective-permute-start = (s16[1040,128]{1,0:T(8,128)(2,1)S(1)}, s16[1040,128]{1,0:T(8,128)(2,1)S(1)}, u32[]{:S(2)}, u32[]{:S(2)}) collective-permute-start(s16[1040,128]{1,0:T(8,128)(2,1)S(1)} %get-tuple-element.20), channel_id=1, source_target_pairs={{4,8},{8,4},{5,9},{9,5},{6,10},{10,6},{7,11},{11,7},{20,24},{24,20... | collective-permute-start | bytes 798728 | tf_op jit(solution)/shard_map/ppermute | solution.py:211
  4.4 12.2 %collective-permute-start.1 = (s16[1040,128]{1,0:T(8,128)(2,1)S(1)}, s16[1040,128]{1,0:T(8,128)(2,1)S(1)}, u32[]{:S(2)}, u32[]{:S(2)}) collective-permute-start(s16[1040,128]{1,0:T(8,128)(2,1)S(1)} %get-tuple-element.21), channel_id=1, source_target_pairs={{0,4},{4,0},{8,12},{12,8},{1,5},{5,1},{9,13},{13,9},{2,6},{6,2},{1... | collective-permute-start | bytes 798728 | tf_op jit(solution)/shard_map/ppermute | solution.py:211
  13.6 3.0 %copy-start.1 = (f32[1024,320]{0,1:T(8,128)S(1)}, f32[1024,320]{0,1:T(8,128)}, u32[]{:S(2)}) copy-start(f32[1024,320]{0,1:T(8,128)} %param.12) | copy-start | bytes 3932164
  13.7 3.0 %copy-start.2 = (f32[1024,128]{1,0:T(8,128)S(1)}, f32[1024,128]{1,0:T(8,128)}, u32[]{:S(2)}) copy-start(f32[1024,128]{1,0:T(8,128)} %z.3) | copy-start | bytes 1572868
  13.7 3.0 %copy-start.5 = (s32[1024,2]{0,1:T(2,128)S(1)}, s32[1024,2]{0,1:T(2,128)}, u32[]{:S(2)}) copy-start(s32[1024,2]{0,1:T(2,128)} %param.15) | copy-start | bytes 24580
  13.7 3.0 %copy-start.7 = (s32[64]{0:T(128)S(1)}, s32[64]{0:T(128)}, u32[]{:S(2)}) copy-start(s32[64]{0:T(128)} %param.13) | copy-start | bytes 772
  14.5 5.5 %collective-permute-start.4 = (s16[176,256]{1,0:T(8,128)(2,1)S(1)}, s16[176,256]{1,0:T(8,128)(2,1)S(1)}, u32[]{:S(2)}, u32[]{:S(2)}) collective-permute-start(s16[176,256]{1,0:T(8,128)(2,1)S(1)} %get-tuple-element.32), channel_id=1, source_target_pairs={{0,12},{4,0},{8,4},{12,8},{1,13},{5,1},{9,5},{13,9},{2,14},{6,2},{... | collective-permute-start | bytes 270344 | tf_op jit(solution)/shard_map/ppermute | solution.py:800
  15.9 10.0 %collective-permute-start.5 = (s16[176,256]{1,0:T(8,128)(2,1)S(1)}, s16[176,256]{1,0:T(8,128)(2,1)S(1)}, u32[]{:S(2)}, u32[]{:S(2)}) collective-permute-start(s16[176,256]{1,0:T(8,128)(2,1)S(1)} %get-tuple-element.33), channel_id=1, source_target_pairs={{0,8},{4,12},{8,0},{12,4},{1,9},{5,13},{9,1},{13,5},{2,10},{6,14},... | collective-permute-start | bytes 270344 | tf_op jit(solution)/shard_map/ppermute | solution.py:800
  16.1 9.7 %collective-permute-start.6 = (s16[176,256]{1,0:T(8,128)(2,1)S(1)}, s16[176,256]{1,0:T(8,128)(2,1)S(1)}, u32[]{:S(2)}, u32[]{:S(2)}) collective-permute-start(s16[176,256]{1,0:T(8,128)(2,1)S(1)} %get-tuple-element.34), channel_id=1, source_target_pairs={{0,4},{4,8},{8,12},{12,0},{1,5},{5,9},{9,13},{13,1},{2,6},{6,10},{... | collective-permute-start | bytes 270344 | tf_op jit(solution)/shard_map/ppermute | solution.py:800
  16.6 22.3 %copy-start.6 = (s32[64]{0:T(128)S(1)}, s32[64]{0:T(128)}, u32[]{:S(2)}) copy-start(s32[64]{0:T(128)} %param.11) | copy-start | bytes 772
  26.2 5.4 %collective-permute-start.9 = (s16[192,256]{1,0:T(8,128)(2,1)S(1)}, s16[192,256]{1,0:T(8,128)(2,1)S(1)}, u32[]{:S(2)}, u32[]{:S(2)}) collective-permute-start(s16[192,256]{1,0:T(8,128)(2,1)S(1)} %total.1.rest_0_), channel_id=1, source_target_pairs={{0,4},{4,0},{8,12},{12,8},{1,5},{5,1},{9,13},{13,9},{2,6},{6,2},{1... | collective-permute-start | bytes 294920 | tf_op jit(solution)/shard_map/ppermute | solution.py:803
  26.2 8.0 %collective-permute-start.8 = (s16[192,256]{1,0:T(8,128)(2,1)S(1)}, s16[192,256]{1,0:T(8,128)(2,1)S(1)}, u32[]{:S(2)}, u32[]{:S(2)}) collective-permute-start(s16[192,256]{1,0:T(8,128)(2,1)S(1)} %total.1.rest_0_), channel_id=1, source_target_pairs={{0,12},{4,8},{8,4},{12,0},{1,13},{5,9},{9,5},{13,1},{2,14},{6,10},... | collective-permute-start | bytes 294920 | tf_op jit(solution)/shard_map/ppermute | solution.py:803
  28.4 10.6 %collective-permute-start.7 = (s16[192,256]{1,0:T(8,128)(2,1)S(1)}, s16[192,256]{1,0:T(8,128)(2,1)S(1)}, u32[]{:S(2)}, u32[]{:S(2)}) collective-permute-start(s16[192,256]{1,0:T(8,128)(2,1)S(1)} %total.1.rest_0_), channel_id=1, source_target_pairs={{0,8},{4,12},{8,0},{12,4},{1,9},{5,13},{9,1},{13,5},{2,10},{6,14},... | collective-permute-start | bytes 294920 | tf_op jit(solution)/shard_map/ppermute | solution.py:803
